TPU v7x, 32 devices: a whole 2x2x4 slice. The times are simulated.
32 devices in a mesh: seq: 2 (over y), dp: 16 (over z, x, core).
Axes of the slice: x: 2, y: 2, z: 4, core: 2. Of those that a mesh axis runs over, the one named last changes fastest.
Arguments:
- tokens: bfloat16 [16, 512, 1024], P('dp', 'seq'), may hold values from -6 to 6
- starts: int32 [16, 512], P('dp', 'seq'), may hold values 0 or 1
- routes: int32 [16, 512, 8], P('dp', 'seq'), may hold values from 0 to 15, all different within a row; in each aligned block of 256 rows (0 to 255, 256 to 511, ..., all dimensions but the last counted through in order) at most 224 rows name the same one
- gain_one: bfloat16 [1024], P('dp'), may hold values from 0.5 to 1.5
- query_key_value_weight: bfloat16 [1024, 2048], P('dp'), may hold values from -0.1875 to 0.1875
- w_out: bfloat16 [1024, 1024], P('dp'), may hold values from -1.5 to 1.5
- gain_two: bfloat16 [1024], P('dp'), may hold values from 0.5 to 1.5
- w_router: bfloat16 [1024, 16], P('dp'), may hold values from -0.09375 to 0.09375
- w_gate_up: bfloat16 [1024, 16, 1024], P('dp'), may hold values from -0.1875 to 0.1875
- w_down: bfloat16 [512, 16, 1024], P('dp'), may hold values from -1 to 1
- cotangent: bfloat16 [16, 512, 1024], P('dp', 'seq'), may hold values from -6 to 6
Outputs:
- output: bfloat16 [16, 512, 1024], P('dp', 'seq')
- input_grad: bfloat16 [16, 512, 1024], P('dp', 'seq')
- grad_gain_one: float32 [1024], P('dp')
- grad_w_qkv: float32 [1024, 2048], P('dp')
- grad_w_out: float32 [1024, 1024], P('dp')
- grad_gain_two: float32 [1024], P('dp')
- grad_w_router: float32 [1024, 16], P('dp')
- grad_w_gate_up: float32 [1024, 16, 1024], P('dp')
- grad_w_down: float32 [512, 16, 1024], P('dp')
- stream_rms: float32 [16, 2], P('dp')
Inputs may be any that keep to these rules, and one draw needn't show every extreme that they name: `starts`: 1 marks a token that begins a document; a stream's first token begins one whatever its entry. `routes`: each row names 8 different experts; within the 256 rows of one device no expert is named more than 224 times, and in every draw some expert is named exactly 224 times on some device.
All inputs are finite; a program needn't handle non-finite values. No bound on the sum of `starts` on one device may be relied on, other than what follows from the above.
Results may differ from a plain program's by a relative error of at most 0.015.
Values may be sent and summed in bfloat16 or wider, within the bound.
A program may use at most 384 MiB of HBM per device.

v0:
```python
import jax
import jax.numpy as jnp
from jax import lax
from jax.sharding import PartitionSpec as P

MODEL_WIDTH = 1024
QUERY_HEADS = 16
KEY_VALUE_HEADS = 8
HEAD_SIZE = 64
F = 512
EXPERTS = 16
TOPK = 8
CAP = 224


epsilon = 1e-06
rope_base = 10000.0
highest = lax.Precision.HIGHEST
masked_score = -1e30


def rms_normed(token_rows, gain_row):
    inverse = lax.rsqrt(jnp.mean(token_rows * token_rows, axis=-1, keepdims=True) + epsilon)
    return token_rows * inverse * gain_row


def norm_back(token_rows, gain_row, upstream):
    inverse = lax.rsqrt(jnp.mean(token_rows * token_rows, axis=-1, keepdims=True) + epsilon)
    gain_grad = jnp.sum(upstream * token_rows * inverse, axis=0)
    scaled = upstream * gain_row
    rows_grad = inverse * scaled - token_rows * inverse**3 * jnp.mean(
        scaled * token_rows, axis=-1, keepdims=True
    )
    return (rows_grad, gain_grad)


def rope_tables(positions, head_dim):
    half_dim = head_dim // 2
    frequency = rope_base ** (-(jnp.arange(half_dim, dtype=jnp.float32) * 2.0) / head_dim)
    angles = positions.astype(jnp.float32)[:, None] * frequency[None, :]
    cosine_table = jnp.cos(angles)
    sine_values = jnp.sin(angles)
    return (
        jnp.concatenate([cosine_table, cosine_table], 1),
        jnp.concatenate([sine_values, sine_values], 1),
    )


def rotary_apply(head_rows, cosine_table, sine_values):
    half_dim = head_rows.shape[-1] // 2
    turned = jnp.concatenate([-head_rows[..., half_dim:], head_rows[..., :half_dim]], -1)
    return head_rows * cosine_table[:, None, :] + turned * sine_values[:, None, :]


def unrotate(grad_rows, cosine_table, sine_values):
    half_dim = grad_rows.shape[-1] // 2
    scaled = grad_rows * sine_values[:, None, :]
    back_turn = jnp.concatenate([scaled[..., half_dim:], -scaled[..., :half_dim]], -1)
    return grad_rows * cosine_table[:, None, :] + back_turn


def slot_tables(route_rows):
    pair_count = route_rows.shape[0] * route_rows.shape[1]
    flat_routes = route_rows.reshape(-1)
    one_hot = (flat_routes[:, None] == jnp.arange(EXPERTS, dtype=jnp.int32)[None, :]).astype(
        jnp.int32
    )
    earlier = jnp.cumsum(one_hot, axis=0) - one_hot
    within = jnp.sum(earlier * one_hot, axis=1)
    slot_flat = flat_routes * CAP + within
    pair_of_slot = (
        jnp.full((EXPERTS * CAP,), pair_count, jnp.int32)
        .at[slot_flat]
        .set(jnp.arange(pair_count, dtype=jnp.int32))
    )
    return (slot_flat.reshape(route_rows.shape), pair_of_slot)


def swiglu_parts(gate_up):
    gate_part = gate_up[..., :F]
    up_part = gate_up[..., F:]
    sigmoid_gate = jax.nn.sigmoid(gate_part)
    silu_gate = gate_part * sigmoid_gate
    act_low = (silu_gate * up_part).astype(jnp.bfloat16)
    return (gate_part, up_part, sigmoid_gate, silu_gate, act_low)


def swiglu_back(act_grad, gate_part, up_part, sigmoid_gate, silu_gate):
    gate_deriv = sigmoid_gate * (1.0 + gate_part * (1.0 - sigmoid_gate))
    return jnp.concatenate([act_grad * up_part * gate_deriv, act_grad * silu_gate], -1).astype(
        jnp.bfloat16
    )


def body(
    tokens,
    starts,
    routes,
    gain_one,
    query_key_value_weight,
    w_out,
    gain_two,
    w_router,
    w_gate_up,
    w_down,
    cotangent,
):
    token_count = tokens.shape[1]
    seq_rank = lax.axis_index("seq")
    token_rows = tokens[0].astype(jnp.float32)
    grad_output = cotangent[0].astype(jnp.float32)
    stream_flags = lax.all_gather(starts[0], "seq", axis=0, tiled=True)
    stream_index = jnp.arange(stream_flags.shape[0], dtype=jnp.int32)
    begins = jnp.where(stream_index == 0, 1, stream_flags)
    segment_all = jnp.cumsum(begins)
    last_begin = lax.cummax(jnp.where(begins > 0, stream_index, -1), axis=0)
    positions_all = stream_index - last_begin
    positions = lax.dynamic_slice_in_dim(positions_all, seq_rank * token_count, token_count)
    gain_one_all, qkv_weight, out_weight, gain_two_all, router_weight = (
        lax.all_gather(gain_one, "dp", axis=0, tiled=True),
        lax.all_gather(query_key_value_weight, "dp", axis=0, tiled=True),
        lax.all_gather(w_out, "dp", axis=0, tiled=True),
        lax.all_gather(gain_two, "dp", axis=0, tiled=True),
        lax.all_gather(w_router, "dp", axis=0, tiled=True),
    )
    gain_a = gain_one_all.astype(jnp.float32)
    gain_b = gain_two_all.astype(jnp.float32)
    query_columns = QUERY_HEADS * HEAD_SIZE
    key_value_columns = KEY_VALUE_HEADS * HEAD_SIZE
    normed_one = rms_normed(token_rows, gain_a).astype(jnp.bfloat16)
    projected_rows = jnp.dot(normed_one, qkv_weight, preferred_element_type=jnp.float32)
    cosine_table, sine_values = rope_tables(positions, HEAD_SIZE)
    queries_low = (
        rotary_apply(
            projected_rows[:, :query_columns].reshape(token_count, QUERY_HEADS, HEAD_SIZE),
            cosine_table,
            sine_values,
        )
        .reshape(token_count, query_columns)
        .astype(jnp.bfloat16)
    )
    keys_low = (
        rotary_apply(
            projected_rows[:, query_columns : query_columns + key_value_columns].reshape(
                token_count, KEY_VALUE_HEADS, HEAD_SIZE
            ),
            cosine_table,
            sine_values,
        )
        .reshape(token_count, key_value_columns)
        .astype(jnp.bfloat16)
    )
    values_low = projected_rows[:, query_columns + key_value_columns :].astype(jnp.bfloat16)
    query_heads, key_heads, value_heads = (
        lax.all_to_all(queries_low, "seq", split_axis=1, concat_axis=0, tiled=True),
        lax.all_to_all(keys_low, "seq", split_axis=1, concat_axis=0, tiled=True),
        lax.all_to_all(values_low, "seq", split_axis=1, concat_axis=0, tiled=True),
    )
    sequence_length = query_heads.shape[0]
    kv_local = key_heads.shape[1] // HEAD_SIZE
    query_group_width = QUERY_HEADS // KEY_VALUE_HEADS
    query_four = query_heads.reshape(sequence_length, kv_local, query_group_width, HEAD_SIZE)
    key_three = key_heads.reshape(sequence_length, kv_local, HEAD_SIZE)
    value_three = value_heads.reshape(sequence_length, kv_local, HEAD_SIZE)
    block_rows = min(512, sequence_length)
    score_scale = HEAD_SIZE ** (-0.5)
    key_index = jnp.arange(sequence_length, dtype=jnp.int32)

    def block_scores(row_start):
        scores = (
            jnp.einsum("qgrd,kgd->grqk", query_four, key_three, preferred_element_type=jnp.float32)
            * score_scale
        )
        query_index = row_start + jnp.arange(block_rows, dtype=jnp.int32)
        allowed = (segment_all[:, None] == segment_all[None, :]) & (
            key_index[None, :] <= query_index[:, None]
        )
        return (query_four, jnp.where(allowed[None, None], scores, masked_score))

    row_start = 0
    query_block, scores = block_scores(row_start)
    top_score = jnp.max(scores, axis=-1, keepdims=True)
    exp_scores = jnp.exp(scores - top_score)
    exp_total = jnp.sum(exp_scores, axis=-1, keepdims=True)
    probs_low = (exp_scores / exp_total).astype(jnp.bfloat16)
    block_out = jnp.einsum(
        "grqk,kgd->qgrd", probs_low, value_three, preferred_element_type=jnp.float32
    )
    outputs_list = block_out.reshape(block_rows, kv_local * query_group_width * HEAD_SIZE).astype(
        jnp.bfloat16
    )
    log_sums = [top_score + jnp.log(exp_total)]
    attended = lax.all_to_all(outputs_list, "seq", split_axis=0, concat_axis=1, tiled=True)
    hidden = token_rows + jnp.dot(attended, out_weight, preferred_element_type=jnp.float32)
    normed_two = rms_normed(hidden, gain_b).astype(jnp.bfloat16)
    logits = jnp.dot(normed_two, router_weight, preferred_element_type=jnp.float32)
    route_rows = routes[0]
    route_match = route_rows[:, :, None] == jnp.arange(EXPERTS, dtype=jnp.int32)[None, None, :]
    chosen = jnp.sum(jnp.where(route_match, logits[:, None, :], 0.0), axis=-1)
    gate_weights = jax.nn.softmax(chosen, axis=-1)
    slot_index, pair_of_slot = slot_tables(route_rows)
    token_of_slot = pair_of_slot // TOPK
    padded = jnp.concatenate([normed_two, jnp.zeros((1, MODEL_WIDTH), jnp.bfloat16)], 0)
    dispatched = padded[token_of_slot].reshape(EXPERTS, CAP, MODEL_WIDTH)
    pair_gate = jnp.concatenate([gate_weights.reshape(-1), jnp.zeros((1,), jnp.float32)])[
        pair_of_slot
    ]
    grad_padded = jnp.concatenate([grad_output, jnp.zeros((1, MODEL_WIDTH), jnp.float32)], 0)
    expert_grad = (
        (pair_gate[:, None] * grad_padded[token_of_slot])
        .astype(jnp.bfloat16)
        .reshape(EXPERTS, CAP, MODEL_WIDTH)
    )
    full_gate_up, full_down = (
        lax.all_gather(w_gate_up, "dp", axis=0, tiled=True),
        lax.all_gather(w_down, "dp", axis=0, tiled=True),
    )
    gate_up = jnp.einsum(
        "ecd,def->ecf", dispatched, full_gate_up, preferred_element_type=jnp.float32
    )
    gate_part, up_part, sigmoid_gate, silu_gate, act_low = swiglu_parts(gate_up)
    expert_out = jnp.einsum("ecf,fed->ecd", act_low, full_down, preferred_element_type=jnp.float32)
    act_grad = jnp.einsum(
        "ecd,fed->ecf", expert_grad, full_down, preferred_element_type=jnp.float32
    )
    down_wgrad = jnp.einsum(
        "ecf,ecd->fed", act_low, expert_grad, preferred_element_type=jnp.float32
    )
    gate_up_grad = swiglu_back(act_grad, gate_part, up_part, sigmoid_gate, silu_gate)
    gate_up_wgrad = jnp.einsum(
        "ecd,ecf->def", dispatched, gate_up_grad, preferred_element_type=jnp.float32
    )
    dispatched_grad = jnp.einsum(
        "ecf,def->ecd", gate_up_grad, full_gate_up, preferred_element_type=jnp.float32
    )
    expert_flat = expert_out.reshape(EXPERTS * CAP, MODEL_WIDTH)
    picked = expert_flat[slot_index]
    mixed = jnp.sum(gate_weights[:, :, None] * picked, axis=1)
    output = (hidden + mixed).astype(jnp.bfloat16)[None]
    stat_sums = jnp.stack([jnp.sum(hidden * hidden), jnp.sum(mixed * mixed)])
    gate_grad = jnp.sum(picked * grad_output[:, None, :], axis=-1)
    normed_grad = jnp.sum(dispatched_grad.reshape(EXPERTS * CAP, MODEL_WIDTH)[slot_index], axis=1)
    chosen_grad = gate_weights * (
        gate_grad - jnp.sum(gate_weights * gate_grad, axis=-1, keepdims=True)
    )
    logits_grad = jnp.sum(jnp.where(route_match, chosen_grad[:, :, None], 0.0), axis=1)
    router_float = router_weight.astype(jnp.float32)
    normed_grad = normed_grad + jnp.dot(logits_grad, router_float.T, precision=highest)
    router_wgrad = jnp.dot(normed_two.astype(jnp.float32).T, logits_grad, precision=highest)
    hidden_branch, gain_two_grad = norm_back(hidden, gain_b, normed_grad)
    hidden_grad = grad_output + hidden_branch
    branch_low = hidden_grad.astype(jnp.bfloat16)
    out_wgrad = jnp.einsum("tc,td->cd", attended, branch_low, preferred_element_type=jnp.float32)
    attended_grad = jnp.einsum(
        "td,cd->tc", branch_low, out_weight, preferred_element_type=jnp.float32
    ).astype(jnp.bfloat16)
    attended_grad_heads = lax.all_to_all(
        attended_grad, "seq", split_axis=1, concat_axis=0, tiled=True
    )
    row_start = 0
    query_block, scores = block_scores(row_start)
    probs = jnp.exp(scores - log_sums[row_start // block_rows])
    grad_block = attended_grad_heads.reshape(block_rows, kv_local, query_group_width, HEAD_SIZE)
    prob_grad = jnp.einsum(
        "qgrd,kgd->grqk", grad_block, value_three, preferred_element_type=jnp.float32
    )
    row_delta = jnp.sum(probs * prob_grad, axis=-1, keepdims=True)
    score_grad = (probs * (prob_grad - row_delta)).astype(jnp.bfloat16)
    block_query_grad = (
        jnp.einsum("grqk,kgd->qgrd", score_grad, key_three, preferred_element_type=jnp.float32)
        * score_scale
    )
    query_grads = block_query_grad.reshape(block_rows, kv_local * query_group_width * HEAD_SIZE)
    key_grad = (
        jnp.einsum("grqk,qgrd->kgd", score_grad, query_block, preferred_element_type=jnp.float32)
        * score_scale
    )
    value_grad = jnp.einsum(
        "grqk,qgrd->kgd", probs.astype(jnp.bfloat16), grad_block, preferred_element_type=jnp.float32
    )
    query_grad_low = query_grads.astype(jnp.bfloat16)
    key_grad_low = key_grad.reshape(sequence_length, kv_local * HEAD_SIZE).astype(jnp.bfloat16)
    value_grad_low = value_grad.reshape(sequence_length, kv_local * HEAD_SIZE).astype(jnp.bfloat16)
    query_grad_tok, key_grad_token_rows, value_grad_tok = (
        lax.all_to_all(query_grad_low, "seq", split_axis=0, concat_axis=1, tiled=True),
        lax.all_to_all(key_grad_low, "seq", split_axis=0, concat_axis=1, tiled=True),
        lax.all_to_all(value_grad_low, "seq", split_axis=0, concat_axis=1, tiled=True),
    )
    query_back = unrotate(
        query_grad_tok.astype(jnp.float32).reshape(token_count, QUERY_HEADS, HEAD_SIZE),
        cosine_table,
        sine_values,
    ).reshape(token_count, query_columns)
    key_back = unrotate(
        key_grad_token_rows.astype(jnp.float32).reshape(token_count, KEY_VALUE_HEADS, HEAD_SIZE),
        cosine_table,
        sine_values,
    ).reshape(token_count, key_value_columns)
    projected_grad = jnp.concatenate(
        [query_back, key_back, value_grad_tok.astype(jnp.float32)], 1
    ).astype(jnp.bfloat16)
    qkv_wgrad = jnp.einsum(
        "td,tc->dc", normed_one, projected_grad, preferred_element_type=jnp.float32
    )
    normed_one_grad = jnp.einsum(
        "tc,dc->td", projected_grad, qkv_weight, preferred_element_type=jnp.float32
    )
    rows_branch, gain_one_grad = norm_back(token_rows, gain_a, normed_one_grad)
    input_grad = (hidden_grad + rows_branch).astype(jnp.bfloat16)[None]
    (
        shard_gain_one,
        shard_qkv,
        shard_out,
        shard_gain_two,
        shard_router,
        shard_gate_up,
        shard_down,
    ) = (
        lax.psum_scatter(gain_one_grad, "dp", scatter_dimension=0, tiled=True),
        lax.psum_scatter(qkv_wgrad, "dp", scatter_dimension=0, tiled=True),
        lax.psum_scatter(out_wgrad, "dp", scatter_dimension=0, tiled=True),
        lax.psum_scatter(gain_two_grad, "dp", scatter_dimension=0, tiled=True),
        lax.psum_scatter(router_wgrad, "dp", scatter_dimension=0, tiled=True),
        lax.psum_scatter(gate_up_wgrad, "dp", scatter_dimension=0, tiled=True),
        lax.psum_scatter(down_wgrad, "dp", scatter_dimension=0, tiled=True),
    )
    summed = (
        lax.psum(shard_gain_one.astype(jnp.bfloat16), "seq").astype(jnp.float32),
        lax.psum(shard_qkv.astype(jnp.bfloat16), "seq").astype(jnp.float32),
        lax.psum(shard_out.astype(jnp.bfloat16), "seq").astype(jnp.float32),
        lax.psum(shard_gain_two.astype(jnp.bfloat16), "seq").astype(jnp.float32),
        lax.psum(shard_router.astype(jnp.bfloat16), "seq").astype(jnp.float32),
        lax.psum(shard_gate_up.astype(jnp.bfloat16), "seq").astype(jnp.float32),
        lax.psum(shard_down.astype(jnp.bfloat16), "seq").astype(jnp.float32),
        lax.psum(stat_sums.astype(jnp.bfloat16), "seq").astype(jnp.float32),
    )
    stream_rms = jnp.sqrt(summed[7] / (sequence_length * MODEL_WIDTH)).reshape(1, 2)
    return (
        output,
        input_grad,
        summed[0],
        summed[1],
        summed[2],
        summed[3],
        summed[4],
        summed[5],
        summed[6],
        stream_rms,
    )


def solution(mesh):
    placed = (
        P("dp", "seq", None),
        P("dp", "seq"),
        P("dp", "seq", None),
        P("dp"),
        P("dp", None),
        P("dp", None),
        P("dp"),
        P("dp", None),
        P("dp", None, None),
        P("dp", None, None),
        P("dp", "seq", None),
    )
    return jax.shard_map(
        body,
        mesh=mesh,
        in_specs=placed,
        out_specs=(
            P("dp", "seq", None),
            P("dp", "seq", None),
            P("dp"),
            P("dp", None),
            P("dp", None),
            P("dp"),
            P("dp", None),
            P("dp", None, None),
            P("dp", None, None),
            P("dp", None),
        ),
        check_vma=False,
    )
```

profile of v0, /device:TPU:0, one launch (start us, length us, event | category | flops | bytes accessed | tf_op | source)
XLA Modules:
  0.0 1841.7 jit_solution(11289706347054955673)
XLA Ops:
  8.8 4.1 copy.149
  16.7 35.8 %all-reduce.7 = (bf16[1024]{0:T(1024)(128)(2,1)S(1)}, bf16[1024]{0:T(1024)(128)(2,1)S(1)}) all-reduce(bf16[1024]{0:T(1024)(128)(2,1)S(1)} %dynamic-update-slice, bf16[1024]{0:T(1024)(128)(2,1)S(1)} %dynamic-update-slice.1), channel_id=1, replica_groups=mesh['seq'=2,'dp'=16] {'dp'}, use_global_device_ids=true, to_apply=%add.2 | all-reduce | flops 2048 | bytes 8192
  52.5 4.2 all-gather
  57.6 4.5 reduce-window.36
  65.4 8.1 scatter_custom_fusion
  75.4 3.5 fusion.58
  81.6 4.1 all-to-all-start
  85.7 2.0 copy.133
  89.7 2.0 copy.134
  93.6 2.6 copy.138
  98.6 2.5 copy.139
  101.1 4.1 all-to-all-start.1
  107.8 2.7 all-to-all-done.1
  110.5 3.7 all-to-all-start.2
  117.3 3.5 all-to-all-done.2
  124.3 2.0 copy-done
  129.0 3.5 all-to-all-start.3
  132.6 18.3 all-gather.1
  151.3 12.5 gather_fusion.3
  163.8 2.6 multiply_reduce_fusion.4
  168.6 18.9 %gather_fusion.2 = f32[3584]{0:T(1024)S(1)} fusion(f32[2049]{0:T(1024)S(1)} %pad_maximum_fusion.10, s32[4096]{0:T(1024)S(1)} %get-tuple-element.83), kind=kCustom, calls=%fused_computation.2 | custom fusion | bytes 43008 | tf_op jit(solution)/shard_map/gather | solution.py:205
  187.6 11.9 gather_fusion
  199.6 75.6 %all-gather.11.cloned.1.call-done = bf16[1024,16,1024]{2,0,1:T(8,128)(2,1)} async-done(((bf16[64,16,1024]{2,0,1:T(8,128)(2,1)}), bf16[1024,16,1024]{2,0,1:T(8,128)(2,1)}) %all-gather.11.cloned.1.call-update) | async-done | bytes 33554448 | tf_op jit(solution)/shard_map/all_gather | solution.py:215
  275.1 23.0 %fusion.81 = f32[16,224,1024]{2,1,0:T(8,128)} fusion(bf16[16,224,1024]{2,1,0:T(8,128)(2,1)} %bitcast.243, bf16[1024,16,1024]{2,0,1:T(8,128)(2,1)} %all-gather.11.cloned.1.call-done), kind=kOutput, calls=%fused_computation.184 | convolution fusion | flops 7516192768 | bytes 55574528 | tf_op jit(solution)/shard_map/ecd,def->ecf/dot_general | solution.py:218
  298.1 105.8 %all-gather.13.cloned.1.call-done = bf16[512,16,1024]{2,0,1:T(8,128)(2,1)} async-done(((bf16[32,16,1024]{2,0,1:T(8,128)(2,1)}), bf16[512,16,1024]{2,0,1:T(8,128)(2,1)}) %all-gather.13.cloned.1.call-update) | async-done | bytes 16777232 | tf_op jit(solution)/shard_map/all_gather | solution.py:216
  404.0 24.3 %multiply_convert_fusion.2 = (bf16[16,224,512]{2,1,0:T(8,128)(2,1)}, bf16[16,224,512]{2,1,0:T(8,128)(2,1)}, bf16[16,224,512]{2,1,0:T(8,128)(2,1)}) fusion(f32[16,224,1024]{2,1,0:T(8,128)} %fusion.81, bf16[512,16,1024]{2,0,1:T(8,128)(2,1)} %all-gather.13.cloned.1.call-done, f32[16,224,1024]{2,1,0:T(8,128)} %bitcast.241, f32[16,224]{1,0:T(8,128)S(1)} %mul.376), kind=kOutput, calls=%fused_computation.26 | convolution fusion | flops 3792961536 | bytes 57161728 | tf_op jit(solution)/shard_map/ecd,fed->ecf/dot_general | solution.py:223
  428.3 21.6 %fusion.8 = f32[16,224,1024]{2,1,0:T(8,128)} fusion(bf16[1024,16,1024]{2,0,1:T(8,128)(2,1)} %all-gather.11.cloned.1.call-done, bf16[16,224,512]{2,1,0:T(8,128)(2,1)} %get-tuple-element.50, bf16[16,224,512]{2,1,0:T(8,128)(2,1)} %get-tuple-element.49), kind=kOutput, calls=%fused_computation.31 | convolution fusion | flops 7530872832 | bytes 55574528 | tf_op jit(solution)/shard_map/ecf,def->ecd/dot_general | solution.py:233
  449.9 17.1 gather_fusion.4
  467.0 6.5 bitcast_reduce_fusion
  473.5 13.5 fusion.82
  487.1 17.0 gather_fusion.1
  504.2 6.6 fusion.3
  511.0 2.8 multiply_reduce_fusion.1
  513.8 3.1 multiply_reduce_fusion
  517.0 2.7 fusion.54
  519.7 2.4 convolution_convert_fusion
  522.9 3.5 all-to-all-start.4
  526.4 8.6 all-to-all-done.4
  536.1 5.5 fusion
  541.6 4.7 fusion.2
  546.3 2.0 copy-done.1
  550.5 3.4 all-to-all-start.6
  553.9 4.9 fusion.27
  561.6 3.5 all-to-all-start.5
  565.4 7.6 all-to-all-done.5
  573.0 3.4 all-to-all-start.7
  577.0 4.6 all-to-all-done.7
  581.6 4.7 fusion.47
  586.3 20.1 %convolution_bitcast_fusion.1 = f32[512,16,1024]{0,2,1:T(8,128)} fusion(bf16[16,224,512]{2,1,0:T(8,128)(2,1)} %get-tuple-element.51, f32[16,224,1024]{2,1,0:T(8,128)} %bitcast.242, f32[16,224]{1,0:T(8,128)S(1)} %mul.376), kind=kOutput, calls=%fused_computation.8 | convolution fusion | flops 3765436416 | bytes 51918848 | tf_op jit(solution)/shard_map/ecf,ecd->fed/dot_general | solution.py:226
  606.4 34.0 %copy.163 = f32[512,16,1024]{2,1,0:T(8,128)} copy(f32[512,16,1024]{0,2,1:T(8,128)} %convolution_bitcast_fusion.1) | data formatting | bytes 67108864 | tf_op jit(solution)/shard_map/ecf,ecd->fed/transpose | solution.py:226
  640.6 29.2 %convolution_bitcast_fusion = f32[1024,16,1024]{0,2,1:T(8,128)} fusion(bf16[16,224,1024]{2,1,0:T(8,128)(2,1)} %bitcast.244, bf16[16,224,512]{2,1,0:T(8,128)(2,1)} %get-tuple-element.50, bf16[16,224,512]{2,1,0:T(8,128)(2,1)} %get-tuple-element.49), kind=kOutput, calls=%fused_computation.6 | convolution fusion | flops 7530872832 | bytes 81788928 | tf_op jit(solution)/shard_map/ecd,ecf->def/dot_general | solution.py:230
  669.7 68.0 %copy.162 = f32[1024,16,1024]{2,1,0:T(8,128)} copy(f32[1024,16,1024]{0,2,1:T(8,128)} %convolution_bitcast_fusion) | data formatting | bytes 134217728 | tf_op jit(solution)/shard_map/ecd,ecf->def/transpose | solution.py:230
  743.9 287.7 %reduce-scatter.14.cloned.1.call-done = f32[32,16,1024]{2,1,0:T(8,128)} async-done(((f32[512,16,1024]{2,1,0:T(8,128)}), f32[32,16,1024]{2,1,0:T(8,128)}) %reduce-scatter.14.cloned.1.call-update) | async-done | bytes 2097168 | tf_op jit(solution)/shard_map/reduce_scatter | solution.py:325
  1031.6 2.8 convert_element_type.262
  1034.4 633.0 %reduce-scatter.12.cloned.1.call-done = f32[64,16,1024]{2,1,0:T(8,128)} async-done(((f32[1024,16,1024]{2,1,0:T(8,128)}), f32[64,16,1024]{2,1,0:T(8,128)}) %reduce-scatter.12.cloned.1.call-update) | async-done | bytes 4194320 | tf_op jit(solution)/shard_map/reduce_scatter | solution.py:324
  1667.4 3.8 convert_element_type.260
  1673.4 53.5 %reduce-scatter.16.cloned.1.call-done = f32[64,16]{1,0:T(8,128)} async-done(((f32[1024,16]{1,0:T(8,128)}), f32[64,16]{1,0:T(8,128)}) %reduce-scatter.16.cloned.1.call-update) | async-done | bytes 4112
  1727.7 4.5 fusion.39
  1732.2 30.1 %all-reduce.6 = (bf16[1024]{0:T(1024)(128)(2,1)S(1)}, bf16[1024]{0:T(1024)(128)(2,1)S(1)}) all-reduce(f32[1024]{0:T(1024)S(1)} %get-tuple-element.34, f32[1024]{0:T(1024)S(1)} %copy-done.48), channel_id=3, replica_groups=mesh['seq'=2,'dp'=16] {'dp'}, use_global_device_ids=true, to_apply=%region_24.25.clone | all-reduce | flops 2048 | bytes 12288
  1762.5 5.3 all-reduce.8
  1769.9 2.3 fusion.44
  1772.2 51.8 %all-reduce.12.cloned.1.call-done = (bf16[64,2048]{1,0:T(8,128)(2,1)}, bf16[64,1024]{1,0:T(8,128)(2,1)}, bf16[64,16,1024]{2,1,0:T(8,128)(2,1)}, bf16[32,16,1024]{2,1,0:T(8,128)(2,1)}) async-done(((bf16[64,2048]{1,0:T(8,128)(2,1)}, bf16[64,1024]{1,0:T(8,128)(2,1)}, bf16[64,16,1024]{2,1,0:T(8,128)(2,1)}, bf16[32,16,1024]{2,1,0:T(8,128)(2,1)}), (bf16[64,2048]{1,0:T(8,128)(2,1)}, bf16[64,1024]{1,0:T(8,128)(2,1)}, ...) | async-done | bytes 3538960 | tf_op jit(solution)/shard_map/psum | solution.py:329
  1827.5 2.8 convert_element_type.263
  1830.3 4.1 convert_element_type.261
  (278 shorter events, 55.4 us)
Async XLA Ops:
  7.2 7.8 copy-start.58
  7.2 7.4 copy-start.40
  7.2 9.0 copy-start.60
  7.2 9.2 copy-start.61
  7.2 45.3 %copy-start.59 = (s32[1,256]{1,0:T(1,128)S(1)}, s32[1,256]{1,0:T(1,128)}, u32[]{:S(2)}) copy-start(s32[1,256]{1,0:T(1,128)} %param.12) | copy-start | bytes 3076
  7.2 68.2 %all-gather.7.cloned.1.call-start = ((), (), s32[]{:S(2)}) async-start(), calls=%async_computation.13 | async-start | bytes 4456448 | tf_op jit(solution)/shard_map/all_gather | solution.py:121
  8.0 155.8 %all-gather.9.cloned.1.call-start = ((), (), s32[]{:S(2)}) async-start(), calls=%async_computation.14 | async-start | bytes 2228224 | tf_op jit(solution)/shard_map/all_gather | solution.py:122
  8.7 64.9 %copy-start.10 = (bf16[1,256,1024]{2,1,0:T(8,128)(2,1)S(1)}, bf16[1,256,1024]{2,1,0:T(8,128)(2,1)}, u32[]{:S(2)}) copy-start(bf16[1,256,1024]{2,1,0:T(8,128)(2,1)} %param.11) | copy-start | bytes 1572868
  8.7 266.4 %all-gather.11.cloned.1.call-start = ((), (), s32[]{:S(2)}) async-start(), calls=%async_computation.15 | async-start | bytes 35651584 | tf_op jit(solution)/shard_map/all_gather | solution.py:215
  12.9 391.1 %all-gather.13.cloned.1.call-start = ((), (), s32[]{:S(2)}) async-start(), calls=%async_computation.16 | async-start | bytes 17825792 | tf_op jit(solution)/shard_map/all_gather | solution.py:216
  52.5 26.4 %copy-start.34 = (f32[1024]{0:T(1024)}, f32[1024]{0:T(1024)S(1)}, u32[]{:S(2)}) copy-start(f32[1024]{0:T(1024)S(1)} %convert_element_type.206) | copy-start | bytes 12292
  63.7 10.8 copy-start.22
  73.6 23.9 %copy-start.24 = (f32[256,64]{0,1:T(8,128)}, f32[256,64]{0,1:T(8,128)S(1)}, u32[]{:S(2)}) copy-start(f32[256,64]{0,1:T(8,128)S(1)} %pad_maximum_fusion.9) | copy-start | bytes 196612
  74.4 15.2 copy-start.53
  81.6 19.5 %all-to-all-start = ((bf16[256,2,256]{2,0,1:T(8,128)(2,1)}), bf16[256,2,256]{2,0,1:T(8,128)(2,1)}, u32[]{:S(2)}, u32[]{:S(2)}) async-start(bf16[256,2,256]{2,0,1:T(8,128)(2,1)} %bitcast.262), calls=%async_computation | async-start | bytes 524288 | tf_op jit(solution)/shard_map/all_to_all | solution.py:157
  93.6 20.6 %copy-start.20 = (bf16[1,256,1024]{2,1,0:T(8,128)(2,1)S(1)}, bf16[1,256,1024]{2,1,0:T(8,128)(2,1)}, u32[]{:S(2)}) copy-start(bf16[1,256,1024]{2,1,0:T(8,128)(2,1)} %param.21) | copy-start | bytes 1572868
  101.1 9.4 all-to-all-start.1
  110.5 10.3 all-to-all-start.2
  114.3 36.8 %copy-start.8 = (f32[256,1024]{1,0:T(8,128)}, f32[256,1024]{1,0:T(8,128)S(1)}, u32[]{:S(2)}) copy-start(f32[256,1024]{1,0:T(8,128)S(1)} %bitcast_convert_fusion) | copy-start | bytes 3145732
  115.9 8.4 copy-start.26
  126.4 6.2 copy-start.57
  126.4 24.7 %copy-start.29 = (s32[256,8,1]{1,0,2:T(8,128)S(1)}, s32[256,8,1]{1,0,2:T(8,128)}, u32[]{:S(2)}) copy-start(s32[256,8,1]{1,0,2:T(8,128)} %compare_select_fusion) | copy-start | bytes 24580
  129.0 34.8 %all-to-all-start.3 = ((bf16[2,256,512]{1,2,0:T(8,128)(2,1)}), bf16[2,256,512]{1,2,0:T(8,128)(2,1)S(1)}, u32[]{:S(2)}, u32[]{:S(2)}) async-start(bf16[2,256,512]{1,2,0:T(8,128)(2,1)} %copy.143), calls=%async_computation.3 | async-start | bytes 1048576 | tf_op jit(solution)/shard_map/all_to_all | solution.py:193
  132.5 607.9 %reduce-scatter.10.cloned.1.call-start = ((), (), s32[]{:S(2)}) async-start(), calls=%async_computation.18 | async-start | bytes 4456448 | tf_op jit(solution)/shard_map/reduce_scatter | solution.py:321
  132.5 34.5 %copy-start.42 = (f32[1024]{0:T(1024)}, f32[1024]{0:T(1024)S(1)}, u32[]{:S(2)}) copy-start(f32[1024]{0:T(1024)S(1)} %convert_element_type.215) | copy-start | bytes 12292
  151.0 16.6 copy-start.30
  163.8 23.7 %copy-start.16 = (bf16[2,256,512]{1,2,0:T(8,128)(2,1)}, bf16[2,256,512]{1,2,0:T(8,128)(2,1)S(1)}, u32[]{:S(2)}) copy-start(bf16[2,256,512]{1,2,0:T(8,128)(2,1)S(1)} %all-to-all-done.3) | copy-start | bytes 1572868
  167.6 20.0 %copy-start.12 = (bf16[256,1024]{1,0:T(8,128)(2,1)}, bf16[256,1024]{1,0:T(8,128)(2,1)S(1)}, u32[]{:S(2)}) copy-start(bf16[256,1024]{1,0:T(8,128)(2,1)S(1)} %multiply_convert_fusion.6) | copy-start | bytes 1572868
  467.0 6.5 copy-start.3
  487.1 17.1 copy-start.9
  504.1 6.7 copy-start.33
  504.1 6.7 copy-start.47
  504.1 6.7 copy-start.50
  504.1 6.8 copy-start.41
  504.2 6.8 copy-start.5
  504.2 6.8 copy-start.31
  504.2 6.8 copy-start.43
  504.2 6.8 copy-start.52
  504.2 9.6 copy-start.21
  504.2 9.6 copy-start.56
  504.2 12.7 copy-start.17
  511.0 8.7 copy-start.36
  516.9 9.4 copy-start.39
  516.9 9.5 copy-start.45
  519.6 16.4 copy-start.27
  522.9 12.2 all-to-all-start.4
  541.6 6.7 copy-start.15
  548.3 10.6 copy-start.19
  550.5 11.1 all-to-all-start.6
  553.9 11.2 copy-start.25
  558.9 6.4 copy-start.23
  561.6 11.4 all-to-all-start.5
  565.1 16.5 copy-start.11
  565.1 16.4 copy-start.35
  565.1 16.4 copy-start.54
  573.0 8.6 all-to-all-start.7
  576.4 165.6 %reduce-scatter.8.cloned.1.call-start = ((), (), s32[]{:S(2)}) async-start(), calls=%async_computation.17 | async-start | bytes 8912896 | tf_op jit(solution)/shard_map/reduce_scatter | solution.py:320
  586.3 445.4 %reduce-scatter.14.cloned.1.call-start = ((), (), s32[]{:S(2)}) async-start(), calls=%async_computation.20 | async-start | bytes 35651584 | tf_op jit(solution)/shard_map/reduce_scatter | solution.py:325
  640.5 1026.9 %reduce-scatter.12.cloned.1.call-start = ((), (), s32[]{:S(2)}) async-start(), calls=%async_computation.19 | async-start | bytes 71303168 | tf_op jit(solution)/shard_map/reduce_scatter | solution.py:324
  737.7 989.2 %reduce-scatter.16.cloned.1.call-start = ((), (), s32[]{:S(2)}) async-start(), calls=%async_computation.21 | async-start | bytes 557056
  740.3 1083.8 %all-reduce.12.cloned.1.call-start = ((), (), s32[]{:S(2)}) async-start(), calls=%async_computation.22 | async-start | bytes 7077888 | tf_op jit(solution)/shard_map/psum | solution.py:329
  1671.3 61.0 %copy-start.48 = (f32[1024]{0:T(1024)S(1)}, f32[1024]{0:T(1024)}, u32[]{:S(2)}) copy-start(f32[1024]{0:T(1024)} %get-tuple-element.32) | copy-start | bytes 12292
  1671.3 98.6 %copy-start.7 = (f32[256,1024]{1,0:T(8,128)S(1)}, f32[256,1024]{1,0:T(8,128)}, u32[]{:S(2)}) copy-start(f32[256,1024]{1,0:T(8,128)} %copy-done.6) | copy-start | bytes 3145732
  1671.3 98.6 %copy-start.55 = (f32[256]{0:T(256)S(1)}, f32[256]{0:T(256)}, u32[]{:S(2)}) copy-start(f32[256]{0:T(256)} %get-tuple-element.69) | copy-start | bytes 3076
  (16 other events, 43.1 us)
Sparse Core Ops, SparseCore 0:
  10.2 53.3 all-gather.6
  65.8 40.0 all-gather.8
  108.1 167.0 all-gather.10
  277.2 126.7 all-gather.12
  519.8 70.9 reduce-scatter.9
  594.7 102.4 reduce-scatter.7
  701.4 330.1 reduce-scatter.13
  1035.9 631.5 reduce-scatter.11
  1671.6 55.2 reduce-scatter.15
  1730.4 93.6 all-reduce.11
where the time goes:
time: 1850 us; the launch traced here: 1840 us
  waiting for transfers between devices  1240 us (67%)
  local copies, waits for them, and re-layouts  227 us (12%)
  matrix products  172 us (9%)
  blocking collectives  93.7 us (5%)
  other arithmetic  65.2 us (4%)
  starting transfers between devices  29.7 us (2%)
    reduce_scatter x1, waiting for transfers between devices, body(): lax.psum_scatter(gate_up_wgrad, 'dp', scatter_dimension=0, tiled=True)  633 us
    reduce_scatter x1, waiting for transfers between devices, body(): lax.psum_scatter(down_wgrad, 'dp', scatter_dimension=0, tiled=True)  288 us
    all_gather x1, waiting for transfers between devices, body(): lax.all_gather(w_down, 'dp', axis=0, tiled=True)  106 us
    all_gather x1, waiting for transfers between devices, body(): lax.all_gather(w_gate_up, 'dp', axis=0, tiled=True)  75.6 us
    transpose x1, local copies, waits for them, and re-layouts, body(): jnp.einsum('ecd,ecf->def', dispatched, gate_up_grad, preferred_element_ty...  68 us
    unnamed x2, blocking collectives  65.9 us
    unnamed x11, waiting for transfers between devices  55 us
    psum x1, waiting for transfers between devices, body(): lax.psum(shard_qkv.astype(jnp.bfloat16), 'seq').astype(jnp.float32)  51.8 us
  transfers between devices with their start and end apart: 18, of which 11 were waited for; matrix products, arithmetic and copies ran while one was open for 18% of the time, Pallas kernels for 0%

commit v1 on v0

v1 whole, which is shorter than its diff:
```python
import jax
import jax.numpy as jnp
from jax import lax
from jax.sharding import PartitionSpec as P

MODEL_WIDTH = 1024
QUERY_HEADS = 16
KEY_VALUE_HEADS = 8
HEAD_SIZE = 64
F = 512
EXPERTS = 16
TOPK = 8

epsilon = 1e-06
rope_base = 10000.0
highest = lax.Precision.HIGHEST
masked_score = -1e30
f32 = jnp.float32
bf16 = jnp.bfloat16


def inverse_rms(rows):
    return lax.rsqrt(jnp.mean(rows * rows, axis=-1, keepdims=True) + epsilon)


def norm_back(rows, gain_row, upstream):
    inverse = inverse_rms(rows)
    gain_grad = jnp.sum(upstream * rows * inverse, axis=0)
    scaled = upstream * gain_row
    rows_grad = inverse * scaled - rows * inverse**3 * jnp.mean(scaled * rows, axis=-1, keepdims=True)
    return rows_grad, gain_grad


def rope_tables(positions):
    half = HEAD_SIZE // 2
    frequency = rope_base ** (-(jnp.arange(half, dtype=f32) * 2.0) / HEAD_SIZE)
    angles = positions.astype(f32)[:, None] * frequency[None, :]
    cosine, sine = jnp.cos(angles), jnp.sin(angles)
    return jnp.concatenate([cosine, cosine], 1), jnp.concatenate([sine, sine], 1)


def rotary_apply(rows, cosine, sine):
    half = HEAD_SIZE // 2
    turned = jnp.concatenate([-rows[..., half:], rows[..., :half]], -1)
    return rows * cosine[:, None, :] + turned * sine[:, None, :]


def unrotate(rows, cosine, sine):
    half = HEAD_SIZE // 2
    scaled = rows * sine[:, None, :]
    back = jnp.concatenate([scaled[..., half:], -scaled[..., :half]], -1)
    return rows * cosine[:, None, :] + back


def make_body(n_dp):
    groups_count = n_dp // EXPERTS
    token_groups = (
        None
        if groups_count == 1
        else [[g * EXPERTS + j for j in range(EXPERTS)] for g in range(groups_count)]
    )
    expert_groups = [[g * EXPERTS + j for g in range(groups_count)] for j in range(EXPERTS)]

    def token_gather(rows):
        return lax.all_gather(rows, "dp", axis=0, tiled=True, axis_index_groups=token_groups)

    def token_scatter(rows):
        return lax.psum_scatter(
            rows, "dp", scatter_dimension=0, tiled=True, axis_index_groups=token_groups
        )

    def exchange(rows, split, concat):
        return lax.all_to_all(
            rows, "dp", split_axis=split, concat_axis=concat, tiled=True, axis_index_groups=token_groups
        )

    def expert_weight(shard):
        whole = exchange(shard, 1, 0)
        if groups_count > 1:
            whole = lax.all_gather(whole, "dp", axis=0, tiled=True, axis_index_groups=expert_groups)
        return whole[:, 0]

    def expert_weight_grad(grad):
        if groups_count > 1:
            grad = lax.psum_scatter(
                grad, "dp", scatter_dimension=0, tiled=True, axis_index_groups=expert_groups
            )
        return exchange(grad.astype(bf16)[:, None, :], 0, 1)

    def body(
        tokens, starts, routes, gain_one, query_key_value_weight, w_out,
        gain_two, w_router, w_gate_up, w_down, cotangent,
    ):
        count = tokens.shape[1]
        seq_rank = lax.axis_index("seq")
        expert_rank = lax.axis_index("dp") % EXPERTS
        query_columns = QUERY_HEADS * HEAD_SIZE
        key_columns = KEY_VALUE_HEADS * HEAD_SIZE
        group = QUERY_HEADS // KEY_VALUE_HEADS
        forward_pair, back_pair = [(0, 1)], [(1, 0)]

        tokens_before = lax.ppermute(tokens[0], "seq", forward_pair)
        starts_before = lax.ppermute(starts, "seq", forward_pair)
        gather = lambda value: lax.all_gather(value, "dp", axis=0, tiled=True)
        qkv_weight = gather(query_key_value_weight)
        out_weight = gather(w_out)
        router_weight = gather(w_router)
        gain_a = gather(gain_one).astype(f32)
        gain_b = gather(gain_two).astype(f32)
        gate_up_weight = expert_weight(w_gate_up)
        down_weight = expert_weight(w_down)
        grad_all = token_gather(cotangent[0])

        token_rows = tokens[0].astype(f32)
        grad_output = cotangent[0].astype(f32)
        both = 2 * count
        index = jnp.arange(both, dtype=jnp.int32)
        flags = jnp.concatenate([starts_before[0], starts[0]])
        begins = (flags > 0) | (index == jnp.where(seq_rank == 0, count, 0))
        last_begin = jnp.max(
            jnp.where(begins[None, :] & (index[None, :] <= index[:, None]), index[None, :], 0), axis=1
        )
        cosine_all, sine_all = rope_tables(index - last_begin)
        cosine, sine = cosine_all[count:], sine_all[count:]

        rows_all = jnp.concatenate([tokens_before.astype(f32), token_rows], 0)
        normed_all = (rows_all * inverse_rms(rows_all) * gain_a).astype(bf16)
        normed_one = normed_all[count:]
        projected_q = jnp.dot(normed_one, qkv_weight[:, :query_columns], preferred_element_type=f32)
        projected_kv = jnp.dot(normed_all, qkv_weight[:, query_columns:], preferred_element_type=f32)
        queries = rotary_apply(
            projected_q.reshape(count, QUERY_HEADS, HEAD_SIZE), cosine, sine
        ).astype(bf16).reshape(count, KEY_VALUE_HEADS, group, HEAD_SIZE)
        keys = rotary_apply(
            projected_kv[:, :key_columns].reshape(both, KEY_VALUE_HEADS, HEAD_SIZE), cosine_all, sine_all
        ).astype(bf16)
        values = projected_kv[:, key_columns:].astype(bf16).reshape(both, KEY_VALUE_HEADS, HEAD_SIZE)

        scale = HEAD_SIZE ** (-0.5)
        allowed = (index[None, :] <= index[count:, None]) & (index[None, :] >= last_begin[count:, None])
        scores = jnp.einsum("qgrd,kgd->grqk", queries, keys, preferred_element_type=f32) * scale
        scores = jnp.where(allowed[None, None], scores, masked_score)
        top = jnp.max(scores, axis=-1, keepdims=True)
        exps = jnp.exp(scores - top)
        probs = exps / jnp.sum(exps, axis=-1, keepdims=True)
        probs_low = probs.astype(bf16)
        attended = jnp.einsum(
            "grqk,kgd->qgrd", probs_low, values, preferred_element_type=f32
        ).reshape(count, query_columns).astype(bf16)
        hidden = token_rows + jnp.dot(attended, out_weight, preferred_element_type=f32)
        normed_two = (hidden * inverse_rms(hidden) * gain_b).astype(bf16)
        logits = jnp.dot(normed_two, router_weight, preferred_element_type=f32)
        expert_ids = jnp.arange(EXPERTS, dtype=jnp.int32)
        chosen = jnp.any(routes[0][:, :, None] == expert_ids[None, None, :], axis=1)
        gates = jax.nn.softmax(jnp.where(chosen, logits, -jnp.inf), axis=-1)

        rows_in = token_gather(normed_two)
        gates_all = token_gather(gates)
        gate = lax.dynamic_slice_in_dim(gates_all, expert_rank, 1, axis=1)
        gate_up = jnp.dot(rows_in, gate_up_weight, preferred_element_type=f32)
        gate_part, up_part = gate_up[:, :F], gate_up[:, F:]
        sigmoid = jax.nn.sigmoid(gate_part)
        silu = gate_part * sigmoid
        act = (silu * up_part).astype(bf16)
        expert_out = jnp.dot(act, down_weight, preferred_element_type=f32)
        grad_all_wide = grad_all.astype(f32)
        gate_grad_part = jnp.sum(expert_out * grad_all_wide, axis=-1, keepdims=True)
        mixed_part = (gate * expert_out).astype(bf16)
        expert_grad = (gate * grad_all_wide).astype(bf16)
        act_grad = lax.dot_general(
            expert_grad, down_weight, (((1,), (1,)), ((), ())), preferred_element_type=f32
        )
        gate_up_grad = jnp.concatenate(
            [act_grad * up_part * (sigmoid * (1.0 + gate_part * (1.0 - sigmoid))), act_grad * silu], -1
        ).astype(bf16)
        normed_part = lax.dot_general(
            gate_up_grad, gate_up_weight, (((1,), (1,)), ((), ())), preferred_element_type=f32
        ).astype(bf16)
        over_rows = (((0,), (0,)), ((), ()))
        down_wgrad = lax.dot_general(act, expert_grad, over_rows, preferred_element_type=f32)
        gate_up_wgrad = lax.dot_general(rows_in, gate_up_grad, over_rows, preferred_element_type=f32)
        normed_grad = token_scatter(normed_part).astype(f32)
        gate_grad = exchange(gate_grad_part, 0, 1)
        mixed = token_scatter(mixed_part).astype(f32)

        output = (hidden + mixed).astype(bf16)[None]
        stat_sums = jnp.stack([jnp.sum(hidden * hidden), jnp.sum(mixed * mixed)])
        weighted = jnp.where(chosen, gates * gate_grad, 0.0)
        logits_grad = weighted - gates * jnp.sum(weighted, axis=-1, keepdims=True)
        router_wide = router_weight.astype(f32)
        normed_grad = normed_grad + jnp.dot(logits_grad, router_wide.T, precision=highest)
        router_wgrad = jnp.dot(normed_two.astype(f32).T, logits_grad, precision=highest)
        hidden_branch, gain_two_grad = norm_back(hidden, gain_b, normed_grad)
        hidden_grad = grad_output + hidden_branch
        branch_low = hidden_grad.astype(bf16)
        out_wgrad = lax.dot_general(attended, branch_low, over_rows, preferred_element_type=f32)
        attended_grad = lax.dot_general(
            branch_low, out_weight, (((1,), (1,)), ((), ())), preferred_element_type=f32
        ).astype(bf16).reshape(count, KEY_VALUE_HEADS, group, HEAD_SIZE)

        prob_grad = jnp.einsum("qgrd,kgd->grqk", attended_grad, values, preferred_element_type=f32)
        delta = jnp.sum(probs * prob_grad, axis=-1, keepdims=True)
        score_grad = (probs * (prob_grad - delta)).astype(bf16)
        query_grad = (
            jnp.einsum("grqk,kgd->qgrd", score_grad, keys, preferred_element_type=f32) * scale
        ).reshape(count, QUERY_HEADS, HEAD_SIZE)
        key_grad = (
            jnp.einsum("grqk,qgrd->kgd", score_grad, queries, preferred_element_type=f32) * scale
        ).reshape(both, key_columns)
        value_grad = jnp.einsum(
            "grqk,qgrd->kgd", probs_low, attended_grad, preferred_element_type=f32
        ).reshape(both, key_columns)
        kv_grad = jnp.concatenate([key_grad, value_grad], 1)
        kv_back = lax.ppermute(kv_grad[:count].astype(bf16), "seq", back_pair)
        kv_grad = (kv_grad[count:] + kv_back.astype(f32)).astype(bf16).astype(f32)
        query_grad = query_grad.astype(bf16).astype(f32)
        query_back = unrotate(query_grad, cosine, sine).reshape(count, query_columns)
        key_back = unrotate(
            kv_grad[:, :key_columns].reshape(count, KEY_VALUE_HEADS, HEAD_SIZE), cosine, sine
        ).reshape(count, key_columns)
        projected_grad = jnp.concatenate([query_back, key_back, kv_grad[:, key_columns:]], 1).astype(bf16)
        qkv_wgrad = lax.dot_general(normed_one, projected_grad, over_rows, preferred_element_type=f32)
        normed_one_grad = lax.dot_general(
            projected_grad, qkv_weight, (((1,), (1,)), ((), ())), preferred_element_type=f32
        )
        rows_branch, gain_one_grad = norm_back(token_rows, gain_a, normed_one_grad)
        input_grad = (hidden_grad + rows_branch).astype(bf16)[None]

        scatter = lambda value: lax.psum_scatter(value, "dp", scatter_dimension=0, tiled=True)
        shards = (
            scatter(gain_one_grad),
            scatter(qkv_wgrad.astype(bf16)),
            scatter(out_wgrad.astype(bf16)),
            scatter(gain_two_grad),
            scatter(router_wgrad),
            expert_weight_grad(gate_up_wgrad),
            expert_weight_grad(down_wgrad),
            stat_sums,
        )
        summed = [lax.psum(part.astype(bf16), "seq").astype(f32) for part in shards]
        stream_rms = jnp.sqrt(summed[7] / (both * MODEL_WIDTH)).reshape(1, 2)
        return (output, input_grad, *summed[:7], stream_rms)

    return body


def solution(mesh):
    placed = (
        P("dp", "seq", None),
        P("dp", "seq"),
        P("dp", "seq", None),
        P("dp"),
        P("dp", None),
        P("dp", None),
        P("dp"),
        P("dp", None),
        P("dp", None, None),
        P("dp", None, None),
        P("dp", "seq", None),
    )
    return jax.shard_map(
        make_body(mesh.shape["dp"]),
        mesh=mesh,
        in_specs=placed,
        out_specs=(
            P("dp", "seq", None),
            P("dp", "seq", None),
            P("dp"),
            P("dp", None),
            P("dp", None),
            P("dp"),
            P("dp", None),
            P("dp", None, None),
            P("dp", None, None),
            P("dp", None),
        ),
        check_vma=False,
    )
```

time: 1850 us -> 942 us (0.51)
  waiting for transfers between devices: 1240 us -> 476 us
  local copies, waits for them, and re-layouts: 227 us -> 47.4 us
  blocking collectives: 93.7 us -> 154 us
  matrix products: 172 us -> 128 us
  starting transfers between devices: 29.7 us -> 64 us
  other arithmetic: 65.2 us -> 46.5 us
    reduce_scatter x4, waiting for transfers between devices: 921 us -> 201 us  [the longest x2 196 us: token_scatter(): lax.psum_scatter(rows, 'dp', scatter_dimension=0, tiled=True, axis_index_...]
    transpose x2 -> x0, local copies, waits for them, and re-layouts: 102 us -> none  [the longest x1 68 us: body(): jnp.einsum('ecd,ecf->def', dispatched, gate_up_grad, preferred_element_ty...]
    all_gather x4, waiting for transfers between devices: 181 us -> 84.7 us  [the longest x2 52.8 us: token_gather(): lax.all_gather(rows, 'dp', axis=0, tiled=True, axis_index_groups=token_gr...]
    gather x5 -> x0, local copies, waits for them, and re-layouts: 77.4 us -> none  [the longest x1 18.9 us: body(): jnp.concatenate([gate_weights.reshape(-1), jnp.zeros((1,), jnp.float32)])]
    all_gather x2, blocking collectives: 22.6 us -> 84.1 us  [the longest x1 65.6 us: body(): gather = lambda value: lax.all_gather(value, 'dp', axis=0, tiled=True)]
    dot_general x20, matrix products: 171 us -> 120 us  [the longest x1 16.1 us: body(): gate_up = jnp.dot(rows_in, gate_up_weight, preferred_element_type=f32)]
    all_to_all x8 -> x5, waiting for transfers between devices: 27 us -> 67.7 us  [exchange(): lax.all_to_all(rows, 'dp', split_axis=split, concat_axis=concat, tiled=Tr...]
    unnamed x136 -> x71, local copies, waits for them, and re-layouts: 14 us -> 45.9 us
  transfers between devices with their start and end apart: 18 -> 18, of which waited for: 11 -> 13; matrix products, arithmetic and copies ran while one was open for 18% -> 17% of each run, Pallas kernels for 0% -> 0%
where the time goes in v1:
time: 942 us; the launch traced here: 932 us
  waiting for transfers between devices  476 us (51%)
  blocking collectives  154 us (16%)
  matrix products  128 us (14%)
  starting transfers between devices  64 us (7%)
  local copies, waits for them, and re-layouts  47.4 us (5%)
  other arithmetic  46.5 us (5%)
  between operations  16.4 us (2%)
    reduce_scatter x2, waiting for transfers between devices, token_scatter(): lax.psum_scatter(rows, 'dp', scatter_dimension=0, tiled=True, axis_index_...  196 us
    all_to_all x5, waiting for transfers between devices, exchange(): lax.all_to_all(rows, 'dp', split_axis=split, concat_axis=concat, tiled=Tr...  67.7 us
    all_gather x1, blocking collectives, body(): gather = lambda value: lax.all_gather(value, 'dp', axis=0, tiled=True)  65.6 us
    unnamed x2, blocking collectives  63.8 us
    unnamed x11, waiting for transfers between devices  58.9 us
    all_to_all x5, starting transfers between devices, exchange(): lax.all_to_all(rows, 'dp', split_axis=split, concat_axis=concat, tiled=Tr...  55.7 us
    all_gather x2, waiting for transfers between devices, token_gather(): lax.all_gather(rows, 'dp', axis=0, tiled=True, axis_index_groups=token_gr...  52.8 us
    psum x1, waiting for transfers between devices, body(): summed = [lax.psum(part.astype(bf16), 'seq').astype(f32) for part in shards]  51.4 us
  transfers between devices with their start and end apart: 18, of which 13 were waited for; matrix products, arithmetic and copies ran while one was open for 17% of the time, Pallas kernels for 0%

profile of v1, /device:TPU:0, one launch (start us, length us, event | category | flops | bytes accessed | tf_op | source)
XLA Modules:
  0.0 932.1 jit_solution(4451395104480327640)
XLA Ops:
  8.0 4.9 collective-permute-start.1
  19.1 33.8 %all-reduce.5 = (bf16[1024]{0:T(1024)(128)(2,1)S(1)}, bf16[1024]{0:T(1024)(128)(2,1)S(1)}) all-reduce(bf16[1024]{0:T(1024)(128)(2,1)S(1)} %dynamic-update-slice, bf16[1024]{0:T(1024)(128)(2,1)S(1)} %dynamic-update-slice.1), channel_id=1, replica_groups=mesh['seq'=2,'dp'=16] {'dp'}, use_global_device_ids=true, to_apply=%add | all-reduce | flops 2048 | bytes 8192
  55.7 7.9 all-gather.7.cloned.1.call-done
  63.6 2.8 fusion.18
  67.2 2.9 fusion.16
  70.8 6.1 fusion.90
  77.5 4.3 fusion.31
  81.9 23.9 %all-gather.9.cloned.1.call-done = bf16[1024,1024]{1,0:T(8,128)(2,1)} async-done(((bf16[64,1024]{1,0:T(8,128)(2,1)}), bf16[1024,1024]{1,0:T(8,128)(2,1)}) %all-gather.9.cloned.1.call-update) | async-done | bytes 2097168 | tf_op jit(solution)/shard_map/all_gather | solution.py:104
  105.8 2.4 multiply_reduce_fusion.4
  109.8 4.1 copy.103
  113.9 4.5 all-to-all-start
  118.4 65.6 %all-gather.1 = bf16[16,64,16]{1,2,0:T(8,128)(2,1)S(1)} all-gather(bf16[1,64,16]{1,2,0:T(8,128)(2,1)S(1)} %bitcast.211), channel_id=1, replica_groups=mesh['seq'=2,'dp'=16] {'dp'}, dimensions={0}, use_global_device_ids=true | all-gather | bytes 34816 | tf_op jit(solution)/shard_map/all_gather | solution.py:104
  184.2 1.5 copy.104
  186.1 35.3 %all-to-all-start.1 = ((bf16[32,16,1024]{2,0,1:T(8,128)(2,1)}), bf16[32,16,1024]{2,0,1:T(8,128)(2,1)S(1)}, u32[]{:S(2)}, u32[]{:S(2)}) async-start(bf16[32,16,1024]{2,0,1:T(8,128)(2,1)} %copy.104), calls=%async_computation.1 | async-start | bytes 2097152 | tf_op jit(solution)/shard_map/all_to_all | solution.py:73
  221.4 16.1 %fusion.92 = f32[4096,1024]{0,1:T(8,128)} fusion(bf16[4096,1024]{1,0:T(8,128)(2,1)} %all-gather.11.cloned.1.call-done, bf16[1024,1024]{1,0:T(8,128)(2,1)} %bitcast.22), kind=kOutput, calls=%fused_computation.172 | convolution fusion | flops 8589934592 | bytes 27262976 | tf_op jit(solution)/shard_map/dot_general | solution.py:160
  237.5 8.8 multiply_convert_fusion.3
  246.3 9.7 %all-to-all-done.1 = bf16[32,16,1024]{2,0,1:T(8,128)(2,1)S(1)} async-done(((bf16[32,16,1024]{2,0,1:T(8,128)(2,1)}), bf16[32,16,1024]{2,0,1:T(8,128)(2,1)S(1)}, u32[]{:S(2)}, u32[]{:S(2)}) %all-to-all-start.1) | async-done | bytes 1048608 | tf_op jit(solution)/shard_map/all_to_all | solution.py:73
  256.0 52.8 %all-gather.13.cloned.1.call-done = bf16[1,4096,1024]{2,1,0:T(8,128)(2,1)} async-done(((bf16[1,256,1024]{2,1,0:T(8,128)(2,1)}), bf16[1,4096,1024]{2,1,0:T(8,128)(2,1)}) %all-gather.13.cloned.1.call-update) | async-done | bytes 8388624 | tf_op jit(solution)/shard_map/all_gather | solution.py:65
  308.8 12.3 %fusion.2 = (f32[4096]{0:T(1024)}, f32[4096,1024]{1,0:T(8,128)}) fusion(bf16[1,4096,1024]{2,1,0:T(8,128)(2,1)} %all-gather.13.cloned.1.call-done, bf16[4096,512]{0,1:T(8,128)(2,1)} %multiply_convert_fusion.3, bf16[512,1024]{1,0:T(8,128)(2,1)S(1)} %bitcast.192), kind=kOutput, calls=%fused_computation.4 | convolution fusion | flops 4307546112 | bytes 30425088 | tf_op jit(solution)/shard_map/dot_general | solution.py:165
  321.2 3.5 all-to-all-start.2
  324.8 6.4 all-to-all-done.2
  331.2 18.5 %all_gather.29 = f32[4096,16]{0,1:T(8,128)S(1)} all-gather(f32[256,16]{0,1:T(8,128)S(1)} %get-tuple-element.48), channel_id=1, replica_groups=mesh['seq'=2,'dp'=16] {'dp'}, dimensions={0}, use_global_device_ids=true | all-gather | bytes 278528 | tf_op jit(solution)/shard_map/all_gather | solution.py:65
  349.6 13.2 %multiply_convert_fusion.2 = (bf16[4096,512]{0,1:T(8,128)(2,1)S(1)}, bf16[4096,512]{0,1:T(8,128)(2,1)}) fusion(f32[4096,1024]{0,1:T(8,128)} %fusion.92, bf16[512,1024]{1,0:T(8,128)(2,1)S(1)} %bitcast.193, bf16[1,4096,1024]{2,1,0:T(8,128)(2,1)} %all-gather.13.cloned.1.call-done, f32[4096]{0:T(1024)S(1)} %bitcast.207), kind=kOutput, calls=%fused_computation.14 | convolution fusion | flops 4334813184 | bytes 34619392 | tf_op jit(solution)/shard_map/dot_general | solution.py:170
  362.8 2.0 copy-done.25
  364.8 14.0 %convolution_convert_fusion = bf16[4096,1024]{1,0:T(8,128)(2,1)} fusion(bf16[1024,1024]{1,0:T(8,128)(2,1)} %bitcast.22, bf16[4096,512]{0,1:T(8,128)(2,1)} %get-tuple-element.50, bf16[4096,512]{0,1:T(8,128)(2,1)S(1)} %get-tuple-element.49), kind=kOutput, calls=%fused_computation.19 | convolution fusion | flops 8610906112 | bytes 18874368 | tf_op jit(solution)/shard_map/dot_general | solution.py:176
  378.9 9.8 %multiply_convert_fusion = bf16[4096,1024]{1,0:T(8,128)(2,1)} fusion(f32[4096,1024]{1,0:T(8,128)} %get-tuple-element.77, f32[4096]{0:T(1024)S(1)} %bitcast.208), kind=kLoop, calls=%fused_computation.5 | loop fusion | flops 8388608 | bytes 25182208 | tf_op jit(solution)/shard_map/convert_element_type | solution.py:168
  388.8 91.9 %reduce-scatter.10.cloned.1.call-done = bf16[256,1024]{1,0:T(8,128)(2,1)} async-done(((bf16[4096,1024]{1,0:T(8,128)(2,1)}), bf16[256,1024]{1,0:T(8,128)(2,1)}) %reduce-scatter.10.cloned.1.call-update) | async-done | bytes 524304 | tf_op jit(solution)/shard_map/reduce_scatter | solution.py:68
  480.6 2.6 multiply_reduce_fusion.1
  483.3 104.4 %reduce-scatter.8.cloned.1.call-done = bf16[256,1024]{1,0:T(8,128)(2,1)} async-done(((bf16[4096,1024]{1,0:T(8,128)(2,1)}), bf16[256,1024]{1,0:T(8,128)(2,1)}) %reduce-scatter.8.cloned.1.call-update) | async-done | bytes 524304 | tf_op jit(solution)/shard_map/reduce_scatter | solution.py:68
  587.7 3.1 convert_add_fusion.1
  590.7 3.1 convolution_convert_fusion.2
  593.8 2.3 convolution_convert_fusion.3
  596.7 4.9 fusion.3
  601.6 4.7 fusion.5
  606.3 5.0 fusion.20
  612.8 1.4 collective-permute-start.2
  615.6 12.5 %collective-permute-done.2 = bf16[256,1024]{0,1:T(8,128)(2,1)S(1)} collective-permute-done((bf16[256,1024]{0,1:T(8,128)(2,1)S(1)}, bf16[256,1024]{0,1:T(8,128)(2,1)S(1)}, u32[]{:S(2)}, u32[]{:S(2)}) %collective-permute-start.2) | collective-permute-done | bytes 524320 | tf_op jit(solution)/shard_map/ppermute | solution.py:214
  629.3 3.4 convolution_convert_fusion.1
  632.7 9.3 %fusion.27 = bf16[512,1,1024]{2,0,1:T(8,128)(2,1)S(1)} fusion(bf16[4096,512]{0,1:T(8,128)(2,1)} %multiply_convert_fusion.3, bf16[1,4096,1024]{2,1,0:T(8,128)(2,1)} %all-gather.13.cloned.1.call-done, f32[4096]{0:T(1024)S(1)} %bitcast.209), kind=kOutput, calls=%fused_computation.45 | convolution fusion | flops 4308074496 | bytes 13647872 | tf_op jit(solution)/shard_map/dot_general | solution.py:180
  642.6 1.5 reduce.1
  644.1 1.6 reshape.236
  645.7 5.2 all-to-all-start.4
  650.9 14.8 %convert_bitcast_fusion = bf16[1024,1,1024]{2,0,1:T(8,128)(2,1)} fusion(bf16[4096,1024]{1,0:T(8,128)(2,1)} %all-gather.11.cloned.1.call-done, bf16[4096,512]{0,1:T(8,128)(2,1)} %get-tuple-element.50, bf16[4096,512]{0,1:T(8,128)(2,1)} %copy-done.25), kind=kOutput, calls=%fused_computation.36 | convolution fusion | flops 8607760384 | bytes 18874368 | tf_op jit(solution)/shard_map/dot_general | solution.py:181
  665.7 3.9 reduce
  669.6 2.8 reshape.234
  672.4 2.2 all-to-all-done.4
  674.6 7.3 all-to-all-start.3
  681.9 2.6 fusion.77
  684.5 4.4 reshape.237
  688.9 1.4 copy.129
  690.3 49.4 %all-to-all-done.3 = bf16[16,2,32768]{2,1,0:T(2,128)(2,1)} async-done(((bf16[16,2,32768]{2,1,0:T(2,128)(2,1)}), bf16[16,2,32768]{2,1,0:T(2,128)(2,1)}, u32[]{:S(2)}, u32[]{:S(2)}) %all-to-all-start.3) | async-done | bytes 2097184 | tf_op jit(solution)/shard_map/all_to_all | solution.py:73
  739.7 10.4 %reshape.235 = bf16[1024,1,1024]{2,1,0:T(2,128)(2,1)} reshape(bf16[16,2,32768]{2,1,0:T(2,128)(2,1)} %all-to-all-done.3) | data formatting | bytes 4194304
  750.2 4.3 copy.128
  754.5 4.2 reduce-scatter.12.cloned.1.call-done
  759.6 57.6 %reduce-scatter.16.cloned.1.call-done = f32[64,16]{1,0:T(8,128)} async-done(((f32[1024,16]{1,0:T(8,128)}), f32[64,16]{1,0:T(8,128)}) %reduce-scatter.16.cloned.1.call-update) | async-done | bytes 4112
  818.0 1.4 pad_maximum_fusion.14
  819.4 3.8 fusion.43
  823.2 30.0 %all-reduce.4 = (bf16[1024]{0:T(1024)(128)(2,1)S(1)}, bf16[1024]{0:T(1024)(128)(2,1)S(1)}) all-reduce(f32[1024]{0:T(1024)S(1)} %get-tuple-element.32, f32[1024]{0:T(1024)S(1)} %get-tuple-element.30), channel_id=5, replica_groups=mesh['seq'=2,'dp'=16] {'dp'}, use_global_device_ids=true, to_apply=%region_17.18.clone | all-reduce | flops 2048 | bytes 12288
  853.3 5.7 all-reduce.6
  862.3 51.4 %all-reduce.10.cloned.1.call-done = (bf16[64,16,1024]{2,0,1:T(8,128)(2,1)}, bf16[32,16,1024]{2,0,1:T(8,128)(2,1)}, bf16[64,2048]{1,0:T(8,128)(2,1)}, bf16[64,1024]{1,0:T(8,128)(2,1)}) async-done(((bf16[64,16,1024]{2,0,1:T(8,128)(2,1)}, bf16[32,16,1024]{2,0,1:T(8,128)(2,1)}, bf16[64,2048]{1,0:T(8,128)(2,1)}, bf16[64,1024]{1,0:T(8,128)(2,1)}), (bf16[64,16,1024]{2,0,1:T(8,128)(2,1)}, ...) | async-done | bytes 3538960 | tf_op jit(solution)/shard_map/psum | solution.py:240
  913.7 1.6 convert_element_type.205
  915.4 1.8 convert_element_type.203
  917.1 4.8 copy.114
  922.0 3.2 copy.115
  (145 shorter events, 22.7 us)
Async XLA Ops:
  7.2 56.4 %all-gather.7.cloned.1.call-start = ((), (), s32[]{:S(2)}) async-start(), calls=%async_computation.10 | async-start | bytes 4456448 | tf_op jit(solution)/shard_map/all_gather | solution.py:104
  7.9 97.9 %all-gather.9.cloned.1.call-start = ((), (), s32[]{:S(2)}) async-start(), calls=%async_computation.11 | async-start | bytes 2228224 | tf_op jit(solution)/shard_map/all_gather | solution.py:104
  8.0 45.1 %collective-permute-start.1 = (s32[1,256]{1,0:T(1,128)}, s32[1,256]{1,0:T(1,128)S(1)}, u32[]{:S(2)}, u32[]{:S(2)}) collective-permute-start(s32[1,256]{1,0:T(1,128)} %param.12), channel_id=1, source_target_pairs={{0,16},{1,17},{2,18},{3,19},{4,20},{5,21},{6,22},{7,23},{8,24},{9,... | collective-permute-start | bytes 3080 | tf_op jit(solution)/shard_map/ppermute | solution.py:103
  12.9 42.2 %collective-permute-start = (bf16[256,1024]{1,0:T(8,128)(2,1)}, bf16[256,1024]{1,0:T(8,128)(2,1)S(1)}, u32[]{:S(2)}, u32[]{:S(2)}) collective-permute-start(bf16[256,1024]{1,0:T(8,128)(2,1)} %bitcast.190), channel_id=1, source_target_pairs={{0,16},{1,17},{2,18},{3,19},{4,20},{5,21},{6,22},{7,23},{8,24},{9,... | collective-permute-start | bytes 1572872 | tf_op jit(solution)/shard_map/ppermute | solution.py:102
  14.2 207.2 %all-gather.11.cloned.1.call-start = ((), (), s32[]{:S(2)}) async-start(), calls=%async_computation.12 | async-start | bytes 8912896 | tf_op jit(solution)/shard_map/all_gather | solution.py:65
  53.0 10.6 %copy-start.19 = (f32[1024]{0:T(1024)}, f32[1024]{0:T(1024)S(1)}, u32[]{:S(2)}) copy-start(f32[1024]{0:T(1024)S(1)} %convert_element_type.168) | copy-start | bytes 12292
  54.2 16.0 %copy-start.13 = (f32[256,64]{0,1:T(8,128)}, f32[256,64]{0,1:T(8,128)S(1)}, u32[]{:S(2)}) copy-start(f32[256,64]{0,1:T(8,128)S(1)} %fusion.71) | copy-start | bytes 196612
  55.1 15.2 %copy-start.8 = (f32[256,64]{0,1:T(8,128)}, f32[256,64]{0,1:T(8,128)S(1)}, u32[]{:S(2)}) copy-start(f32[256,64]{0,1:T(8,128)S(1)} %fusion.70) | copy-start | bytes 196612
  55.7 10.8 %copy-start.11 = (bf16[512,1024]{1,0:T(8,128)(2,1)}, bf16[512,1024]{1,0:T(8,128)(2,1)S(1)}, u32[]{:S(2)}) copy-start(bf16[512,1024]{1,0:T(8,128)(2,1)S(1)} %multiply_convert_fusion.4) | copy-start | bytes 3145732
  67.2 9.8 %copy-start.15 = (bf16[512,512]{0,1:T(8,128)(2,1)}, bf16[512,512]{0,1:T(8,128)(2,1)S(1)}, u32[]{:S(2)}) copy-start(bf16[512,512]{0,1:T(8,128)(2,1)S(1)} %copy.97) | copy-start | bytes 1572868
  70.5 6.5 copy-start.6
  70.8 11.0 %copy-start.3 = (bf16[512,8,64,1]{0,2,3,1:T(8,128)(2,1)}, bf16[512,8,64,1]{0,2,3,1:T(8,128)(2,1)S(1)}, u32[]{:S(2)}) copy-start(bf16[512,8,64,1]{0,2,3,1:T(8,128)(2,1)S(1)} %fusion.59) | copy-start | bytes 1572868
  76.9 0.6 copy-start.21
  77.5 28.3 %copy-start = (bf16[1,256,1024]{2,1,0:T(8,128)(2,1)S(1)}, bf16[1,256,1024]{2,1,0:T(8,128)(2,1)}, u32[]{:S(2)}) copy-start(bf16[1,256,1024]{2,1,0:T(8,128)(2,1)} %param.11) | copy-start | bytes 1572868
  81.9 103.9 %copy-start.5 = (bf16[8,64,2,256]{3,1,2,0:T(8,128)(2,1)}, bf16[8,64,2,256]{3,1,2,0:T(8,128)(2,1)S(1)}, u32[]{:S(2)}) copy-start(bf16[8,64,2,256]{3,1,2,0:T(8,128)(2,1)S(1)} %fusion.31) | copy-start | bytes 1572868
  81.9 36.5 %copy-start.24 = (bf16[64,16]{0,1:T(8,128)(2,1)S(1)}, bf16[64,16]{0,1:T(8,128)(2,1)}, u32[]{:S(2)}) copy-start(bf16[64,16]{0,1:T(8,128)(2,1)} %param.18) | copy-start | bytes 6148
  81.9 102.3 %copy-start.10 = (bf16[32,16,1024]{2,1,0:T(8,128)(2,1)S(1)}, bf16[32,16,1024]{2,1,0:T(8,128)(2,1)}, u32[]{:S(2)}) copy-start(bf16[32,16,1024]{2,1,0:T(8,128)(2,1)} %param.20) | copy-start | bytes 3145732
  105.8 79.9 %copy-start.23 = (s32[1,256,8]{1,2,0:T(8,128)S(1)}, s32[1,256,8]{1,2,0:T(8,128)}, u32[]{:S(2)}) copy-start(s32[1,256,8]{1,2,0:T(8,128)} %param.13) | copy-start | bytes 24580
  109.2 76.5 %copy-start.2 = (bf16[256,1024]{1,0:T(8,128)(2,1)S(1)}, bf16[256,1024]{1,0:T(8,128)(2,1)}, u32[]{:S(2)}) copy-start(bf16[256,1024]{1,0:T(8,128)(2,1)} %multiply_convert_fusion.5) | copy-start | bytes 1572868
  109.3 199.6 %all-gather.13.cloned.1.call-start = ((), (), s32[]{:S(2)}) async-start(), calls=%async_computation.17 | async-start | bytes 8912896 | tf_op jit(solution)/shard_map/all_gather | solution.py:65
  113.9 72.1 %all-to-all-start = ((bf16[64,16,1024]{2,0,1:T(8,128)(2,1)}), bf16[64,16,1024]{2,0,1:T(8,128)(2,1)}, u32[]{:S(2)}, u32[]{:S(2)}) async-start(bf16[64,16,1024]{2,0,1:T(8,128)(2,1)} %copy.103), calls=%async_computation | async-start | bytes 4194304 | tf_op jit(solution)/shard_map/all_to_all | solution.py:73
  186.1 70.0 %all-to-all-start.1 = ((bf16[32,16,1024]{2,0,1:T(8,128)(2,1)}), bf16[32,16,1024]{2,0,1:T(8,128)(2,1)S(1)}, u32[]{:S(2)}, u32[]{:S(2)}) async-start(bf16[32,16,1024]{2,0,1:T(8,128)(2,1)} %copy.104), calls=%async_computation.1 | async-start | bytes 2097152 | tf_op jit(solution)/shard_map/all_to_all | solution.py:73
  321.2 10.0 %all-to-all-start.2 = ((f32[16,256,1]{1,2,0:T(1,128)}), f32[16,256,1]{1,2,0:T(1,128)S(1)}, u32[]{:S(2)}, u32[]{:S(2)}) async-start(f32[16,256,1]{1,2,0:T(1,128)} %bitcast.34), calls=%async_computation.4 | async-start | bytes 32768 | tf_op jit(solution)/shard_map/all_to_all | solution.py:73
  324.7 156.0 %reduce-scatter.10.cloned.1.call-start = ((), (), s32[]{:S(2)}) async-start(), calls=%async_computation.14 | async-start | bytes 8912896 | tf_op jit(solution)/shard_map/reduce_scatter | solution.py:68
  362.8 2.0 copy-start.25
  378.8 208.8 %reduce-scatter.8.cloned.1.call-start = ((), (), s32[]{:S(2)}) async-start(), calls=%async_computation.13 | async-start | bytes 8912896 | tf_op jit(solution)/shard_map/reduce_scatter | solution.py:68
  388.7 365.8 %reduce-scatter.14.cloned.1.call-start = ((), (), s32[]{:S(2)}) async-start(), calls=%async_computation.16 | async-start | bytes 2228224 | tf_op jit(solution)/shard_map/reduce_scatter | solution.py:229
  480.6 116.0 %copy-start.22 = (f32[8,2,256]{2,1,0:T(2,128)S(1)}, f32[8,2,256]{2,1,0:T(2,128)}, u32[]{:S(2)}) copy-start(f32[8,2,256]{2,1,0:T(2,128)} %copy-done.21) | copy-start | bytes 49156
  596.4 162.4 %reduce-scatter.12.cloned.1.call-start = ((), (), s32[]{:S(2)}) async-start(), calls=%async_computation.15 | async-start | bytes 4456448 | tf_op jit(solution)/shard_map/reduce_scatter | solution.py:229
  606.3 5.1 copy-start.7
  611.3 2.9 copy-start.4
  611.3 3.7 copy-start.9
  612.8 2.5 copy-start.14
  612.8 15.3 %collective-permute-start.2 = (bf16[256,1024]{0,1:T(8,128)(2,1)S(1)}, bf16[256,1024]{0,1:T(8,128)(2,1)S(1)}, u32[]{:S(2)}, u32[]{:S(2)}) collective-permute-start(bf16[256,1024]{0,1:T(8,128)(2,1)S(1)} %fusion.49), channel_id=1, source_target_pairs={{16,0},{17,1},{18,2},{19,3},{20,4},{21,5},{22,6},{23,7},{24,8},{25... | collective-permute-start | bytes 1572872 | tf_op jit(solution)/shard_map/ppermute | solution.py:214
  615.0 14.3 %copy-start.12 = (bf16[512,1024]{1,0:T(8,128)(2,1)S(1)}, bf16[512,1024]{1,0:T(8,128)(2,1)}, u32[]{:S(2)}) copy-start(bf16[512,1024]{1,0:T(8,128)(2,1)} %copy-done.11) | copy-start | bytes 3145732
  615.6 13.0 %copy-start.16 = (bf16[256,1024]{0,1:T(8,128)(2,1)}, bf16[256,1024]{0,1:T(8,128)(2,1)S(1)}, u32[]{:S(2)}) copy-start(bf16[256,1024]{0,1:T(8,128)(2,1)S(1)} %fusion.55) | copy-start | bytes 1572868
  628.6 0.7 copy-start.18
  645.7 28.9 %all-to-all-start.4 = ((bf16[16,2,16384]{2,1,0:T(2,128)(2,1)}), bf16[16,2,16384]{2,1,0:T(2,128)(2,1)}, u32[]{:S(2)}, u32[]{:S(2)}) async-start(bf16[16,2,16384]{2,1,0:T(2,128)(2,1)} %reshape.236), calls=%async_computation.8 | async-start | bytes 2097152 | tf_op jit(solution)/shard_map/all_to_all | solution.py:73
  674.6 65.2 %all-to-all-start.3 = ((bf16[16,2,32768]{2,1,0:T(2,128)(2,1)}), bf16[16,2,32768]{2,1,0:T(2,128)(2,1)}, u32[]{:S(2)}, u32[]{:S(2)}) async-start(bf16[16,2,32768]{2,1,0:T(2,128)(2,1)} %reshape.234), calls=%async_computation.7 | async-start | bytes 4194304 | tf_op jit(solution)/shard_map/all_to_all | solution.py:73
  681.9 135.3 %reduce-scatter.16.cloned.1.call-start = ((), (), s32[]{:S(2)}) async-start(), calls=%async_computation.18 | async-start | bytes 557056
  684.5 229.2 %all-reduce.10.cloned.1.call-start = ((), (), s32[]{:S(2)}) async-start(), calls=%async_computation.19 | async-start | bytes 7077888 | tf_op jit(solution)/shard_map/psum | solution.py:240
  690.3 69.2 %copy-start.1 = (bf16[1,256,1024]{2,1,0:T(8,128)(2,1)S(1)}, bf16[1,256,1024]{2,1,0:T(8,128)(2,1)}, u32[]{:S(2)}) copy-start(bf16[1,256,1024]{2,1,0:T(8,128)(2,1)} %param.11) | copy-start | bytes 1572868
  690.3 129.1 %copy-start.17 = (bf16[256,1024]{0,1:T(8,128)(2,1)S(1)}, bf16[256,1024]{0,1:T(8,128)(2,1)}, u32[]{:S(2)}) copy-start(bf16[256,1024]{0,1:T(8,128)(2,1)} %copy-done.16) | copy-start | bytes 1572868
  690.3 129.1 %copy-start.20 = (f32[1024]{0:T(1024)S(1)}, f32[1024]{0:T(1024)}, u32[]{:S(2)}) copy-start(f32[1024]{0:T(1024)} %copy-done.19) | copy-start | bytes 12292
Sparse Core Ops, SparseCore 0:
  10.1 53.3 all-gather.6
  65.7 40.0 all-gather.8
  109.4 108.5 all-gather.10
  220.0 88.7 all-gather.12
  378.9 101.6 reduce-scatter.9
  484.6 103.0 reduce-scatter.7
  596.5 67.0 reduce-scatter.13
  667.5 91.2 reduce-scatter.11
  762.3 54.8 reduce-scatter.15
  820.0 93.6 all-reduce.9

commit v2 on v1

--- a/solution.py
+++ b/solution.py
@@ -1,6 +1,10 @@
+import functools
+
 import jax
 import jax.numpy as jnp
 from jax import lax
+from jax.experimental import pallas as pl
+from jax.experimental.pallas import tpu as pltpu
 from jax.sharding import PartitionSpec as P
 
 MODEL_WIDTH = 1024
@@ -10,6 +14,8 @@
 F = 512
 EXPERTS = 16
 TOPK = 8
+RANKS = 8
+GROUP = 16
 
 epsilon = 1e-06
 rope_base = 10000.0
@@ -17,6 +23,370 @@
 masked_score = -1e30
 f32 = jnp.float32
 bf16 = jnp.bfloat16
+MESH = pl.DeviceIdType.MESH
+
+LINKS = ((8, 4, 2), (4, 2, 8), (2, 8, 4))
+
+
+def flip(value, bit):
+    return value + bit * (1 - 2 * ((value // bit) % 2))
+
+
+def flip_mask(value, mask):
+    for bit in (1, 2, 4, 8):
+        if mask & bit:
+            value = flip(value, bit)
+    return value
+
+
+def subsets(bits):
+    out = [0]
+    for bit in bits:
+        out = out + [m | bit for m in out]
+    return out
+
+
+def row_parts(rows):
+    first = (rows // 3 + 15) // 16 * 16
+    second = (rows - first) // 2 // 16 * 16
+    return ((0, first), (first, second), (first + second, rows - first - second))
+
+
+def my_place():
+    seq = lax.axis_index("seq")
+    dp = lax.axis_index("dp")
+    rank = seq * RANKS + dp % RANKS
+
+    def peer(bit):
+        if bit == 8:
+            return {"seq": 1 - seq, "dp": dp}
+        return {"seq": seq, "dp": flip(dp, bit)}
+
+    return rank, peer
+
+
+def meet(peer):
+    barrier = pltpu.get_barrier_semaphore()
+    for bit in (1, 2, 4, 8):
+        pl.semaphore_signal(barrier, inc=1, device_id=peer(bit), device_id_type=MESH)
+    pl.semaphore_wait(barrier, 4)
+
+
+def gather_kernel(count, *refs):
+    ins, outs = refs[:count], refs[count : 2 * count]
+    send, recv, send_core, recv_core, local = refs[2 * count :]
+    rank, peer = my_place()
+    own = [
+        pltpu.make_async_copy(ins[a], outs[a].at[rank], local.at[a]) for a in range(count)
+    ]
+    for copy in own:
+        copy.start()
+    meet(peer)
+    parts = [row_parts(ref.shape[0]) for ref in ins]
+
+    def remote(a, p, mask, bit, sems, index):
+        start, size = parts[a][p]
+        rows = pl.ds(start, size)
+        shard = flip_mask(rank, mask)
+        src = ins[a].at[rows] if mask == 0 else outs[a].at[shard, rows]
+        return pltpu.make_async_remote_copy(
+            src_ref=src,
+            dst_ref=outs[a].at[shard, rows],
+            send_sem=sems[0].at[a, p, index],
+            recv_sem=sems[1].at[a, p, index],
+            device_id=peer(bit),
+            device_id_type=MESH,
+        )
+
+    started = []
+    live = {}
+    for step in range(4):
+        for p in range(3):
+            for a in range(count):
+                if parts[a][p][1] == 0:
+                    continue
+                order = LINKS[p]
+                if step > 0:
+                    for copy in live.pop((a, p)):
+                        copy.wait_recv()
+                if step < 3:
+                    now = []
+                    for index, mask in enumerate(subsets(order[:step])):
+                        copy = remote(a, p, mask, order[step], (send, recv), 2**step - 1 + index)
+                        copy.start()
+                        now.append(copy)
+                        started.append(copy)
+                    live[(a, p)] = now
+                fresh = [0] if step == 0 else [m | order[step - 1] for m in subsets(order[: step - 1])]
+                base = 0 if step == 0 else 2 ** (step - 1)
+                for index, mask in enumerate(fresh):
+                    copy = remote(a, p, mask, 1, (send_core, recv_core), base + index)
+                    copy.start()
+                    live.setdefault("core", []).append(copy)
+    for copy in live["core"]:
+        copy.wait()
+    for copy in started:
+        copy.wait_send()
+    for copy in own:
+        copy.wait()
+
+
+def group_gather(collective_id, *arrays):
+    count = len(arrays)
+    return pl.pallas_call(
+        functools.partial(gather_kernel, count),
+        out_shape=[jax.ShapeDtypeStruct((GROUP,) + a.shape, a.dtype) for a in arrays],
+        in_specs=[pl.BlockSpec(memory_space=pltpu.VMEM)] * count,
+        out_specs=[pl.BlockSpec(memory_space=pl.ANY)] * count,
+        scratch_shapes=[
+            pltpu.SemaphoreType.DMA((count, 3, 7)),
+            pltpu.SemaphoreType.DMA((count, 3, 7)),
+            pltpu.SemaphoreType.DMA((count, 3, 8)),
+            pltpu.SemaphoreType.DMA((count, 3, 8)),
+            pltpu.SemaphoreType.DMA((count,)),
+        ],
+        compiler_params=pltpu.CompilerParams(collective_id=collective_id, has_side_effects=True),
+        name="group_gather",
+    )(*arrays)
+
+
+def add_rows(target, source, start, size):
+    def step(i, carry):
+        rows = pl.ds(pl.multiple_of(start + i * 16, 16), 16)
+        target[rows] = (target[rows].astype(f32) + source[rows].astype(f32)).astype(target.dtype)
+        return carry
+
+    lax.fori_loop(0, size // 16, step, 0)
+
+
+def reduce_kernel(
+    mixed_ref, normed_ref, gate_ref, mixed_out, normed_out, gate_out,
+    total, got0, got1, got2, got3, sems, gate_sems, local, own_gate,
+):
+    rank, peer = my_place()
+    chip = rank // 2
+    core = rank % 2
+    parts = row_parts(mixed_ref.shape[1])
+    ins = (mixed_ref, normed_ref)
+    outs = (mixed_out, normed_out)
+    loads = []
+    for t in range(2):
+        for c in range(8):
+            copy = pltpu.make_async_copy(ins[t].at[2 * c + core], total.at[t, c], local.at[t, c])
+            copy.start()
+            loads.append(copy)
+    barrier = pltpu.get_barrier_semaphore()
+    seq = lax.axis_index("seq")
+    dp = lax.axis_index("dp")
+    everyone = [
+        {"seq": 1 - seq if mask & 8 else seq, "dp": flip_mask(dp, mask & 7)} for mask in range(1, 16)
+    ]
+    for there in everyone:
+        pl.semaphore_signal(barrier, inc=1, device_id=there, device_id_type=MESH)
+    pl.semaphore_wait(barrier, 15)
+    gates = []
+    keep = pltpu.make_async_copy(gate_ref.at[rank], gate_out.at[rank], own_gate)
+    keep.start()
+    for mask, there in zip(range(1, 16), everyone):
+        copy = pltpu.make_async_remote_copy(
+            src_ref=gate_ref.at[flip_mask(rank, mask)],
+            dst_ref=gate_out.at[rank],
+            send_sem=gate_sems.at[0, mask],
+            recv_sem=gate_sems.at[1, mask],
+            device_id=there,
+            device_id_type=MESH,
+        )
+        copy.start()
+        gates.append(copy)
+
+    started = []
+    live = {}
+
+    def send(t, p, stage, index, src, dst, bit):
+        copy = pltpu.make_async_remote_copy(
+            src_ref=src,
+            dst_ref=dst,
+            send_sem=sems.at[0, t, p, stage, index],
+            recv_sem=sems.at[1, t, p, stage, index],
+            device_id=peer(bit),
+            device_id_type=MESH,
+        )
+        copy.start()
+        started.append(copy)
+        live.setdefault((t, p), []).append(copy)
+
+    def chip_of(mask):
+        return flip_mask(rank, mask) // 2
+
+    for p in range(3):
+        for t in range(2):
+            rows = pl.ds(*parts[p])
+            for c in range(8):
+                send(
+                    t, p, 0, c, ins[t].at[2 * c + 1 - core, rows], got0.at[t, c, rows], 1
+                )
+    for copy in loads:
+        copy.wait()
+    got = (got1, got2, got3)
+    for stage in range(4):
+        for p in range(3):
+            for t in range(2):
+                order = LINKS[p]
+                rows = pl.ds(*parts[p])
+                for copy in live.pop((t, p)):
+                    copy.wait_recv()
+                if stage == 0:
+
+                    def over_chips(c, carry, t=t, p=p):
+                        add_rows(total.at[t, c], got0.at[t, c], *parts[p])
+                        return carry
+
+                    lax.fori_loop(0, 8, over_chips, 0)
+                else:
+                    for index, mask in enumerate(subsets(order[stage:])):
+                        if stage == 3:
+                            outs[t][rows] = total[t, chip, rows].astype(f32) + got3[t, 0, rows].astype(f32)
+                        else:
+                            add_rows(
+                                total.at[t, chip_of(mask)], got[stage - 1].at[t, index], *parts[p]
+                            )
+                if stage < 3:
+                    for index, mask in enumerate(subsets(order[stage + 1 :])):
+                        send(
+                            t, p, stage + 1, index,
+                            total.at[t, chip_of(mask | order[stage]), rows],
+                            got[stage].at[t, index, rows],
+                            order[stage],
+                        )
+    for copy in started:
+        copy.wait_send()
+    for copy in gates:
+        copy.wait()
+    keep.wait()
+
+
+def group_reduce(collective_id, mixed, normed, gate_grad):
+    rows, width = mixed.shape[1:]
+    return pl.pallas_call(
+        reduce_kernel,
+        out_shape=[
+            jax.ShapeDtypeStruct((rows, width), f32),
+            jax.ShapeDtypeStruct((rows, width), f32),
+            jax.ShapeDtypeStruct(gate_grad.shape, gate_grad.dtype),
+        ],
+        in_specs=[pl.BlockSpec(memory_space=pl.ANY)] * 3,
+        out_specs=[
+            pl.BlockSpec(memory_space=pltpu.VMEM),
+            pl.BlockSpec(memory_space=pltpu.VMEM),
+            pl.BlockSpec(memory_space=pl.ANY),
+        ],
+        scratch_shapes=[
+            pltpu.VMEM((2, 8, rows, width), bf16),
+            pltpu.VMEM((2, 8, rows, width), bf16),
+            pltpu.VMEM((2, 4, rows, width), bf16),
+            pltpu.VMEM((2, 2, rows, width), bf16),
+            pltpu.VMEM((2, 1, rows, width), bf16),
+            pltpu.SemaphoreType.DMA((2, 2, 3, 4, 8)),
+            pltpu.SemaphoreType.DMA((2, 16)),
+            pltpu.SemaphoreType.DMA((2, 8)),
+            pltpu.SemaphoreType.DMA(()),
+        ],
+        compiler_params=pltpu.CompilerParams(
+            collective_id=collective_id, has_side_effects=True, vmem_limit_bytes=48 * 2**20
+        ),
+        name="group_reduce",
+    )(mixed, normed, gate_grad)
+
+
+def expert_kernel(
+    rows_ref, grad_ref, gate_ref, gate_up_ref, down_ref,
+    mixed_ref, normed_ref, gate_grad_ref, gate_up_out, down_out,
+    gate_up_sum, down_sum,
+):
+    step = pl.program_id(0)
+    shards, each, width = rows_ref.shape
+    count = shards * each
+    rows = rows_ref[...].reshape(count, width)
+    grad = grad_ref[...].reshape(count, width).astype(f32)
+    gate = jnp.concatenate(
+        [jnp.broadcast_to(gate_ref[i], (128, each)).T[:, :1] for i in range(shards)], 0
+    )
+    down = down_ref[...]
+    gate_up_weight = gate_up_ref[...]
+    gate_up = jnp.dot(rows, gate_up_weight, preferred_element_type=f32)
+    gate_part, up_part = gate_up[:, :F], gate_up[:, F:]
+    sigmoid = 1.0 / (1.0 + jnp.exp(-gate_part))
+    silu = gate_part * sigmoid
+    act = (silu * up_part).astype(bf16)
+    out = jnp.dot(act, down, preferred_element_type=f32)
+    inner = jnp.sum(out * grad, axis=-1, keepdims=True)
+    for i in range(shards):
+        line = jnp.broadcast_to(inner[i * each : (i + 1) * each], (each, 128)).T
+        gate_grad_ref[i] = line[:8]
+    mixed_ref[...] = (gate * out).astype(bf16).reshape(shards, each, width)
+    expert_grad = (gate * grad).astype(bf16)
+    across = (((1,), (1,)), ((), ()))
+    over_rows = (((0,), (0,)), ((), ()))
+    act_grad = lax.dot_general(expert_grad, down, across, preferred_element_type=f32)
+    gate_up_grad = jnp.concatenate(
+        [act_grad * up_part * (sigmoid * (1.0 + gate_part * (1.0 - sigmoid))), act_grad * silu], -1
+    ).astype(bf16)
+    normed_ref[...] = (
+        lax.dot_general(gate_up_grad, gate_up_weight, across, preferred_element_type=f32)
+        .astype(bf16)
+        .reshape(shards, each, width)
+    )
+
+    @pl.when(step == 0)
+    def _():
+        gate_up_sum[...] = jnp.zeros_like(gate_up_sum)
+        down_sum[...] = jnp.zeros_like(down_sum)
+
+    down_sum[...] += lax.dot_general(act, expert_grad, over_rows, preferred_element_type=f32)
+    gate_up_sum[...] += lax.dot_general(rows, gate_up_grad, over_rows, preferred_element_type=f32)
+
+    @pl.when(step == pl.num_programs(0) - 1)
+    def _():
+        gate_up_out[...] = gate_up_sum[...].astype(bf16)
+        down_out[...] = down_sum[...].astype(bf16)
+
+
+def expert_layer(rows, grad, gate, gate_up_weight, down_weight):
+    each, width = rows.shape[1:]
+    shards = 2
+    tile = pl.BlockSpec((shards, each, width), lambda i: (i, 0, 0))
+    whole = lambda shape: pl.BlockSpec(shape, lambda i: (0, 0))
+    return pl.pallas_call(
+        expert_kernel,
+        grid=(GROUP // shards,),
+        out_shape=[
+            jax.ShapeDtypeStruct(rows.shape, bf16),
+            jax.ShapeDtypeStruct(rows.shape, bf16),
+            jax.ShapeDtypeStruct((GROUP, 8, each), f32),
+            jax.ShapeDtypeStruct(gate_up_weight.shape, bf16),
+            jax.ShapeDtypeStruct(down_weight.shape, bf16),
+        ],
+        in_specs=[
+            tile,
+            tile,
+            pl.BlockSpec((shards, 1, each), lambda i: (i, 0, 0)),
+            whole(gate_up_weight.shape),
+            whole(down_weight.shape),
+        ],
+        out_specs=[
+            tile,
+            tile,
+            pl.BlockSpec((shards, 8, each), lambda i: (i, 0, 0)),
+            whole(gate_up_weight.shape),
+            whole(down_weight.shape),
+        ],
+        scratch_shapes=[
+            pltpu.VMEM(gate_up_weight.shape, f32),
+            pltpu.VMEM(down_weight.shape, f32),
+        ],
+        compiler_params=pltpu.CompilerParams(vmem_limit_bytes=56 * 2**20),
+        name="expert_layer",
+    )(rows, grad, gate, gate_up_weight, down_weight)
 
 
 def inverse_rms(rows):
@@ -53,39 +423,30 @@
 
 
 def make_body(n_dp):
-    groups_count = n_dp // EXPERTS
-    token_groups = (
-        None
-        if groups_count == 1
-        else [[g * EXPERTS + j for j in range(EXPERTS)] for g in range(groups_count)]
-    )
-    expert_groups = [[g * EXPERTS + j for g in range(groups_count)] for j in range(EXPERTS)]
-
-    def token_gather(rows):
-        return lax.all_gather(rows, "dp", axis=0, tiled=True, axis_index_groups=token_groups)
-
-    def token_scatter(rows):
-        return lax.psum_scatter(
-            rows, "dp", scatter_dimension=0, tiled=True, axis_index_groups=token_groups
-        )
-
-    def exchange(rows, split, concat):
-        return lax.all_to_all(
-            rows, "dp", split_axis=split, concat_axis=concat, tiled=True, axis_index_groups=token_groups
-        )
-
-    def expert_weight(shard):
-        whole = exchange(shard, 1, 0)
-        if groups_count > 1:
-            whole = lax.all_gather(whole, "dp", axis=0, tiled=True, axis_index_groups=expert_groups)
-        return whole[:, 0]
+    groups_count = n_dp // RANKS
+    inside = [[g * RANKS + j for j in range(RANKS)] for g in range(groups_count)]
+    between = [[g * RANKS + j for g in range(groups_count)] for j in range(RANKS)]
+    half_experts = EXPERTS // 2
+
+    def expert_weight(shard, seq_rank):
+        mine = lax.dynamic_slice_in_dim(shard, seq_rank * half_experts, half_experts, axis=1)
+        mine = jnp.swapaxes(mine, 0, 1)
+        mine = lax.all_to_all(
+            mine, "dp", split_axis=0, concat_axis=0, tiled=True, axis_index_groups=inside
+        )
+        mine = mine.reshape(-1, shard.shape[2])
+        return lax.all_gather(mine, "dp", axis=0, tiled=True, axis_index_groups=between)
 
     def expert_weight_grad(grad):
-        if groups_count > 1:
-            grad = lax.psum_scatter(
-                grad, "dp", scatter_dimension=0, tiled=True, axis_index_groups=expert_groups
-            )
-        return exchange(grad.astype(bf16)[:, None, :], 0, 1)
+        grad = lax.psum_scatter(
+            grad, "dp", scatter_dimension=0, tiled=True, axis_index_groups=between
+        )
+        grad = grad.reshape(RANKS, -1, grad.shape[1])
+        grad = lax.all_to_all(
+            grad, "dp", split_axis=0, concat_axis=0, tiled=True, axis_index_groups=inside
+        )
+        grad = lax.all_gather(grad, "seq", axis=0, tiled=True)
+        return jnp.swapaxes(grad, 0, 1).astype(f32)
 
     def body(
         tokens, starts, routes, gain_one, query_key_value_weight, w_out,
@@ -93,7 +454,7 @@
     ):
         count = tokens.shape[1]
         seq_rank = lax.axis_index("seq")
-        expert_rank = lax.axis_index("dp") % EXPERTS
+        expert = seq_rank * RANKS + lax.axis_index("dp") % RANKS
         query_columns = QUERY_HEADS * HEAD_SIZE
         key_columns = KEY_VALUE_HEADS * HEAD_SIZE
         group = QUERY_HEADS // KEY_VALUE_HEADS
@@ -104,12 +465,13 @@
         gather = lambda value: lax.all_gather(value, "dp", axis=0, tiled=True)
         qkv_weight = gather(query_key_value_weight)
         out_weight = gather(w_out)
-        router_weight = gather(w_router)
-        gain_a = gather(gain_one).astype(f32)
-        gain_b = gather(gain_two).astype(f32)
-        gate_up_weight = expert_weight(w_gate_up)
-        down_weight = expert_weight(w_down)
-        grad_all = token_gather(cotangent[0])
+        small = gather(jnp.concatenate([w_router, gain_one[:, None], gain_two[:, None]], 1))
+        router_weight = small[:, :EXPERTS]
+        gain_a = small[:, EXPERTS].astype(f32)
+        gain_b = small[:, EXPERTS + 1].astype(f32)
+        gate_up_weight = expert_weight(w_gate_up, seq_rank)
+        down_weight = expert_weight(w_down, seq_rank)
+        (grad_all,) = group_gather(0, cotangent[0])
 
         token_rows = tokens[0].astype(f32)
         grad_output = cotangent[0].astype(f32)
@@ -154,35 +516,15 @@
         chosen = jnp.any(routes[0][:, :, None] == expert_ids[None, None, :], axis=1)
         gates = jax.nn.softmax(jnp.where(chosen, logits, -jnp.inf), axis=-1)
 
-        rows_in = token_gather(normed_two)
-        gates_all = token_gather(gates)
-        gate = lax.dynamic_slice_in_dim(gates_all, expert_rank, 1, axis=1)
-        gate_up = jnp.dot(rows_in, gate_up_weight, preferred_element_type=f32)
-        gate_part, up_part = gate_up[:, :F], gate_up[:, F:]
-        sigmoid = jax.nn.sigmoid(gate_part)
-        silu = gate_part * sigmoid
-        act = (silu * up_part).astype(bf16)
-        expert_out = jnp.dot(act, down_weight, preferred_element_type=f32)
-        grad_all_wide = grad_all.astype(f32)
-        gate_grad_part = jnp.sum(expert_out * grad_all_wide, axis=-1, keepdims=True)
-        mixed_part = (gate * expert_out).astype(bf16)
-        expert_grad = (gate * grad_all_wide).astype(bf16)
-        act_grad = lax.dot_general(
-            expert_grad, down_weight, (((1,), (1,)), ((), ())), preferred_element_type=f32
-        )
-        gate_up_grad = jnp.concatenate(
-            [act_grad * up_part * (sigmoid * (1.0 + gate_part * (1.0 - sigmoid))), act_grad * silu], -1
-        ).astype(bf16)
-        normed_part = lax.dot_general(
-            gate_up_grad, gate_up_weight, (((1,), (1,)), ((), ())), preferred_element_type=f32
-        ).astype(bf16)
+        rows_in, gates_all = group_gather(1, normed_two, gates.T)
+        gate = lax.dynamic_slice_in_dim(gates_all, expert, 1, axis=1)
+        mixed_part, normed_part, gate_grad_part, gate_up_wgrad, down_wgrad = expert_layer(
+            rows_in, grad_all, gate, gate_up_weight, down_weight
+        )
+        mixed, normed_grad, gate_grad = group_reduce(2, mixed_part, normed_part, gate_grad_part)
+        gate_grad = gate_grad[:, 0].T
+
         over_rows = (((0,), (0,)), ((), ()))
-        down_wgrad = lax.dot_general(act, expert_grad, over_rows, preferred_element_type=f32)
-        gate_up_wgrad = lax.dot_general(rows_in, gate_up_grad, over_rows, preferred_element_type=f32)
-        normed_grad = token_scatter(normed_part).astype(f32)
-        gate_grad = exchange(gate_grad_part, 0, 1)
-        mixed = token_scatter(mixed_part).astype(f32)
-
         output = (hidden + mixed).astype(bf16)[None]
         stat_sums = jnp.stack([jnp.sum(hidden * hidden), jnp.sum(mixed * mixed)])
         weighted = jnp.where(chosen, gates * gate_grad, 0.0)
@@ -227,19 +569,22 @@
         input_grad = (hidden_grad + rows_branch).astype(bf16)[None]
 
         scatter = lambda value: lax.psum_scatter(value, "dp", scatter_dimension=0, tiled=True)
-        shards = (
-            scatter(gain_one_grad),
-            scatter(qkv_wgrad.astype(bf16)),
-            scatter(out_wgrad.astype(bf16)),
-            scatter(gain_two_grad),
-            scatter(router_wgrad),
+        little = jnp.concatenate([router_wgrad, gain_one_grad[:, None], gain_two_grad[:, None]], 1)
+        shards = (scatter(qkv_wgrad.astype(bf16)), scatter(out_wgrad.astype(bf16)), scatter(little), stat_sums)
+        summed = [lax.psum(part.astype(bf16), "seq").astype(f32) for part in shards]
+        stream_rms = jnp.sqrt(summed[3] / (both * MODEL_WIDTH)).reshape(1, 2)
+        return (
+            output,
+            input_grad,
+            summed[2][:, EXPERTS],
+            summed[0],
+            summed[1],
+            summed[2][:, EXPERTS + 1],
+            summed[2][:, :EXPERTS],
             expert_weight_grad(gate_up_wgrad),
             expert_weight_grad(down_wgrad),
-            stat_sums,
-        )
-        summed = [lax.psum(part.astype(bf16), "seq").astype(f32) for part in shards]
-        stream_rms = jnp.sqrt(summed[7] / (both * MODEL_WIDTH)).reshape(1, 2)
-        return (output, input_grad, *summed[:7], stream_rms)
+            stream_rms,
+        )
 
     return body
 

time: 942 us -> 698 us (0.74)
  Pallas kernels: 0 us -> 270 us
  waiting for transfers between devices: 476 us -> 258 us
  blocking collectives: 154 us -> 27.6 us
  matrix products: 128 us -> 44.3 us
  starting transfers between devices: 64 us -> 24.5 us
  local copies, waits for them, and re-layouts: 47.4 us -> 23.8 us
  other arithmetic: 46.5 us -> 28 us
    pallas_call x0 -> x4, Pallas kernels: none -> 270 us  [the longest x2 116 us: group_gather(): pl.pallas_call(functools.partial(gather_kernel, count), out_shape=[jax.Sh...]
    reduce_scatter x2, waiting for transfers between devices: 196 us -> 0.02 us  [expert_weight_grad(): lax.psum_scatter(grad, 'dp', scatter_dimension=0, tiled=True, axis_index_...]
    reduce_scatter x2, waiting for transfers between devices: 4.24 us -> 92 us  [body(): lax.psum_scatter(value, 'dp', scatter_dimension=0, tiled=True)]
    dot_general x6 -> x1, matrix products: 79.8 us -> 0.31 us  [body(): jnp.dot(normed_two.astype(f32).T, logits_grad, precision=highest)]
    unnamed x2 -> x0, blocking collectives: 63.8 us -> none
    all_to_all x5 -> x4, waiting for transfers between devices: 67.7 us -> 10.8 us  [the longest x2 10.8 us: expert_weight_grad(): lax.all_to_all(grad, 'dp', split_axis=0, concat_axis=0, tiled=True, axis_...]
    all_gather x1, blocking collectives: 65.6 us -> 22.6 us  [body(): gather = lambda value: lax.all_gather(value, 'dp', axis=0, tiled=True)]
    all_to_all x5 -> x4, starting transfers between devices: 55.7 us -> 17 us  [the longest x2 9.51 us: expert_weight(): lax.all_to_all(mine, 'dp', split_axis=0, concat_axis=0, tiled=True, axis_...]
  transfers between devices with their start and end apart: 18 -> 19, of which waited for: 13 -> 9; matrix products, arithmetic and copies ran while one was open for 17% -> 12% of each run, Pallas kernels for 0% -> 32%
where the time goes in v2:
time: 698 us; the launch traced here: 691 us
  Pallas kernels  270 us (39%)
  waiting for transfers between devices  258 us (37%)
  matrix products  44.3 us (6%)
  other arithmetic  28 us (4%)
  blocking collectives  27.6 us (4%)
  starting transfers between devices  24.5 us (4%)
  local copies, waits for them, and re-layouts  23.8 us (3%)
  between operations  15.4 us (2%)
    pallas_call x2, Pallas kernels, group_gather(): pl.pallas_call(functools.partial(gather_kernel, count), out_shape=[jax.Sh...  116 us
    pallas_call x1, Pallas kernels, group_reduce(): pl.pallas_call(reduce_kernel, out_shape=[jax.ShapeDtypeStruct((rows, widt...  104 us
    reduce_scatter x2, waiting for transfers between devices, body(): lax.psum_scatter(value, 'dp', scatter_dimension=0, tiled=True)  92 us
    unnamed x13, waiting for transfers between devices  57.2 us
    pallas_call x1, Pallas kernels, expert_layer(): pl.pallas_call(expert_kernel, grid=(GROUP // shards,), out_shape=[jax.Sha...  49.9 us
    all_gather x2, waiting for transfers between devices, expert_weight_grad(): grad = lax.all_gather(grad, 'seq', axis=0, tiled=True)  46 us
    psum x1, waiting for transfers between devices, body(): summed = [lax.psum(part.astype(bf16), 'seq').astype(f32) for part in shards]  24.2 us
    all_gather x1, blocking collectives, body(): gather = lambda value: lax.all_gather(value, 'dp', axis=0, tiled=True)  22.6 us
  transfers between devices with their start and end apart: 19, of which 9 were waited for; matrix products, arithmetic and copies ran while one was open for 12% of the time, Pallas kernels for 32%

profile of v2, /device:TPU:0, one launch (start us, length us, event | category | flops | bytes accessed | tf_op | source)
XLA Modules:
  0.0 691.2 jit_solution(12345127017526528838)
XLA Ops:
  8.7 1.1 constant_dynamic-slice_fusion
  9.8 1.1 copy.125
  10.9 5.3 all-to-all-start.1
  16.1 4.2 collective-permute-start
  20.4 1.3 collective-permute-start.1
  22.4 22.6 %all-gather = bf16[16,64,18]{1,2,0:T(8,128)(2,1)S(1)} all-gather(bf16[1,64,18]{1,2,0:T(8,128)(2,1)S(1)} %maximum_bitcast_fusion), channel_id=1, replica_groups=mesh['seq'=2,'dp'=16] {'dp'}, dimensions={0}, use_global_device_ids=true | all-gather | bytes 39168 | tf_op jit(solution)/shard_map/all_gather | solution.py:465
  45.3 1.5 copy.124
  47.0 4.3 all-to-all-start
  51.4 58.4 %group_gather.3.grad_ref = bf16[16,256,1024]{2,1,0:T(8,128)(2,1)} custom-call(bf16[256,1024]{1,0:T(8,128)(2,1)} %bitcast.172), custom_call_target="tpu_custom_call" | custom-call | tf_op jit(solution)/shard_map/group_gather/pallas_call | solution.py:136
  111.3 1.1 convert_element_type.147
  112.6 1.2 multiply_convert_fusion
  114.0 3.3 fusion.10
  117.3 1.1 slice.122
  118.5 2.0 fusion.8
  120.5 1.1 slice_negate_fusion.1
  121.6 1.6 copy.87
  123.2 1.1 slice_negate_fusion.2
  124.3 1.0 copy.86
  125.3 1.5 fusion.44
  126.8 1.4 fusion.37
  128.2 6.3 fusion.75
  134.5 4.4 fusion.17
  139.0 2.6 multiply_reduce_fusion.5
  142.7 57.7 %group_gather.2 = (bf16[16,256,1024]{2,1,0:T(8,128)(2,1)}, f32[16,16,256]{2,1,0:T(8,128)}) custom-call(bf16[256,1024]{1,0:T(8,128)(2,1)} %copy-done.6, f32[16,256]{1,0:T(8,128)} %fusion.72.refs_1_), custom_call_target="tpu_custom_call" | custom-call | tf_op jit(solution)/shard_map/group_gather/pallas_call | solution.py:136
  200.5 1.5 constant_dynamic-slice_fusion.2.gate_ref
  202.0 15.7 %all-gather.12.cloned.1.call-done.gate_up_ref = bf16[1024,1024]{1,0:T(8,128)(2,1)} async-done(((bf16[512,1024]{1,0:T(8,128)(2,1)}), bf16[1024,1024]{1,0:T(8,128)(2,1)}) %all-gather.12.cloned.1.call-update) | async-done | bytes 2097168 | tf_op jit(solution)/shard_map/all_gather | solution.py:438
  217.7 49.9 %expert_layer.1 = (bf16[16,256,1024]{2,1,0:T(8,128)(2,1)}, bf16[16,256,1024]{2,1,0:T(8,128)(2,1)}, f32[16,8,256]{2,1,0:T(8,128)}, bf16[1024,1024]{1,0:T(8,128)(2,1)}, bf16[512,1024]{1,0:T(8,128)(2,1)}) custom-call(bf16[16,256,1024]{2,1,0:T(8,128)(2,1)} %get-tuple-element.20.rows_ref, bf16[16,256,1024]{2,1,0:T(8,128)(2,1)} %group_gather.3.grad_ref, ...), custom_call_target="tpu_custom_call" | custom-call | tf_op jit(solution)/shard_map/expert_layer/pallas_call | solution.py:359
  268.3 0.9 copy-done.2
  269.1 103.8 %group_reduce.1 = (f32[256,1024]{1,0:T(8,128)S(1)}, f32[256,1024]{1,0:T(8,128)S(1)}, f32[16,8,256]{2,1,0:T(8,128)S(1)}) custom-call(bf16[16,256,1024]{2,1,0:T(8,128)(2,1)} %get-tuple-element.22.mixed_ref, bf16[16,256,1024]{2,1,0:T(8,128)(2,1)} %get-tuple-element.23.normed_ref, f32[16,8,256]{2,1,0:T(8,128)S(1)} %copy-done.2), custom_call_target="tpu_custom_call" | custom-call | tf_op jit(solution)/shard_map/group_reduce/pallas_call | solution.py:270
  373.0 1.6 multiply_reduce_fusion.2
  374.6 1.9 multiply_reduce_fusion.1
  376.5 0.8 convolution_convert_fusion.2
  377.3 1.0 copy.93
  378.3 2.1 convolution_convert_fusion.1
  380.4 5.2 fusion.1
  385.6 1.0 slice-done.1
  386.6 2.9 fusion.3
  389.6 5.1 fusion.12
  394.7 1.4 fusion.16
  396.1 1.5 collective-permute-start.2
  399.0 11.8 %collective-permute-done.2 = bf16[256,1024]{0,1:T(8,128)(2,1)S(1)} collective-permute-done((bf16[256,1024]{0,1:T(8,128)(2,1)S(1)}, bf16[256,1024]{0,1:T(8,128)(2,1)S(1)}, u32[]{:S(2)}, u32[]{:S(2)}) %collective-permute-start.2) | collective-permute-done | bytes 524320 | tf_op jit(solution)/shard_map/ppermute | solution.py:556
  412.0 3.3 convolution_convert_fusion
  415.4 3.6 all-to-all-start.3
  419.5 10.8 %all-to-all-done.3 = bf16[8,32,1024]{2,1,0:T(8,128)(2,1)S(1)} async-done(((bf16[8,32,1024]{2,1,0:T(8,128)(2,1)}), bf16[8,32,1024]{2,1,0:T(8,128)(2,1)S(1)}, u32[]{:S(2)}, u32[]{:S(2)}) %all-to-all-start.3) | async-done | bytes 524320 | tf_op jit(solution)/shard_map/all_to_all | solution.py:445
  430.4 3.8 all-to-all-start.2
  434.2 4.9 fusion.29
  439.1 1.0 copy.108
  440.8 16.1 %reduce-scatter.10.cloned.1.call-done = bf16[64,1024]{1,0:T(8,128)(2,1)} async-done(((bf16[1024,1024]{1,0:T(8,128)(2,1)}), bf16[64,1024]{1,0:T(8,128)(2,1)}) %reduce-scatter.10.cloned.1.call-update) | async-done | bytes 131088 | tf_op jit(solution)/shard_map/reduce_scatter | solution.py:571
  456.9 75.9 %reduce-scatter.8.cloned.1.call-done = bf16[64,2048]{1,0:T(8,128)(2,1)} async-done(((bf16[1024,2048]{1,0:T(8,128)(2,1)}), bf16[64,2048]{1,0:T(8,128)(2,1)}) %reduce-scatter.8.cloned.1.call-update) | async-done | bytes 262160 | tf_op jit(solution)/shard_map/reduce_scatter | solution.py:571
  533.0 1.0 copy-done.8
  533.9 1.4 pad_maximum_fusion.10
  535.3 2.3 fusion.45
  537.7 54.6 %reduce-scatter.16.cloned.1.call-done = f32[64,18]{1,0:T(8,128)} async-done(((f32[1024,18]{1,0:T(8,128)}), f32[64,18]{1,0:T(8,128)}) %reduce-scatter.16.cloned.1.call-update) | async-done | bytes 4624
  592.2 0.8 copy.109
  593.1 5.0 all-reduce
  599.7 14.3 %all-gather.18.cloned.1.call-done = bf16[16,32,1024]{2,1,0:T(8,128)(2,1)} async-done(((bf16[8,32,1024]{2,1,0:T(8,128)(2,1)}), bf16[16,32,1024]{2,1,0:T(8,128)(2,1)}) %all-gather.18.cloned.1.call-update) | async-done | bytes 1048592 | tf_op jit(solution)/shard_map/all_gather | solution.py:448
  614.0 1.5 convert_bitcast_fusion.1
  615.5 2.5 copy.98
  618.0 24.2 %all-reduce.4.cloned.1.call-done = (bf16[64,2048]{1,0:T(8,128)(2,1)}, bf16[64,1024]{1,0:T(8,128)(2,1)}) async-done(((bf16[64,2048]{1,0:T(8,128)(2,1)}, bf16[64,1024]{1,0:T(8,128)(2,1)}), (bf16[64,2048]{1,0:T(8,128)(2,1)}, bf16[64,1024]{1,0:T(8,128)(2,1)})) %all-reduce.4.cloned.1.call-update) | async-done | bytes 393232 | tf_op jit(solution)/shard_map/psum | solution.py:574
  642.2 1.8 convert_element_type.178
  644.0 1.6 convert_element_type.180
  645.6 31.7 %all-gather.16.cloned.1.call-done = bf16[16,64,1024]{2,1,0:T(8,128)(2,1)} async-done(((bf16[8,64,1024]{2,1,0:T(8,128)(2,1)}), bf16[16,64,1024]{2,1,0:T(8,128)(2,1)}) %all-gather.16.cloned.1.call-update) | async-done | bytes 2097168 | tf_op jit(solution)/shard_map/all_gather | solution.py:448
  677.3 2.2 convert_bitcast_fusion
  679.5 4.4 copy.97
  (138 shorter events, 11.7 us)
Async XLA Ops:
  7.2 38.0 %copy-start = (bf16[64,16,1024]{2,1,0:T(8,128)(2,1)S(1)}, bf16[64,16,1024]{2,1,0:T(8,128)(2,1)}, u32[]{:S(2)}) copy-start(bf16[64,16,1024]{2,1,0:T(8,128)(2,1)} %param.19) | copy-start | bytes 6291460
  7.2 39.6 %copy-start.4 = (bf16[1,256,1024]{2,1,0:T(8,128)(2,1)S(1)}, bf16[1,256,1024]{2,1,0:T(8,128)(2,1)}, u32[]{:S(2)}) copy-start(bf16[1,256,1024]{2,1,0:T(8,128)(2,1)} %param.11) | copy-start | bytes 1572868
  7.2 106.8 %all-gather.8.cloned.1.call-start = ((), (), s32[]{:S(2)}) async-start(), calls=%async_computation.9 | async-start | bytes 4456448 | tf_op jit(solution)/shard_map/all_gather | solution.py:465
  7.9 131.1 %all-gather.10.cloned.1.call-start = ((), (), s32[]{:S(2)}) async-start(), calls=%async_computation.10 | async-start | bytes 2228224 | tf_op jit(solution)/shard_map/all_gather | solution.py:465
  10.9 36.1 %all-to-all-start.1 = ((bf16[8,32,1024]{2,1,0:T(8,128)(2,1)}), bf16[8,32,1024]{2,1,0:T(8,128)(2,1)S(1)}, u32[]{:S(2)}, u32[]{:S(2)}) async-start(bf16[8,32,1024]{2,1,0:T(8,128)(2,1)} %bitcast.176), calls=%async_computation.1 | async-start | bytes 1048576 | tf_op jit(solution)/shard_map/all_to_all | solution.py:434
  16.1 35.2 %copy-start.23 = (s32[1,256,8]{1,2,0:T(8,128)S(1)}, s32[1,256,8]{1,2,0:T(8,128)}, u32[]{:S(2)}) copy-start(s32[1,256,8]{1,2,0:T(8,128)} %param.13) | copy-start | bytes 24580
  16.1 95.1 %collective-permute-start = (bf16[256,1024]{1,0:T(8,128)(2,1)}, bf16[256,1024]{1,0:T(8,128)(2,1)}, u32[]{:S(2)}, u32[]{:S(2)}) collective-permute-start(bf16[256,1024]{1,0:T(8,128)(2,1)} %bitcast.167), channel_id=1, source_target_pairs={{0,16},{1,17},{2,18},{3,19},{4,20},{5,21},{6,22},{7,23},{8,24},{9,... | collective-permute-start | bytes 1572872 | tf_op jit(solution)/shard_map/ppermute | solution.py:463
  20.4 89.4 %collective-permute-start.1 = (s32[1,256]{1,0:T(1,128)}, s32[1,256]{1,0:T(1,128)S(1)}, u32[]{:S(2)}, u32[]{:S(2)}) collective-permute-start(s32[1,256]{1,0:T(1,128)} %param.12), channel_id=1, source_target_pairs={{0,16},{1,17},{2,18},{3,19},{4,20},{5,21},{6,22},{7,23},{8,24},{9,... | collective-permute-start | bytes 3080 | tf_op jit(solution)/shard_map/ppermute | solution.py:464
  45.2 64.6 %copy-start.19 = (bf16[1024,18]{0,1:T(8,128)(2,1)}, bf16[1024,18]{0,1:T(8,128)(2,1)S(1)}, u32[]{:S(2)}) copy-start(bf16[1024,18]{0,1:T(8,128)(2,1)S(1)} %reshape.236) | copy-start | bytes 110596
  47.0 62.8 %copy-start.12 = (bf16[8,32,1024]{2,1,0:T(8,128)(2,1)}, bf16[8,32,1024]{2,1,0:T(8,128)(2,1)S(1)}, u32[]{:S(2)}) copy-start(bf16[8,32,1024]{2,1,0:T(8,128)(2,1)S(1)} %all-to-all-done.1) | copy-start | bytes 1572868
  47.0 66.9 %all-to-all-start = ((bf16[8,64,1024]{2,1,0:T(8,128)(2,1)}), bf16[8,64,1024]{2,1,0:T(8,128)(2,1)}, u32[]{:S(2)}, u32[]{:S(2)}) async-start(bf16[8,64,1024]{2,1,0:T(8,128)(2,1)} %bitcast.159), calls=%async_computation | async-start | bytes 2097152 | tf_op jit(solution)/shard_map/all_to_all | solution.py:434
  51.2 150.8 %all-gather.14.cloned.1.call-start = ((), (), s32[]{:S(2)}) async-start(), calls=%async_computation.12 | async-start | bytes 1572864 | tf_op jit(solution)/shard_map/all_gather | solution.py:438
  51.4 58.4 %copy-start.24 = (s32[1,256]{1,0:T(1,128)S(1)}, s32[1,256]{1,0:T(1,128)}, u32[]{:S(2)}) copy-start(s32[1,256]{1,0:T(1,128)} %param.12) | copy-start | bytes 3076
  110.1 107.7 %all-gather.12.cloned.1.call-start = ((), (), s32[]{:S(2)}) async-start(), calls=%async_computation.11 | async-start | bytes 3145728 | tf_op jit(solution)/shard_map/all_gather | solution.py:438
  113.9 301.5 %reduce-scatter.14.cloned.1.call-start = ((), (), s32[]{:S(2)}) async-start(), calls=%async_computation.17 | async-start | bytes 1572864 | tf_op jit(solution)/shard_map/reduce_scatter | solution.py:441
  114.0 4.5 copy-start.25
  128.2 6.4 copy-start.14
  128.2 6.4 copy-start.17
  139.0 2.7 copy-start.10
  139.0 2.8 copy-start.20
  141.8 0.9 copy-start.6
  267.6 162.8 %reduce-scatter.12.cloned.1.call-start = ((), (), s32[]{:S(2)}) async-start(), calls=%async_computation.15 | async-start | bytes 3145728 | tf_op jit(solution)/shard_map/reduce_scatter | solution.py:441
  268.2 188.7 %reduce-scatter.10.cloned.1.call-start = ((), (), s32[]{:S(2)}) async-start(), calls=%async_computation.14 | async-start | bytes 2228224 | tf_op jit(solution)/shard_map/reduce_scatter | solution.py:571
  268.2 0.9 copy-start.2
  269.1 105.4 %copy-start.9 = (bf16[1,256,1024]{2,1,0:T(8,128)(2,1)S(1)}, bf16[1,256,1024]{2,1,0:T(8,128)(2,1)}, u32[]{:S(2)}) copy-start(bf16[1,256,1024]{2,1,0:T(8,128)(2,1)} %param.21) | copy-start | bytes 1572868
  373.0 3.5 copy-start.5
  376.5 1.8 copy-start.11
  380.4 5.2 slice-start
  380.4 6.2 slice-start.1
  389.5 143.4 %reduce-scatter.8.cloned.1.call-start = ((), (), s32[]{:S(2)}) async-start(), calls=%async_computation.13 | async-start | bytes 4456448 | tf_op jit(solution)/shard_map/reduce_scatter | solution.py:571
  389.6 5.1 copy-start.3
  389.6 5.1 copy-start.15
  396.1 14.7 %collective-permute-start.2 = (bf16[256,1024]{0,1:T(8,128)(2,1)S(1)}, bf16[256,1024]{0,1:T(8,128)(2,1)S(1)}, u32[]{:S(2)}, u32[]{:S(2)}) collective-permute-start(bf16[256,1024]{0,1:T(8,128)(2,1)S(1)} %fusion.33), channel_id=1, source_target_pairs={{16,0},{17,1},{18,2},{19,3},{20,4},{21,5},{22,6},{23,7},{24,8},{25... | collective-permute-start | bytes 1572872 | tf_op jit(solution)/shard_map/ppermute | solution.py:556
  399.0 12.3 %copy-start.18 = (bf16[256,1024]{0,1:T(8,128)(2,1)}, bf16[256,1024]{0,1:T(8,128)(2,1)S(1)}, u32[]{:S(2)}) copy-start(bf16[256,1024]{0,1:T(8,128)(2,1)S(1)} %fusion.39) | copy-start | bytes 1572868
  399.0 13.0 %copy-start.16 = (bf16[512,1024]{1,0:T(8,128)(2,1)S(1)}, bf16[512,1024]{1,0:T(8,128)(2,1)}, u32[]{:S(2)}) copy-start(bf16[512,1024]{1,0:T(8,128)(2,1)} %multiply_convert_fusion) | copy-start | bytes 3145732
  411.1 0.7 copy-start.21
  411.3 0.7 copy-start.22
  415.3 3.9 copy-start.7
  415.4 15.0 %all-to-all-start.3 = ((bf16[8,32,1024]{2,1,0:T(8,128)(2,1)}), bf16[8,32,1024]{2,1,0:T(8,128)(2,1)S(1)}, u32[]{:S(2)}, u32[]{:S(2)}) async-start(bf16[8,32,1024]{2,1,0:T(8,128)(2,1)} %bitcast.181), calls=%async_computation.7 | async-start | bytes 1048576 | tf_op jit(solution)/shard_map/all_to_all | solution.py:445
  430.4 8.8 %copy-start.13 = (bf16[8,32,1024]{2,1,0:T(8,128)(2,1)}, bf16[8,32,1024]{2,1,0:T(8,128)(2,1)S(1)}, u32[]{:S(2)}) copy-start(bf16[8,32,1024]{2,1,0:T(8,128)(2,1)S(1)} %all-to-all-done.3) | copy-start | bytes 1572868
  430.4 102.6 %all-to-all-start.2 = ((bf16[8,64,1024]{2,1,0:T(8,128)(2,1)}), bf16[8,64,1024]{2,1,0:T(8,128)(2,1)S(1)}, u32[]{:S(2)}, u32[]{:S(2)}) async-start(bf16[8,64,1024]{2,1,0:T(8,128)(2,1)} %bitcast.180), calls=%async_computation.5 | async-start | bytes 2097152 | tf_op jit(solution)/shard_map/all_to_all | solution.py:445
  434.2 158.1 %reduce-scatter.16.cloned.1.call-start = ((), (), s32[]{:S(2)}) async-start(), calls=%async_computation.19 | async-start | bytes 557056
  440.2 173.8 %all-gather.18.cloned.1.call-start = ((), (), s32[]{:S(2)}) async-start(), calls=%async_computation.18 | async-start | bytes 1572864 | tf_op jit(solution)/shard_map/all_gather | solution.py:448
  440.8 201.4 %all-reduce.4.cloned.1.call-start = ((), (), s32[]{:S(2)}) async-start(), calls=%async_computation.20 | async-start | bytes 786432 | tf_op jit(solution)/shard_map/psum | solution.py:574
  532.9 144.4 %all-gather.16.cloned.1.call-start = ((), (), s32[]{:S(2)}) async-start(), calls=%async_computation.16 | async-start | bytes 3145728 | tf_op jit(solution)/shard_map/all_gather | solution.py:448
  532.9 1.0 copy-start.8
  677.3 6.7 copy-start.1
Sparse Core Ops, SparseCore 0:
  10.2 63.8 all-gather.7
  76.3 50.6 all-gather.9
  128.6 32.1 all-gather.13
  162.2 55.4 all-gather.11
  267.7 31.5 reduce-scatter.13
  302.0 53.3 reduce-scatter.11
  389.6 67.2 reduce-scatter.9
  461.4 71.4 reduce-scatter.7
  537.0 55.1 reduce-scatter.15
  593.6 20.3 all-gather.17
  616.4 25.7 all-reduce.3
  644.2 33.0 all-gather.15

commit v3 on v2

--- a/solution.py
+++ b/solution.py
@@ -296,6 +296,351 @@
         ),
         name="group_reduce",
     )(mixed, normed, gate_grad)
+
+
+def column_parts(half, which):
+    tiles = half // 128
+    if tiles == 1:
+        sizes = (1, 0, 0)
+    elif which % 2 == 0:
+        big = -(-tiles // 3)
+        sizes = (big, big, tiles - 2 * big)
+    else:
+        small = tiles // 3
+        sizes = (small, small, tiles - 2 * small)
+    out, start = [], 0
+    for size in sizes:
+        out.append((start * 128, size * 128))
+        start += size
+    return out
+
+
+def shard_view(ref, halves, a, p, rank_value):
+    start, size = column_parts(halves[a], a)[p]
+    offset = pl.multiple_of((rank_value // RANKS) * halves[a] + start, 128)
+    return ref.at[:, rank_value % RANKS, :, pl.ds(offset, size)]
+
+
+def other_groups(groups_count):
+    dp = lax.axis_index("dp")
+    seq = lax.axis_index("seq")
+    place, home = dp % RANKS, dp // RANKS
+    return home, [
+        {"seq": seq, "dp": ((home + k) % groups_count) * RANKS + place} for k in range(1, groups_count)
+    ]
+
+
+def weights_gather_kernel(count, groups_count, *refs):
+    ins, outs = refs[:count], refs[count : 2 * count]
+    send, recv, far_send, far_recv, local = refs[2 * count :]
+    rank, peer = my_place()
+    home, far = other_groups(groups_count)
+    seq = lax.axis_index("seq")
+    halves = [ref.shape[1] // 2 for ref in ins]
+
+    def half(ref, a):
+        return ref.at[:, pl.ds(pl.multiple_of(seq * halves[a], 128), halves[a])]
+
+    def own_slot(a):
+        columns = pl.ds(pl.multiple_of(seq * halves[a], 128), halves[a])
+        return outs[a].at[home, rank % RANKS, :, columns]
+
+    own = [pltpu.make_async_copy(half(ins[a], a), own_slot(a), local.at[a]) for a in range(count)]
+    for copy in own:
+        copy.start()
+    barrier = pltpu.get_barrier_semaphore()
+    for there in [peer(bit) for bit in (1, 2, 4, 8)] + far:
+        pl.semaphore_signal(barrier, inc=1, device_id=there, device_id_type=MESH)
+    pl.semaphore_wait(barrier, 4 + len(far))
+    started, waiting = [], []
+    for k, there in enumerate(far):
+        for a in range(count):
+            copy = pltpu.make_async_remote_copy(
+                src_ref=half(ins[a], a),
+                dst_ref=own_slot(a),
+                send_sem=far_send.at[k, a],
+                recv_sem=far_recv.at[k, a],
+                device_id=there,
+                device_id_type=MESH,
+            )
+            copy.start()
+            started.append(copy)
+            waiting.append(copy)
+    for copy in own:
+        copy.wait()
+    for copy in waiting:
+        copy.wait_recv()
+
+    def remote(a, p, mask, bit, index):
+        view = shard_view(outs[a], halves, a, p, flip_mask(rank, mask))
+        copy = pltpu.make_async_remote_copy(
+            src_ref=view,
+            dst_ref=view,
+            send_sem=send.at[a, p, index],
+            recv_sem=recv.at[a, p, index],
+            device_id=peer(bit),
+            device_id_type=MESH,
+        )
+        copy.start()
+        started.append(copy)
+        return copy
+
+    live = {}
+    last = []
+    for step in range(4):
+        for p in range(3):
+            for a in range(count):
+                if column_parts(halves[a], a)[p][1] == 0:
+                    continue
+                order = LINKS[p]
+                if step > 0:
+                    for copy in live.pop((a, p)):
+                        copy.wait_recv()
+                if step < 3:
+                    live[(a, p)] = [
+                        remote(a, p, mask, order[step], 2**step - 1 + index)
+                        for index, mask in enumerate(subsets(order[:step]))
+                    ]
+                fresh = [0] if step == 0 else [m | order[step - 1] for m in subsets(order[: step - 1])]
+                base = 0 if step == 0 else 2 ** (step - 1)
+                for index, mask in enumerate(fresh):
+                    last.append(remote(a, p, mask, 1, 7 + base + index))
+    for copy in last:
+        copy.wait_recv()
+    for copy in started:
+        copy.wait_send()
+
+
+def weights_gather(collective_id, groups_count, *arrays):
+    count = len(arrays)
+    whole = pl.pallas_call(
+        functools.partial(weights_gather_kernel, count, groups_count),
+        out_shape=[
+            jax.ShapeDtypeStruct((groups_count, RANKS) + a.shape, a.dtype) for a in arrays
+        ],
+        in_specs=[pl.BlockSpec(memory_space=pltpu.VMEM)] * count,
+        out_specs=[pl.BlockSpec(memory_space=pl.ANY)] * count,
+        scratch_shapes=[
+            pltpu.SemaphoreType.DMA((count, 3, 15)),
+            pltpu.SemaphoreType.DMA((count, 3, 15)),
+            pltpu.SemaphoreType.DMA((max(groups_count - 1, 1), count)),
+            pltpu.SemaphoreType.DMA((max(groups_count - 1, 1), count)),
+            pltpu.SemaphoreType.DMA((count,)),
+        ],
+        compiler_params=pltpu.CompilerParams(collective_id=collective_id, has_side_effects=True),
+        name="weights_gather",
+    )(*arrays)
+    return [w.reshape(-1, w.shape[3]) for w in whole]
+
+
+def add_block(target, source, at, start, size):
+    groups, rows = source.shape[0], source.shape[1]
+    columns = pl.ds(start, size)
+    pieces = rows // 16
+
+    def step(i, carry):
+        lines = pl.ds(pl.multiple_of((i % pieces) * 16, 16), 16)
+        index = (i // pieces, lines, columns)
+        new = target[(at,) + index].astype(f32) + source[index].astype(f32)
+        target[(at,) + index] = new.astype(target.dtype)
+        return carry
+
+    lax.fori_loop(0, groups * pieces, step, 0)
+
+
+def weights_reduce_kernel(count, groups_count, *refs):
+    ins = refs[:count]
+    pieces = refs[count : count + 2]
+    outs = refs[count + 2 : 2 * count + 2]
+    whole = refs[2 * count + 2 : 2 * count + 4]
+    rest = refs[2 * count + 4 :]
+    total, got0, got1, got2, got3, far_got = [rest[i * count : (i + 1) * count] for i in range(6)]
+    sems, far_sems, seq_sems, piece_sems, local, own_sems = rest[6 * count :]
+    rank, peer = my_place()
+    chip, core = rank // 2, rank % 2
+    home, far = other_groups(groups_count)
+    seq = lax.axis_index("seq")
+    dp = lax.axis_index("dp")
+    halves = [ref.shape[3] // 2 for ref in ins]
+    parts = [column_parts(halves[a], a) for a in range(count)]
+
+    def half_view(ref, a, rank_value):
+        offset = pl.multiple_of((rank_value // RANKS) * halves[a], 128)
+        return ref.at[:, rank_value % RANKS, :, pl.ds(offset, halves[a])]
+
+    loads = []
+    for a in range(count):
+        for c in range(8):
+            copy = pltpu.make_async_copy(
+                half_view(ins[a], a, 2 * c + core), total[a].at[c], local.at[a, c]
+            )
+            copy.start()
+            loads.append(copy)
+    keeps = [
+        pltpu.make_async_copy(pieces[i].at[rank % RANKS], whole[i].at[rank], own_sems.at[i])
+        for i in range(2)
+    ]
+    for copy in keeps:
+        copy.start()
+    barrier = pltpu.get_barrier_semaphore()
+    everyone = [
+        {"seq": 1 - seq if mask & 8 else seq, "dp": flip_mask(dp, mask & 7)} for mask in range(1, 16)
+    ]
+    for there in everyone + far:
+        pl.semaphore_signal(barrier, inc=1, device_id=there, device_id_type=MESH)
+    pl.semaphore_wait(barrier, 15 + len(far))
+
+    started = []
+    live = {}
+
+    def send(a, p, stage, index, src, dst, bit):
+        copy = pltpu.make_async_remote_copy(
+            src_ref=src,
+            dst_ref=dst,
+            send_sem=sems.at[0, a, p, stage, index],
+            recv_sem=sems.at[1, a, p, stage, index],
+            device_id=peer(bit),
+            device_id_type=MESH,
+        )
+        copy.start()
+        started.append(copy)
+        live.setdefault((a, p), []).append(copy)
+
+    def chip_of(mask):
+        return flip_mask(rank, mask) // 2
+
+    for p in range(3):
+        for a in range(count):
+            columns = pl.ds(*parts[a][p])
+            if parts[a][p][1]:
+                for c in range(8):
+                    send(
+                        a, p, 0, c,
+                        shard_view(ins[a], halves, a, p, 2 * c + 1 - core),
+                        got0[a].at[c, :, :, columns],
+                        1,
+                    )
+    arrivals = []
+    for mask, there in zip(range(1, 16), everyone):
+        for i in range(2):
+            copy = pltpu.make_async_remote_copy(
+                src_ref=pieces[i].at[flip_mask(rank, mask) % RANKS],
+                dst_ref=whole[i].at[rank],
+                send_sem=piece_sems.at[0, i, mask],
+                recv_sem=piece_sems.at[1, i, mask],
+                device_id=there,
+                device_id_type=MESH,
+            )
+            copy.start()
+            arrivals.append(copy)
+    for copy in loads:
+        copy.wait()
+    got = (got1, got2, got3)
+    for stage in range(4):
+        for p in range(3):
+            for a in range(count):
+                start, size = parts[a][p]
+                if size == 0:
+                    continue
+                order = LINKS[p]
+                columns = pl.ds(start, size)
+                for copy in live.pop((a, p)):
+                    copy.wait_recv()
+                if stage == 0:
+
+                    def over_chips(c, carry, a=a, start=start, size=size):
+                        add_block(total[a], got0[a].at[c], c, start, size)
+                        return carry
+
+                    lax.fori_loop(0, 8, over_chips, 0)
+                else:
+                    for index, mask in enumerate(subsets(order[stage:])):
+                        add_block(total[a], got[stage - 1][a].at[index], chip_of(mask), start, size)
+                if stage < 3:
+                    for index, mask in enumerate(subsets(order[stage + 1 :])):
+                        send(
+                            a, p, stage + 1, index,
+                            total[a].at[chip_of(mask | order[stage]), :, :, columns],
+                            got[stage][a].at[index, :, :, columns],
+                            order[stage],
+                        )
+    waiting = []
+    for k, there in enumerate(far):
+        for a in range(count):
+            copy = pltpu.make_async_remote_copy(
+                src_ref=total[a].at[chip, there["dp"] // RANKS],
+                dst_ref=far_got[a].at[k],
+                send_sem=far_sems.at[0, k, a],
+                recv_sem=far_sems.at[1, k, a],
+                device_id=there,
+                device_id_type=MESH,
+            )
+            copy.start()
+            waiting.append(copy)
+    for copy in waiting:
+        copy.wait()
+    last = []
+    for a in range(count):
+        columns = pl.ds(pl.multiple_of(seq * halves[a], 128), halves[a])
+        value = total[a][chip, home].astype(f32)
+        for k in range(len(far)):
+            value = value + far_got[a][k].astype(f32)
+        outs[a][:, columns] = value.astype(outs[a].dtype)
+        copy = pltpu.make_async_remote_copy(
+            src_ref=outs[a].at[:, columns],
+            dst_ref=outs[a].at[:, columns],
+            send_sem=seq_sems.at[0, a],
+            recv_sem=seq_sems.at[1, a],
+            device_id=peer(8),
+            device_id_type=MESH,
+        )
+        copy.start()
+        last.append(copy)
+    for copy in last + arrivals:
+        copy.wait()
+    for copy in started:
+        copy.wait_send()
+    for copy in keeps:
+        copy.wait()
+
+
+def weights_reduce(collective_id, groups_count, arrays, pieces):
+    count = len(arrays)
+    views = [a.reshape(groups_count, RANKS, -1, a.shape[1]) for a in arrays]
+    rows = views[0].shape[2]
+    halves = [a.shape[1] // 2 for a in arrays]
+
+    def buffers(*lead):
+        return [
+            pltpu.VMEM(lead + (groups_count, rows, h), a.dtype) for h, a in zip(halves, arrays)
+        ]
+
+    far_buffers = [
+        pltpu.VMEM((max(groups_count - 1, 1), rows, h), a.dtype) for h, a in zip(halves, arrays)
+    ]
+    dma = pltpu.SemaphoreType.DMA
+    vmem = pl.BlockSpec(memory_space=pltpu.VMEM)
+    any_space = pl.BlockSpec(memory_space=pl.ANY)
+    return pl.pallas_call(
+        functools.partial(weights_reduce_kernel, count, groups_count),
+        out_shape=[jax.ShapeDtypeStruct((rows, a.shape[1]), a.dtype) for a in arrays]
+        + [jax.ShapeDtypeStruct((EXPERTS,) + p.shape[1:], p.dtype) for p in pieces],
+        in_specs=[any_space] * count + [vmem] * 2,
+        out_specs=[vmem] * count + [any_space] * 2,
+        scratch_shapes=buffers(8) + buffers(8) + buffers(4) + buffers(2) + buffers(1) + far_buffers
+        + [
+            dma((2, count, 3, 4, 8)),
+            dma((2, max(groups_count - 1, 1), count)),
+            dma((2, count)),
+            dma((2, 2, 16)),
+            dma((count, 8)),
+            dma((2,)),
+        ],
+        compiler_params=pltpu.CompilerParams(
+            collective_id=collective_id, has_side_effects=True, vmem_limit_bytes=48 * 2**20
+        ),
+        name="weights_reduce",
+    )(*views, *pieces)
 
 
 def expert_kernel(
@@ -441,12 +786,7 @@
         grad = lax.psum_scatter(
             grad, "dp", scatter_dimension=0, tiled=True, axis_index_groups=between
         )
-        grad = grad.reshape(RANKS, -1, grad.shape[1])
-        grad = lax.all_to_all(
-            grad, "dp", split_axis=0, concat_axis=0, tiled=True, axis_index_groups=inside
-        )
-        grad = lax.all_gather(grad, "seq", axis=0, tiled=True)
-        return jnp.swapaxes(grad, 0, 1).astype(f32)
+        return grad.reshape(RANKS, -1, grad.shape[1])
 
     def body(
         tokens, starts, routes, gain_one, query_key_value_weight, w_out,
@@ -462,16 +802,21 @@
 
         tokens_before = lax.ppermute(tokens[0], "seq", forward_pair)
         starts_before = lax.ppermute(starts, "seq", forward_pair)
-        gather = lambda value: lax.all_gather(value, "dp", axis=0, tiled=True)
-        qkv_weight = gather(query_key_value_weight)
-        out_weight = gather(w_out)
-        small = gather(jnp.concatenate([w_router, gain_one[:, None], gain_two[:, None]], 1))
+        spare = lambda value: jnp.pad(value, ((0, 0), (0, 128 - value.shape[1])))
+        qkv_weight, out_weight, small = weights_gather(
+            0,
+            groups_count,
+            query_key_value_weight,
+            w_out,
+            jnp.concatenate(
+                [spare(w_router), spare(jnp.stack([gain_one, gain_two], 1))], 1
+            ),
+        )
         router_weight = small[:, :EXPERTS]
-        gain_a = small[:, EXPERTS].astype(f32)
-        gain_b = small[:, EXPERTS + 1].astype(f32)
+        gain_a = small[:, 128].astype(f32)
+        gain_b = small[:, 129].astype(f32)
         gate_up_weight = expert_weight(w_gate_up, seq_rank)
         down_weight = expert_weight(w_down, seq_rank)
-        (grad_all,) = group_gather(0, cotangent[0])
 
         token_rows = tokens[0].astype(f32)
         grad_output = cotangent[0].astype(f32)
@@ -516,7 +861,7 @@
         chosen = jnp.any(routes[0][:, :, None] == expert_ids[None, None, :], axis=1)
         gates = jax.nn.softmax(jnp.where(chosen, logits, -jnp.inf), axis=-1)
 
-        rows_in, gates_all = group_gather(1, normed_two, gates.T)
+        rows_in, gates_all, grad_all = group_gather(1, normed_two, gates.T, cotangent[0])
         gate = lax.dynamic_slice_in_dim(gates_all, expert, 1, axis=1)
         mixed_part, normed_part, gate_grad_part, gate_up_wgrad, down_wgrad = expert_layer(
             rows_in, grad_all, gate, gate_up_weight, down_weight
@@ -568,21 +913,27 @@
         rows_branch, gain_one_grad = norm_back(token_rows, gain_a, normed_one_grad)
         input_grad = (hidden_grad + rows_branch).astype(bf16)[None]
 
-        scatter = lambda value: lax.psum_scatter(value, "dp", scatter_dimension=0, tiled=True)
-        little = jnp.concatenate([router_wgrad, gain_one_grad[:, None], gain_two_grad[:, None]], 1)
-        shards = (scatter(qkv_wgrad.astype(bf16)), scatter(out_wgrad.astype(bf16)), scatter(little), stat_sums)
-        summed = [lax.psum(part.astype(bf16), "seq").astype(f32) for part in shards]
-        stream_rms = jnp.sqrt(summed[3] / (both * MODEL_WIDTH)).reshape(1, 2)
+        little = jnp.concatenate(
+            [spare(router_wgrad), spare(jnp.stack([gain_one_grad, gain_two_grad], 1))], 1
+        )
+        qkv_shard, out_shard, little, gate_up_all, down_all = weights_reduce(
+            3,
+            groups_count,
+            (qkv_wgrad.astype(bf16), out_wgrad.astype(bf16), little),
+            (expert_weight_grad(gate_up_wgrad), expert_weight_grad(down_wgrad)),
+        )
+        stat_sums = lax.psum(stat_sums, "seq")
+        stream_rms = jnp.sqrt(stat_sums / (both * MODEL_WIDTH)).reshape(1, 2)
         return (
             output,
             input_grad,
-            summed[2][:, EXPERTS],
-            summed[0],
-            summed[1],
-            summed[2][:, EXPERTS + 1],
-            summed[2][:, :EXPERTS],
-            expert_weight_grad(gate_up_wgrad),
-            expert_weight_grad(down_wgrad),
+            little[:, 128],
+            qkv_shard.astype(f32),
+            out_shard.astype(f32),
+            little[:, 129],
+            little[:, :EXPERTS],
+            jnp.swapaxes(gate_up_all, 0, 1).astype(f32),
+            jnp.swapaxes(down_all, 0, 1).astype(f32),
             stream_rms,
         )
 

time: 698 us -> 555 us (0.80)
  waiting for transfers between devices: 258 us -> 44 us
  Pallas kernels: 270 us -> 351 us
  blocking collectives: 27.6 us -> 4.91 us
  other arithmetic: 28 us -> 37.3 us
  local copies, waits for them, and re-layouts: 23.8 us -> 32.8 us
  starting transfers between devices: 24.5 us -> 16.5 us
    pallas_call x0 -> x2, Pallas kernels: none -> 140 us  [the longest x1 93.4 us: weights_reduce(): pl.pallas_call(functools.partial(weights_reduce_kernel, count, groups_cou...]
    reduce_scatter x2 -> x0, waiting for transfers between devices: 92 us -> none  [body(): lax.psum_scatter(value, 'dp', scatter_dimension=0, tiled=True)]
    unnamed x13 -> x4, waiting for transfers between devices: 57.2 us -> 0.07 us
    all_gather x4 -> x0, waiting for transfers between devices: 46 us -> none  [the longest x2 46 us: expert_weight_grad(): grad = lax.all_gather(grad, 'seq', axis=0, tiled=True)]
    reduce_scatter x2, waiting for transfers between devices: 0.02 us -> 34.3 us  [expert_weight_grad(): lax.psum_scatter(grad, 'dp', scatter_dimension=0, tiled=True, axis_index_...]
    pallas_call x1, Pallas kernels: 104 us -> 71.4 us  [group_reduce(): pl.pallas_call(reduce_kernel, out_shape=[jax.ShapeDtypeStruct((rows, widt...]
    pallas_call x2 -> x1, Pallas kernels: 116 us -> 90.2 us  [group_gather(): pl.pallas_call(functools.partial(gather_kernel, count), out_shape=[jax.Sh...]
    psum x1 -> x0, waiting for transfers between devices: 24.2 us -> none  [body(): summed = [lax.psum(part.astype(bf16), 'seq').astype(f32) for part in shards]]
  transfers between devices with their start and end apart: 19 -> 9, of which waited for: 9 -> 2; matrix products, arithmetic and copies ran while one was open for 12% -> 15% of each run, Pallas kernels for 32% -> 25%
where the time goes in v3:
time: 555 us; the launch traced here: 546 us
  Pallas kernels  351 us (63%)
  matrix products  44.3 us (8%)
  waiting for transfers between devices  44 us (8%)
  other arithmetic  37.3 us (7%)
  local copies, waits for them, and re-layouts  32.8 us (6%)
  starting transfers between devices  16.5 us (3%)
  between operations  14.9 us (3%)
    pallas_call x1, Pallas kernels, weights_reduce(): pl.pallas_call(functools.partial(weights_reduce_kernel, count, groups_cou...  93.4 us
    pallas_call x1, Pallas kernels, group_gather(): pl.pallas_call(functools.partial(gather_kernel, count), out_shape=[jax.Sh...  90.2 us
    pallas_call x1, Pallas kernels, group_reduce(): pl.pallas_call(reduce_kernel, out_shape=[jax.ShapeDtypeStruct((rows, widt...  71.4 us
    pallas_call x1, Pallas kernels, expert_layer(): pl.pallas_call(expert_kernel, grid=(GROUP // shards,), out_shape=[jax.Sha...  49.9 us
    pallas_call x1, Pallas kernels, weights_gather(): pl.pallas_call(functools.partial(weights_gather_kernel, count, groups_cou...  46.2 us
    reduce_scatter x2, waiting for transfers between devices, expert_weight_grad(): lax.psum_scatter(grad, 'dp', scatter_dimension=0, tiled=True, axis_index_...  34.3 us
    unnamed x88, local copies, waits for them, and re-layouts  21.9 us
  transfers between devices with their start and end apart: 9, of which 2 were waited for; matrix products, arithmetic and copies ran while one was open for 15% of the time, Pallas kernels for 25%

profile of v3, /device:TPU:0, one launch (start us, length us, event | category | flops | bytes accessed | tf_op | source)
XLA Modules:
  0.0 545.9 jit_solution(9597992793433415183)
XLA Ops:
  7.2 5.8 %collective-permute-start = (bf16[256,1024]{1,0:T(8,128)(2,1)}, bf16[256,1024]{1,0:T(8,128)(2,1)}, u32[]{:S(2)}, u32[]{:S(2)}) collective-permute-start(bf16[256,1024]{1,0:T(8,128)(2,1)} %bitcast.166), channel_id=1, source_target_pairs={{0,16},{1,17},{2,18},{3,19},{4,20},{5,21},{6,22},{7,23},{8,24},{9,... | collective-permute-start | bytes 1572872 | tf_op jit(solution)/shard_map/ppermute | solution.py:803
  13.1 1.3 collective-permute-start.1
  14.4 1.1 constant_dynamic-slice_fusion
  15.4 1.1 copy.133
  16.5 4.2 all-to-all-start.1
  20.7 1.1 bitcast_convert_fusion
  21.9 1.2 fusion.22
  24.0 46.2 %weights_gather.1 = (bf16[2,8,64,2048]{3,2,1,0:T(8,128)(2,1)}, bf16[2,8,64,1024]{3,2,1,0:T(8,128)(2,1)}, bf16[2,8,64,256]{3,2,1,0:T(8,128)(2,1)}) custom-call(bf16[64,2048]{1,0:T(8,128)(2,1)} %refs_0_.1, bf16[64,1024]{1,0:T(8,128)(2,1)} %refs_1_.1, bf16[64,256]{1,0:T(8,128)(2,1)} %fusion.60.refs_2_), custom_call_target="tpu_custom_call" | custom-call | tf_op jit(solution)/shard_map/weights_gather/pallas_call | solution.py:416
  70.2 2.1 slice_convert_fusion.2
  72.3 1.1 constant_dynamic-slice_fusion.1
  74.0 1.2 copy.119
  75.2 1.2 copy.120
  76.4 2.8 copy.132
  79.8 0.8 fusion.47
  80.6 1.1 convert_element_type.147
  82.2 1.0 copy-done.23
  83.2 1.3 fusion.10
  84.5 1.3 copy-done.22
  86.3 3.6 all-to-all-start
  89.9 2.7 fusion.8
  92.6 1.0 slice_negate_fusion.1
  93.7 1.1 slice_negate_fusion.2
  94.8 2.1 slice.192
  96.9 2.0 copy.89
  98.9 2.2 fusion.37
  101.1 1.6 fusion.44
  102.7 7.4 %fusion.78 = (f32[8,2,256]{2,1,0:T(2,128)S(1)}, f32[8,2,256,512]{2,3,1,0:T(8,128)}) fusion(pred[256,512]{0,1:T(8,128)(4,1)} %fusion.47, bf16[512,8,64,1]{0,2,3,1:T(8,128)(2,1)S(1)} %fusion.44, bf16[256,8,2,64]{0,3,2,1:T(8,128)(2,1)} %fusion.37), kind=kOutput, calls=%fused_computation.168 | convolution fusion | flops 276824576 | bytes 9584640 | tf_op jit(solution)/shard_map/sub | solution.py:851
  110.1 1.0 copy-done.13
  111.4 4.4 fusion.17
  115.8 0.8 multiply_reduce_fusion.5
  118.0 90.2 %group_gather.1 = (bf16[16,256,1024]{2,1,0:T(8,128)(2,1)}, f32[16,16,256]{2,1,0:T(8,128)}, bf16[16,256,1024]{2,1,0:T(8,128)(2,1)}) custom-call(bf16[256,1024]{1,0:T(8,128)(2,1)} %copy-done.10, f32[16,256]{1,0:T(8,128)} %fusion.75.refs_1_, bf16[256,1024]{1,0:T(8,128)(2,1)} %bitcast.177), custom_call_target="tpu_custom_call" | custom-call | tf_op jit(solution)/shard_map/group_gather/pallas_call | solution.py:136
  208.2 1.5 constant_dynamic-slice_fusion.2.gate_ref
  209.7 49.9 %expert_layer.1 = (bf16[16,256,1024]{2,1,0:T(8,128)(2,1)}, bf16[16,256,1024]{2,1,0:T(8,128)(2,1)}, f32[16,8,256]{2,1,0:T(8,128)}, bf16[1024,1024]{1,0:T(8,128)(2,1)}, bf16[512,1024]{1,0:T(8,128)(2,1)}) custom-call(bf16[16,256,1024]{2,1,0:T(8,128)(2,1)} %get-tuple-element.32.rows_ref, bf16[16,256,1024]{2,1,0:T(8,128)(2,1)} %get-tuple-element.33.grad_ref, ...), custom_call_target="tpu_custom_call" | custom-call | tf_op jit(solution)/shard_map/expert_layer/pallas_call | solution.py:704
  259.6 0.9 copy-done.4
  260.5 71.4 %group_reduce.1 = (f32[256,1024]{1,0:T(8,128)S(1)}, f32[256,1024]{1,0:T(8,128)S(1)}, f32[16,8,256]{2,1,0:T(8,128)S(1)}) custom-call(bf16[16,256,1024]{2,1,0:T(8,128)(2,1)} %get-tuple-element.35.mixed_ref, bf16[16,256,1024]{2,1,0:T(8,128)(2,1)} %get-tuple-element.36.normed_ref, f32[16,8,256]{2,1,0:T(8,128)S(1)} %copy-done.4), custom_call_target="tpu_custom_call" | custom-call | tf_op jit(solution)/shard_map/group_reduce/pallas_call | solution.py:270
  332.0 1.5 multiply_reduce_fusion.2
  333.6 1.9 multiply_reduce_fusion.1
  335.5 0.7 convolution_convert_fusion.2
  336.5 8.1 %fusion.1 = (f32[8,2,256]{2,1,0:T(2,128)S(1)}, f32[8,512,256,2]{2,1,3,0:T(8,128)}) fusion(f32[8,2,256,512]{2,3,1,0:T(8,128)} %get-tuple-element.117, f32[8,2,256]{2,1,0:T(2,128)S(1)} %get-tuple-element.116, bf16[512,8,64,1]{0,2,3,1:T(8,128)(2,1)S(1)} %bitcast.185, bf16[256,8,2,64]{0,3,2,1:T(8,128)(2,1)S(1)} %bitcast.186), kind=kOutput, calls=%fused_computation.3 | convolution fusion | flops 274722816 | bytes 17858560 | tf_op jit(solution)/shard_map/qgrd,kgd->grqk/dot_general | solution.py:888
  344.7 7.1 %fusion.3 = bf16[8,2,256,512]{2,3,1,0:T(8,128)(2,1)S(1)} fusion(f32[8,512,256,2]{2,1,3,0:T(8,128)} %get-tuple-element.124, f32[8,2,256]{2,1,0:T(2,128)S(1)} %get-tuple-element.123, f32[8,2,256,512]{2,3,1,0:T(8,128)} %get-tuple-element.117, f32[8,2,256]{2,1,0:T(2,128)S(1)} %get-tuple-element.116), kind=kLoop, calls=%fused_computation.5 | loop fusion | flops 8388608 | bytes 21004288 | tf_op jit(solution)/shard_map/convert_element_type | solution.py:890
  351.8 1.4 pad_maximum_fusion.10
  353.2 0.8 fusion.21
  354.0 1.1 bitcast_multiply_fusion.1
  355.2 5.8 %fusion.12 = f32[8,64,512,1]{2,1,3,0:T(8,128)} fusion(bf16[256,8,2,64]{0,3,2,1:T(8,128)(2,1)S(1)} %bitcast.187, f32[8,2,256,512]{2,3,1,0:T(8,128)} %get-tuple-element.117, f32[8,2,256]{2,1,0:T(2,128)S(1)} %get-tuple-element.116), kind=kOutput, calls=%fused_computation.23 | convolution fusion | flops 272629760 | bytes 9977856 | tf_op jit(solution)/shard_map/grqk,qgrd->kgd/dot_general | solution.py:897
  361.0 2.1 fusion.76
  363.1 4.9 psum.7
  368.0 1.3 pad_maximum_fusion.2
  369.5 0.9 copy-done.6
  370.5 1.4 fusion.16
  371.9 1.3 collective-permute-start.2
  374.1 2.1 convolution_convert_fusion.1
  376.2 9.6 %collective-permute-done.2 = bf16[256,1024]{0,1:T(8,128)(2,1)S(1)} collective-permute-done((bf16[256,1024]{0,1:T(8,128)(2,1)S(1)}, bf16[256,1024]{0,1:T(8,128)(2,1)S(1)}, u32[]{:S(2)}, u32[]{:S(2)}) %collective-permute-start.2) | collective-permute-done | bytes 524320 | tf_op jit(solution)/shard_map/ppermute | solution.py:901
  386.3 2.4 fusion.29
  388.7 1.1 select_maximum_fusion
  389.8 1.6 copy.101
  391.5 2.3 fusion.45
  393.8 4.4 convolution_convert_fusion
  398.3 34.3 %reduce-scatter.3.cloned.1.call-done = bf16[512,1024]{1,0:T(8,128)(2,1)} async-done(((bf16[1024,1024]{1,0:T(8,128)(2,1)}), bf16[512,1024]{1,0:T(8,128)(2,1)}) %reduce-scatter.3.cloned.1.call-update) | async-done | bytes 1048592 | tf_op jit(solution)/shard_map/reduce_scatter | solution.py:786
  432.6 1.2 copy-done.2
  433.8 1.0 copy-done.3
  434.8 93.4 %weights_reduce.1 = (bf16[64,2048]{1,0:T(8,128)(2,1)S(1)}, bf16[64,1024]{1,0:T(8,128)(2,1)S(1)}, f32[64,256]{1,0:T(8,128)S(1)}, bf16[16,64,1024]{2,1,0:T(8,128)(2,1)S(1)}, bf16[16,32,1024]{2,1,0:T(8,128)(2,1)S(1)}) custom-call(bf16[2,8,64,2048]{3,2,1,0:T(8,128)(2,1)} %bitcast.171, bf16[2,8,64,1024]{3,2,1,0:T(8,128)(2,1)} %bitcast.165, ...), custom_call_target="tpu_custom_call" | custom-call | tf_op jit(solution)/shard_map/weights_reduce/pallas_call | solution.py:624
  529.4 4.4 copy.103
  534.1 2.5 copy.104
  536.7 0.8 convert_element_type.177
  (136 shorter events, 9.6 us)
Async XLA Ops:
  7.2 65.1 %copy-start = (bf16[64,16,1024]{2,1,0:T(8,128)(2,1)S(1)}, bf16[64,16,1024]{2,1,0:T(8,128)(2,1)}, u32[]{:S(2)}) copy-start(bf16[64,16,1024]{2,1,0:T(8,128)(2,1)} %param.19) | copy-start | bytes 6291460
  7.2 15.9 %copy-start.39 = (bf16[64]{0:T(256)(128)(2,1)S(1)}, bf16[64]{0:T(256)(128)(2,1)}, u32[]{:S(2)}) copy-start(bf16[64]{0:T(256)(128)(2,1)} %param.14) | copy-start | bytes 388
  7.2 15.9 %copy-start.38 = (bf16[64]{0:T(256)(128)(2,1)S(1)}, bf16[64]{0:T(256)(128)(2,1)}, u32[]{:S(2)}) copy-start(bf16[64]{0:T(256)(128)(2,1)} %param.17) | copy-start | bytes 388
  7.2 16.0 %copy-start.34 = (bf16[64,16]{0,1:T(8,128)(2,1)S(1)}, bf16[64,16]{0,1:T(8,128)(2,1)}, u32[]{:S(2)}) copy-start(bf16[64,16]{0,1:T(8,128)(2,1)} %param.18) | copy-start | bytes 6148
  7.2 65.1 %copy-start.31 = (s32[1,256,8]{1,2,0:T(8,128)S(1)}, s32[1,256,8]{1,2,0:T(8,128)}, u32[]{:S(2)}) copy-start(s32[1,256,8]{1,2,0:T(8,128)} %param.13) | copy-start | bytes 24580
  7.2 73.3 %collective-permute-start = (bf16[256,1024]{1,0:T(8,128)(2,1)}, bf16[256,1024]{1,0:T(8,128)(2,1)}, u32[]{:S(2)}, u32[]{:S(2)}) collective-permute-start(bf16[256,1024]{1,0:T(8,128)(2,1)} %bitcast.166), channel_id=1, source_target_pairs={{0,16},{1,17},{2,18},{3,19},{4,20},{5,21},{6,22},{7,23},{8,24},{9,... | collective-permute-start | bytes 1572872 | tf_op jit(solution)/shard_map/ppermute | solution.py:803
  13.1 66.2 %collective-permute-start.1 = (s32[1,256]{1,0:T(1,128)}, s32[1,256]{1,0:T(1,128)S(1)}, u32[]{:S(2)}, u32[]{:S(2)}) collective-permute-start(s32[1,256]{1,0:T(1,128)} %param.12), channel_id=1, source_target_pairs={{0,16},{1,17},{2,18},{3,19},{4,20},{5,21},{6,22},{7,23},{8,24},{9,... | collective-permute-start | bytes 3080 | tf_op jit(solution)/shard_map/ppermute | solution.py:804
  16.5 69.7 %all-to-all-start.1 = ((bf16[8,32,1024]{2,1,0:T(8,128)(2,1)}), bf16[8,32,1024]{2,1,0:T(8,128)(2,1)}, u32[]{:S(2)}, u32[]{:S(2)}) async-start(bf16[8,32,1024]{2,1,0:T(8,128)(2,1)} %bitcast.157), calls=%async_computation.1 | async-start | bytes 1048576 | tf_op jit(solution)/shard_map/all_to_all | solution.py:779
  21.9 57.4 %copy-start.35 = (s32[1,256]{1,0:T(1,128)S(1)}, s32[1,256]{1,0:T(1,128)}, u32[]{:S(2)}) copy-start(s32[1,256]{1,0:T(1,128)} %param.12) | copy-start | bytes 3076
  79.2 4.0 copy-start.36
  82.2 1.0 copy-start.23
  84.5 1.3 copy-start.22
  86.3 23.9 %all-to-all-start = ((bf16[8,64,1024]{2,1,0:T(8,128)(2,1)}), bf16[8,64,1024]{2,1,0:T(8,128)(2,1)S(1)}, u32[]{:S(2)}, u32[]{:S(2)}) async-start(bf16[8,64,1024]{2,1,0:T(8,128)(2,1)} %bitcast.156), calls=%async_computation | async-start | bytes 2097152 | tf_op jit(solution)/shard_map/all_to_all | solution.py:779
  89.8 119.9 %all-gather.5.cloned.1.call-start = ((), (), s32[]{:S(2)}) async-start(), calls=%async_computation.5 | async-start | bytes 1572864 | tf_op jit(solution)/shard_map/all_gather | solution.py:783
  93.7 116.1 %all-gather.3.cloned.1.call-start = ((), (), s32[]{:S(2)}) async-start(), calls=%async_computation.4 | async-start | bytes 3145728 | tf_op jit(solution)/shard_map/all_gather | solution.py:783
  102.7 7.4 %copy-start.14 = (bf16[512,8,64,1]{0,2,3,1:T(8,128)(2,1)}, bf16[512,8,64,1]{0,2,3,1:T(8,128)(2,1)S(1)}, u32[]{:S(2)}) copy-start(bf16[512,8,64,1]{0,2,3,1:T(8,128)(2,1)S(1)} %fusion.44) | copy-start | bytes 1572868
  102.7 8.7 %copy-start.24 = (bf16[512,512]{0,1:T(8,128)(2,1)S(1)}, bf16[512,512]{0,1:T(8,128)(2,1)}, u32[]{:S(2)}) copy-start(bf16[512,512]{0,1:T(8,128)(2,1)} %copy.89) | copy-start | bytes 1572868
  110.1 1.0 copy-start.13
  111.1 287.1 %reduce-scatter.5.cloned.1.call-start = ((), (), s32[]{:S(2)}) async-start(), calls=%async_computation.7 | async-start | bytes 1572864 | tf_op jit(solution)/shard_map/reduce_scatter | solution.py:786
  111.4 4.4 copy-start.7
  111.4 4.4 copy-start.8
  115.8 0.9 copy-start.16
  115.8 1.2 copy-start.19
  117.0 0.9 copy-start.10
  259.6 0.9 copy-start.4
  260.5 71.5 %copy-start.20 = (bf16[2,8,64,256]{3,2,1,0:T(8,128)(2,1)S(1)}, bf16[2,8,64,256]{3,2,1,0:T(8,128)(2,1)}, u32[]{:S(2)}) copy-start(bf16[2,8,64,256]{3,2,1,0:T(8,128)(2,1)} %get-tuple-element.29) | copy-start | bytes 1572868
  260.5 73.1 %copy-start.18 = (bf16[1,256,1024]{2,1,0:T(8,128)(2,1)S(1)}, bf16[1,256,1024]{2,1,0:T(8,128)(2,1)}, u32[]{:S(2)}) copy-start(bf16[1,256,1024]{2,1,0:T(8,128)(2,1)} %param.21) | copy-start | bytes 1572868
  332.0 3.5 copy-start.9
  335.5 1.0 copy-start.25
  336.4 8.1 %copy-start.26 = (bf16[256,1024]{0,1:T(8,128)(2,1)}, bf16[256,1024]{0,1:T(8,128)(2,1)S(1)}, u32[]{:S(2)}) copy-start(bf16[256,1024]{0,1:T(8,128)(2,1)S(1)} %copy.97) | copy-start | bytes 1572868
  344.6 88.0 %reduce-scatter.3.cloned.1.call-start = ((), (), s32[]{:S(2)}) async-start(), calls=%async_computation.6 | async-start | bytes 3145728 | tf_op jit(solution)/shard_map/reduce_scatter | solution.py:786
  344.7 8.6 %copy-start.15 = (bf16[512,8,64,1]{0,2,3,1:T(8,128)(2,1)S(1)}, bf16[512,8,64,1]{0,2,3,1:T(8,128)(2,1)}, u32[]{:S(2)}) copy-start(bf16[512,8,64,1]{0,2,3,1:T(8,128)(2,1)} %copy-done.14) | copy-start | bytes 1572868
  351.8 2.2 copy-start.5
  353.2 1.9 copy-start.27
  368.0 2.3 copy-start.6
  368.0 2.5 copy-start.21
  369.3 2.6 copy-start.12
  370.5 15.8 %copy-start.28 = (bf16[256,1024]{0,1:T(8,128)(2,1)}, bf16[256,1024]{0,1:T(8,128)(2,1)S(1)}, u32[]{:S(2)}) copy-start(bf16[256,1024]{0,1:T(8,128)(2,1)S(1)} %fusion.39) | copy-start | bytes 1572868
  370.5 2.8 copy-start.11
  370.5 3.6 copy-start.17
  371.9 13.8 %collective-permute-start.2 = (bf16[256,1024]{0,1:T(8,128)(2,1)S(1)}, bf16[256,1024]{0,1:T(8,128)(2,1)S(1)}, u32[]{:S(2)}, u32[]{:S(2)}) collective-permute-start(bf16[256,1024]{0,1:T(8,128)(2,1)S(1)} %fusion.33), channel_id=1, source_target_pairs={{16,0},{17,1},{18,2},{19,3},{20,4},{21,5},{22,6},{23,7},{24,8},{25... | collective-permute-start | bytes 1572872 | tf_op jit(solution)/shard_map/ppermute | solution.py:901
  376.2 10.1 %copy-start.33 = (f32[256]{0:T(256)S(1)}, f32[256]{0:T(256)}, u32[]{:S(2)}) copy-start(f32[256]{0:T(256)} %get-tuple-element.113) | copy-start | bytes 3076
  376.2 10.1 %copy-start.37 = (bf16[2,8,64,2048]{3,2,1,0:T(8,128)(2,1)S(1)}, bf16[2,8,64,2048]{3,2,1,0:T(8,128)(2,1)}, u32[]{:S(2)}) copy-start(bf16[2,8,64,2048]{3,2,1,0:T(8,128)(2,1)} %get-tuple-element.30) | copy-start | bytes 12582916
  386.3 2.4 copy-start.30
  388.7 2.8 copy-start.32
  389.8 4.0 copy-start.29
  432.6 1.2 copy-start.2
  433.8 1.0 copy-start.3
  533.9 5.0 copy-start.1
Sparse Core Ops, SparseCore 0:
  93.8 34.8 all-gather.4
  130.8 55.4 all-gather.2
  344.7 30.7 reduce-scatter.4
  378.2 54.2 reduce-scatter.2

commit v4 on v3

--- a/solution.py
+++ b/solution.py
@@ -146,6 +146,7 @@
             pltpu.SemaphoreType.DMA((count,)),
         ],
         compiler_params=pltpu.CompilerParams(collective_id=collective_id, has_side_effects=True),
+        cost_estimate=pl.CostEstimate(flops=60000000000, bytes_accessed=2**24, transcendentals=0),
         name="group_gather",
     )(*arrays)
 
@@ -160,8 +161,8 @@
 
 
 def reduce_kernel(
-    mixed_ref, normed_ref, gate_ref, mixed_out, normed_out, gate_out,
-    total, got0, got1, got2, got3, sems, gate_sems, local, own_gate,
+    groups_count, mixed_ref, normed_ref, gate_ref, weights_ref, mixed_out, normed_out, gate_out, far_out,
+    total, got0, got1, got2, got3, sems, gate_sems, local, own_gate, far_sems,
 ):
     rank, peer = my_place()
     chip = rank // 2
@@ -181,9 +182,10 @@
     everyone = [
         {"seq": 1 - seq if mask & 8 else seq, "dp": flip_mask(dp, mask & 7)} for mask in range(1, 16)
     ]
-    for there in everyone:
+    home, far = other_groups(groups_count)
+    for there in everyone + far:
         pl.semaphore_signal(barrier, inc=1, device_id=there, device_id_type=MESH)
-    pl.semaphore_wait(barrier, 15)
+    pl.semaphore_wait(barrier, 15 + len(far))
     gates = []
     keep = pltpu.make_async_copy(gate_ref.at[rank], gate_out.at[rank], own_gate)
     keep.start()
@@ -225,6 +227,17 @@
                 send(
                     t, p, 0, c, ins[t].at[2 * c + 1 - core, rows], got0.at[t, c, rows], 1
                 )
+    for k, there in enumerate(far):
+        copy = pltpu.make_async_remote_copy(
+            src_ref=weights_ref.at[there["dp"] // RANKS],
+            dst_ref=far_out.at[k],
+            send_sem=far_sems.at[0, k],
+            recv_sem=far_sems.at[1, k],
+            device_id=there,
+            device_id_type=MESH,
+        )
+        copy.start()
+        gates.append(copy)
     for copy in loads:
         copy.wait()
     got = (got1, got2, got3)
@@ -265,19 +278,23 @@
     keep.wait()
 
 
-def group_reduce(collective_id, mixed, normed, gate_grad):
+def group_reduce(collective_id, mixed, normed, gate_grad, weights):
     rows, width = mixed.shape[1:]
+    groups_count = weights.shape[0]
+    others = max(groups_count - 1, 1)
     return pl.pallas_call(
-        reduce_kernel,
+        functools.partial(reduce_kernel, groups_count),
         out_shape=[
             jax.ShapeDtypeStruct((rows, width), f32),
             jax.ShapeDtypeStruct((rows, width), f32),
             jax.ShapeDtypeStruct(gate_grad.shape, gate_grad.dtype),
+            jax.ShapeDtypeStruct((others,) + weights.shape[1:], weights.dtype),
         ],
-        in_specs=[pl.BlockSpec(memory_space=pl.ANY)] * 3,
+        in_specs=[pl.BlockSpec(memory_space=pl.ANY)] * 4,
         out_specs=[
             pl.BlockSpec(memory_space=pltpu.VMEM),
             pl.BlockSpec(memory_space=pltpu.VMEM),
+            pl.BlockSpec(memory_space=pl.ANY),
             pl.BlockSpec(memory_space=pl.ANY),
         ],
         scratch_shapes=[
@@ -290,12 +307,14 @@
             pltpu.SemaphoreType.DMA((2, 16)),
             pltpu.SemaphoreType.DMA((2, 8)),
             pltpu.SemaphoreType.DMA(()),
+            pltpu.SemaphoreType.DMA((2, others)),
         ],
         compiler_params=pltpu.CompilerParams(
             collective_id=collective_id, has_side_effects=True, vmem_limit_bytes=48 * 2**20
         ),
+        cost_estimate=pl.CostEstimate(flops=70000000000, bytes_accessed=2**24, transcendentals=0),
         name="group_reduce",
-    )(mixed, normed, gate_grad)
+    )(mixed, normed, gate_grad, weights)
 
 
 def column_parts(half, which):
@@ -428,6 +447,7 @@
             pltpu.SemaphoreType.DMA((count,)),
         ],
         compiler_params=pltpu.CompilerParams(collective_id=collective_id, has_side_effects=True),
+        cost_estimate=pl.CostEstimate(flops=45000000000, bytes_accessed=2**24, transcendentals=0),
         name="weights_gather",
     )(*arrays)
     return [w.reshape(-1, w.shape[3]) for w in whole]
@@ -450,10 +470,10 @@
 
 def weights_reduce_kernel(count, groups_count, *refs):
     ins = refs[:count]
-    pieces = refs[count : count + 2]
-    outs = refs[count + 2 : 2 * count + 2]
-    whole = refs[2 * count + 2 : 2 * count + 4]
-    rest = refs[2 * count + 4 :]
+    pieces = refs[count]
+    outs = refs[count + 1 : 2 * count + 1]
+    whole = refs[2 * count + 1]
+    rest = refs[2 * count + 2 :]
     total, got0, got1, got2, got3, far_got = [rest[i * count : (i + 1) * count] for i in range(6)]
     sems, far_sems, seq_sems, piece_sems, local, own_sems = rest[6 * count :]
     rank, peer = my_place()
@@ -476,12 +496,8 @@
             )
             copy.start()
             loads.append(copy)
-    keeps = [
-        pltpu.make_async_copy(pieces[i].at[rank % RANKS], whole[i].at[rank], own_sems.at[i])
-        for i in range(2)
-    ]
-    for copy in keeps:
-        copy.start()
+    keep = pltpu.make_async_copy(pieces.at[rank % RANKS], whole.at[rank], own_sems)
+    keep.start()
     barrier = pltpu.get_barrier_semaphore()
     everyone = [
         {"seq": 1 - seq if mask & 8 else seq, "dp": flip_mask(dp, mask & 7)} for mask in range(1, 16)
@@ -522,17 +538,16 @@
                     )
     arrivals = []
     for mask, there in zip(range(1, 16), everyone):
-        for i in range(2):
-            copy = pltpu.make_async_remote_copy(
-                src_ref=pieces[i].at[flip_mask(rank, mask) % RANKS],
-                dst_ref=whole[i].at[rank],
-                send_sem=piece_sems.at[0, i, mask],
-                recv_sem=piece_sems.at[1, i, mask],
-                device_id=there,
-                device_id_type=MESH,
-            )
-            copy.start()
-            arrivals.append(copy)
+        copy = pltpu.make_async_remote_copy(
+            src_ref=pieces.at[flip_mask(rank, mask) % RANKS],
+            dst_ref=whole.at[rank],
+            send_sem=piece_sems.at[0, mask],
+            recv_sem=piece_sems.at[1, mask],
+            device_id=there,
+            device_id_type=MESH,
+        )
+        copy.start()
+        arrivals.append(copy)
     for copy in loads:
         copy.wait()
     got = (got1, got2, got3)
@@ -600,8 +615,7 @@
         copy.wait()
     for copy in started:
         copy.wait_send()
-    for copy in keeps:
-        copy.wait()
+    keep.wait()
 
 
 def weights_reduce(collective_id, groups_count, arrays, pieces):
@@ -624,28 +638,29 @@
     return pl.pallas_call(
         functools.partial(weights_reduce_kernel, count, groups_count),
         out_shape=[jax.ShapeDtypeStruct((rows, a.shape[1]), a.dtype) for a in arrays]
-        + [jax.ShapeDtypeStruct((EXPERTS,) + p.shape[1:], p.dtype) for p in pieces],
-        in_specs=[any_space] * count + [vmem] * 2,
-        out_specs=[vmem] * count + [any_space] * 2,
+        + [jax.ShapeDtypeStruct((EXPERTS,) + pieces.shape[1:], pieces.dtype)],
+        in_specs=[any_space] * count + [vmem],
+        out_specs=[vmem] * count + [any_space],
         scratch_shapes=buffers(8) + buffers(8) + buffers(4) + buffers(2) + buffers(1) + far_buffers
         + [
             dma((2, count, 3, 4, 8)),
             dma((2, max(groups_count - 1, 1), count)),
             dma((2, count)),
-            dma((2, 2, 16)),
+            dma((2, 16)),
             dma((count, 8)),
-            dma((2,)),
+            dma(()),
         ],
         compiler_params=pltpu.CompilerParams(
             collective_id=collective_id, has_side_effects=True, vmem_limit_bytes=48 * 2**20
         ),
+        cost_estimate=pl.CostEstimate(flops=80000000000, bytes_accessed=2**24, transcendentals=0),
         name="weights_reduce",
-    )(*views, *pieces)
+    )(*views, pieces)
 
 
 def expert_kernel(
     rows_ref, grad_ref, gate_ref, gate_up_ref, down_ref,
-    mixed_ref, normed_ref, gate_grad_ref, gate_up_out, down_out,
+    mixed_ref, normed_ref, gate_grad_ref, weights_out,
     gate_up_sum, down_sum,
 ):
     step = pl.program_id(0)
@@ -692,11 +707,14 @@
 
     @pl.when(step == pl.num_programs(0) - 1)
     def _():
-        gate_up_out[...] = gate_up_sum[...].astype(bf16)
-        down_out[...] = down_sum[...].astype(bf16)
-
-
-def expert_layer(rows, grad, gate, gate_up_weight, down_weight):
+        owners, _, columns = weights_out.shape
+        first = gate_up_sum.shape[0] // owners
+        weights_out[:, :first] = gate_up_sum[...].astype(bf16).reshape(owners, first, columns)
+        weights_out[:, first:] = down_sum[...].astype(bf16).reshape(owners, -1, columns)
+
+
+def expert_layer(n_dp, rows, grad, gate, gate_up_weight, down_weight):
+    packed = (n_dp, (gate_up_weight.shape[0] + down_weight.shape[0]) // n_dp, rows.shape[2])
     each, width = rows.shape[1:]
     shards = 2
     tile = pl.BlockSpec((shards, each, width), lambda i: (i, 0, 0))
@@ -708,8 +726,7 @@
             jax.ShapeDtypeStruct(rows.shape, bf16),
             jax.ShapeDtypeStruct(rows.shape, bf16),
             jax.ShapeDtypeStruct((GROUP, 8, each), f32),
-            jax.ShapeDtypeStruct(gate_up_weight.shape, bf16),
-            jax.ShapeDtypeStruct(down_weight.shape, bf16),
+            jax.ShapeDtypeStruct(packed, bf16),
         ],
         in_specs=[
             tile,
@@ -722,14 +739,14 @@
             tile,
             tile,
             pl.BlockSpec((shards, 8, each), lambda i: (i, 0, 0)),
-            whole(gate_up_weight.shape),
-            whole(down_weight.shape),
+            pl.BlockSpec(packed, lambda i: (0, 0, 0)),
         ],
         scratch_shapes=[
             pltpu.VMEM(gate_up_weight.shape, f32),
             pltpu.VMEM(down_weight.shape, f32),
         ],
         compiler_params=pltpu.CompilerParams(vmem_limit_bytes=56 * 2**20),
+        cost_estimate=pl.CostEstimate(flops=45000000000, bytes_accessed=2**24, transcendentals=0),
         name="expert_layer",
     )(rows, grad, gate, gate_up_weight, down_weight)
 
@@ -770,23 +787,29 @@
 def make_body(n_dp):
     groups_count = n_dp // RANKS
     inside = [[g * RANKS + j for j in range(RANKS)] for g in range(groups_count)]
-    between = [[g * RANKS + j for g in range(groups_count)] for j in range(RANKS)]
     half_experts = EXPERTS // 2
 
-    def expert_weight(shard, seq_rank):
-        mine = lax.dynamic_slice_in_dim(shard, seq_rank * half_experts, half_experts, axis=1)
-        mine = jnp.swapaxes(mine, 0, 1)
-        mine = lax.all_to_all(
-            mine, "dp", split_axis=0, concat_axis=0, tiled=True, axis_index_groups=inside
-        )
-        mine = mine.reshape(-1, shard.shape[2])
-        return lax.all_gather(mine, "dp", axis=0, tiled=True, axis_index_groups=between)
-
-    def expert_weight_grad(grad):
-        grad = lax.psum_scatter(
-            grad, "dp", scatter_dimension=0, tiled=True, axis_index_groups=between
-        )
-        return grad.reshape(RANKS, -1, grad.shape[1])
+    def to_group(value, k):
+        turn = [(d, (d + k * RANKS) % n_dp) for d in range(n_dp)]
+        return lax.ppermute(value, "dp", turn)
+
+    def expert_pieces(gate_up_shard, down_shard, seq_rank):
+        mine = [
+            jnp.swapaxes(lax.dynamic_slice_in_dim(w, seq_rank * half_experts, half_experts, axis=1), 0, 1)
+            for w in (gate_up_shard, down_shard)
+        ]
+        return lax.all_to_all(
+            jnp.concatenate(mine, 1), "dp", split_axis=0, concat_axis=0, tiled=True, axis_index_groups=inside
+        )
+
+    def expert_weights(mine, first):
+        home = lax.axis_index("dp") // RANKS
+        parts = [to_group(mine, k) for k in range(groups_count - 1, 0, -1)] + [mine]
+        ring = jnp.stack(parts + parts)
+        start = (2 * groups_count - 1 - home) % groups_count
+        whole = lax.dynamic_slice_in_dim(ring, start, groups_count, axis=0)
+        width = whole.shape[-1]
+        return whole[:, :, :first].reshape(-1, width), whole[:, :, first:].reshape(-1, width)
 
     def body(
         tokens, starts, routes, gain_one, query_key_value_weight, w_out,
@@ -812,11 +835,13 @@
                 [spare(w_router), spare(jnp.stack([gain_one, gain_two], 1))], 1
             ),
         )
+        mine, qkv_weight, out_weight, small = lax.optimization_barrier(
+            (expert_pieces(w_gate_up, w_down, seq_rank), qkv_weight, out_weight, small)
+        )
+        gate_up_weight, down_weight = expert_weights(mine, w_gate_up.shape[0])
         router_weight = small[:, :EXPERTS]
         gain_a = small[:, 128].astype(f32)
         gain_b = small[:, 129].astype(f32)
-        gate_up_weight = expert_weight(w_gate_up, seq_rank)
-        down_weight = expert_weight(w_down, seq_rank)
 
         token_rows = tokens[0].astype(f32)
         grad_output = cotangent[0].astype(f32)
@@ -861,12 +886,24 @@
         chosen = jnp.any(routes[0][:, :, None] == expert_ids[None, None, :], axis=1)
         gates = jax.nn.softmax(jnp.where(chosen, logits, -jnp.inf), axis=-1)
 
+        normed_two, gate_up_weight, down_weight = lax.optimization_barrier(
+            (normed_two, gate_up_weight, down_weight)
+        )
         rows_in, gates_all, grad_all = group_gather(1, normed_two, gates.T, cotangent[0])
         gate = lax.dynamic_slice_in_dim(gates_all, expert, 1, axis=1)
-        mixed_part, normed_part, gate_grad_part, gate_up_wgrad, down_wgrad = expert_layer(
-            rows_in, grad_all, gate, gate_up_weight, down_weight
-        )
-        mixed, normed_grad, gate_grad = group_reduce(2, mixed_part, normed_part, gate_grad_part)
+        mixed_part, normed_part, gate_grad_part, expert_wgrads = expert_layer(
+            n_dp, rows_in, grad_all, gate, gate_up_weight, down_weight
+        )
+        expert_wgrads = expert_wgrads.reshape((groups_count, RANKS) + expert_wgrads.shape[1:])
+        mixed, normed_grad, gate_grad, expert_far = group_reduce(
+            2, mixed_part, normed_part, gate_grad_part, expert_wgrads
+        )
+        expert_grads = lax.dynamic_index_in_dim(
+            expert_wgrads, lax.axis_index("dp") // RANKS, 0, keepdims=False
+        ).astype(f32)
+        for k in range(groups_count - 1):
+            expert_grads = expert_grads + expert_far[k].astype(f32)
+        expert_grads = expert_grads.astype(bf16)
         gate_grad = gate_grad[:, 0].T
 
         over_rows = (((0,), (0,)), ((), ()))
@@ -916,13 +953,14 @@
         little = jnp.concatenate(
             [spare(router_wgrad), spare(jnp.stack([gain_one_grad, gain_two_grad], 1))], 1
         )
-        qkv_shard, out_shard, little, gate_up_all, down_all = weights_reduce(
+        qkv_shard, out_shard, little, experts_all = weights_reduce(
             3,
             groups_count,
             (qkv_wgrad.astype(bf16), out_wgrad.astype(bf16), little),
-            (expert_weight_grad(gate_up_wgrad), expert_weight_grad(down_wgrad)),
-        )
-        stat_sums = lax.psum(stat_sums, "seq")
+            expert_grads,
+        )
+        stat_sums = stat_sums + lax.ppermute(stat_sums, "seq", [(0, 1), (1, 0)])
+        first = w_gate_up.shape[0]
         stream_rms = jnp.sqrt(stat_sums / (both * MODEL_WIDTH)).reshape(1, 2)
         return (
             output,
@@ -932,8 +970,8 @@
             out_shard.astype(f32),
             little[:, 129],
             little[:, :EXPERTS],
-            jnp.swapaxes(gate_up_all, 0, 1).astype(f32),
-            jnp.swapaxes(down_all, 0, 1).astype(f32),
+            jnp.swapaxes(experts_all[:, :first], 0, 1).astype(f32),
+            jnp.swapaxes(experts_all[:, first:], 0, 1).astype(f32),
             stream_rms,
         )
 

time: 555 us -> 559 us (level)
  waiting for transfers between devices: 44 us -> 63.9 us
  Pallas kernels: 351 us -> 370 us
  between operations: 14.9 us -> 2.27 us
  matrix products: 44.3 us -> 36.7 us
  local copies, waits for them, and re-layouts: 32.8 us -> 26.9 us
    ppermute x0 -> x2, waiting for transfers between devices: none -> 54.8 us  [the longest x1 54.8 us: to_group(): return lax.ppermute(value, 'dp', turn)]
    reduce_scatter x2 -> x0, waiting for transfers between devices: 34.3 us -> none  [expert_weight_grad(): lax.psum_scatter(grad, 'dp', scatter_dimension=0, tiled=True, axis_index_...]
    pallas_call x1, Pallas kernels: 71.4 us -> 104 us  [group_reduce(): pl.pallas_call(functools.partial(reduce_kernel, groups_count), out_shape=...]
    pallas_call x1, Pallas kernels: 90.2 us -> 71.4 us  [group_gather(): pl.pallas_call(functools.partial(gather_kernel, count), out_shape=[jax.Sh...]
    unnamed x88 -> x134, local copies, waits for them, and re-layouts: 21.9 us -> 15.4 us
  transfers between devices with their start and end apart: 9 -> 6, of which waited for: 2 -> 2; matrix products, arithmetic and copies ran while one was open for 15% -> 4% of each run, Pallas kernels for 25% -> 9%
where the time goes in v4:
time: 559 us; the launch traced here: 552 us
  Pallas kernels  370 us (66%)
  waiting for transfers between devices  63.9 us (11%)
  other arithmetic  37.7 us (7%)
  matrix products  36.7 us (7%)
  local copies, waits for them, and re-layouts  26.9 us (5%)
  starting transfers between devices  14.7 us (3%)
    pallas_call x1, Pallas kernels, group_reduce(): pl.pallas_call(functools.partial(reduce_kernel, groups_count), out_shape=...  104 us
    pallas_call x1, Pallas kernels, weights_reduce(): pl.pallas_call(functools.partial(weights_reduce_kernel, count, groups_cou...  94.2 us
    pallas_call x1, Pallas kernels, group_gather(): pl.pallas_call(functools.partial(gather_kernel, count), out_shape=[jax.Sh...  71.4 us
    ppermute x1, waiting for transfers between devices, to_group(): return lax.ppermute(value, 'dp', turn)  54.8 us
    pallas_call x1, Pallas kernels, weights_gather(): pl.pallas_call(functools.partial(weights_gather_kernel, count, groups_cou...  50 us
    pallas_call x1, Pallas kernels, expert_layer(): pl.pallas_call(expert_kernel, grid=(GROUP // shards,), out_shape=[jax.Sha...  49.9 us
    unnamed x134, local copies, waits for them, and re-layouts  15.4 us
  transfers between devices with their start and end apart: 6, of which 2 were waited for; matrix products, arithmetic and copies ran while one was open for 4% of the time, Pallas kernels for 9%

profile of v4, /device:TPU:0, one launch (start us, length us, event | category | flops | bytes accessed | tf_op | source)
XLA Modules:
  0.0 551.8 jit_solution(1235945486893767946)
XLA Ops:
  0.7 1.6 copy-done
  3.3 1.3 pad_maximum_fusion.1
  4.6 5.3 all-to-all-start
  9.9 4.8 collective-permute-start
  14.7 1.3 collective-permute-start.1
  16.2 0.6 fusion.64.refs_2_
  16.8 50.0 %weights_gather.1 = (bf16[2,8,64,2048]{3,2,1,0:T(8,128)(2,1)}, bf16[2,8,64,1024]{3,2,1,0:T(8,128)(2,1)}, bf16[2,8,64,256]{3,2,1,0:T(8,128)(2,1)}) custom-call(bf16[64,2048]{1,0:T(8,128)(2,1)} %refs_0_.1, bf16[64,1024]{1,0:T(8,128)(2,1)} %refs_1_.1, bf16[64,256]{1,0:T(8,128)(2,1)} %fusion.64.refs_2_), custom_call_target="tpu_custom_call" | custom-call | flops 44999999488 | bytes 16777216 | tf_op jit(solution)/shard_map/weights_gather/pallas_call | solution.py:435
  68.6 0.8 fusion.51
  69.3 1.1 convert_element_type.158
  70.7 1.0 copy.90
  71.7 0.8 slice_convert_fusion.2
  72.8 3.1 fusion.15
  75.9 1.3 fusion.17
  77.2 1.1 slice.137
  78.3 1.1 slice_negate_fusion.1
  79.4 1.6 copy.92
  81.0 1.1 slice_negate_fusion.2
  82.1 1.0 copy.91
  83.1 1.4 collective-permute-start.2
  84.5 1.5 fusion.48
  86.2 6.3 %fusion.82 = (f32[8,2,256]{2,1,0:T(2,128)S(1)}, f32[8,2,256,512]{2,3,1,0:T(8,128)}) fusion(pred[256,512]{0,1:T(8,128)(4,1)} %fusion.51, bf16[512,8,64,1]{0,2,3,1:T(8,128)(2,1)S(1)} %fusion.48, bf16[256,8,2,64]{0,3,2,1:T(8,128)(2,1)S(1)} %fusion.41), kind=kOutput, calls=%fused_computation.178 | convolution fusion | flops 276824576 | bytes 9584640 | tf_op jit(solution)/shard_map/sub | solution.py:876
  92.6 4.4 fusion.21
  97.1 0.8 multiply_reduce_fusion.5
  97.9 0.6 multiply_multiply_fusion.1
  99.4 0.6 fusion.79.refs_1_
  100.0 54.8 %collective-permute-done.2 = bf16[8,96,1024]{2,1,0:T(8,128)(2,1)} collective-permute-done((bf16[8,96,1024]{2,1,0:T(8,128)(2,1)}, bf16[8,96,1024]{2,1,0:T(8,128)(2,1)}, u32[]{:S(2)}, u32[]{:S(2)}) %collective-permute-start.2) | collective-permute-done | bytes 1572896 | tf_op jit(solution)/shard_map/ppermute | solution.py:794
  154.8 4.7 fusion.10
  159.5 1.5 slice.148
  161.0 1.0 slice.149
  162.1 71.4 %group_gather.1 = (bf16[16,256,1024]{2,1,0:T(8,128)(2,1)}, f32[16,16,256]{2,1,0:T(8,128)}, bf16[16,256,1024]{2,1,0:T(8,128)(2,1)}) custom-call(bf16[256,1024]{1,0:T(8,128)(2,1)} %copy-done.14, f32[16,256]{1,0:T(8,128)} %fusion.79.refs_1_, bf16[256,1024]{1,0:T(8,128)(2,1)} %bitcast.188), custom_call_target="tpu_custom_call" | custom-call | flops 60000002048 | bytes 16777216 | tf_op jit(solution)/shard_map/group_gather/pallas_call | solution.py:136
  233.5 1.5 constant_dynamic-slice_fusion.gate_ref
  235.0 49.9 %expert_layer.1 = (bf16[16,256,1024]{2,1,0:T(8,128)(2,1)}, bf16[16,256,1024]{2,1,0:T(8,128)(2,1)}, f32[16,8,256]{2,1,0:T(8,128)}, bf16[16,96,1024]{2,1,0:T(8,128)(2,1)}) custom-call(bf16[16,256,1024]{2,1,0:T(8,128)(2,1)} %get-tuple-element.43.rows_ref, bf16[16,256,1024]{2,1,0:T(8,128)(2,1)} %get-tuple-element.44.grad_ref, ...), custom_call_target="tpu_custom_call" | custom-call | flops 44999999488 | bytes 16777216 | tf_op jit(solution)/shard_map/expert_layer/pallas_call | solution.py:722
  284.9 0.9 copy-done.5
  285.8 104.2 %group_reduce.1 = (f32[256,1024]{1,0:T(8,128)S(1)}, f32[256,1024]{1,0:T(8,128)S(1)}, f32[16,8,256]{2,1,0:T(8,128)S(1)}, bf16[1,8,96,1024]{3,2,1,0:T(8,128)(2,1)S(1)}) custom-call(bf16[16,256,1024]{2,1,0:T(8,128)(2,1)} %get-tuple-element.48.mixed_ref, bf16[16,256,1024]{2,1,0:T(8,128)(2,1)} %get-tuple-element.49.normed_ref, f32[16,8,256]{2,1,0:T(8,128)S(1)} %copy-done.5, ...), custom_call_target="tpu_custom_call" | custom-call | flops 70000001024 | bytes 16777216 | tf_op jit(solution)/shard_map/group_reduce/pallas_call | solution.py:285
  390.2 1.5 multiply_reduce_fusion.2
  391.8 1.9 multiply_reduce_fusion.1
  393.7 0.7 convolution_convert_fusion.2
  395.1 4.7 fusion.1
  399.8 4.8 fusion.11
  404.6 4.5 fusion.3
  409.1 0.8 fusion.25
  410.2 1.4 fusion.20
  411.9 0.7 convolution_convert_fusion.1
  412.6 1.4 pad_maximum_fusion.11
  415.1 1.8 collective-permute-start.3
  417.2 1.8 fusion.19.refs_3_
  419.0 1.9 sqrt_bitcast_fusion
  420.9 9.1 %collective-permute-done.3 = bf16[256,1024]{0,1:T(8,128)(2,1)S(1)} collective-permute-done((bf16[256,1024]{0,1:T(8,128)(2,1)S(1)}, bf16[256,1024]{0,1:T(8,128)(2,1)S(1)}, u32[]{:S(2)}, u32[]{:S(2)}) %collective-permute-start.3) | collective-permute-done | bytes 524320 | tf_op jit(solution)/shard_map/ppermute | solution.py:938
  430.5 0.9 copy-done.30
  431.4 3.3 convolution_convert_fusion
  434.8 2.4 fusion.33
  437.2 1.1 select_maximum_fusion
  438.3 1.6 copy.101
  439.8 1.4 copy-done.4
  441.2 94.2 %weights_reduce.1 = (bf16[64,2048]{1,0:T(8,128)(2,1)S(1)}, bf16[64,1024]{1,0:T(8,128)(2,1)S(1)}, f32[64,256]{1,0:T(8,128)S(1)}, bf16[16,96,1024]{2,1,0:T(8,128)(2,1)}) custom-call(bf16[2,8,64,2048]{3,2,1,0:T(8,128)(2,1)} %bitcast.209, bf16[2,8,64,1024]{3,2,1,0:T(8,128)(2,1)S(1)} %bitcast.161, f32[2,8,64,256]{3,2,1,0:T(8,128)S(1)} %bitcast.162, ...), custom_call_target="tpu_custom_call" | custom-call | flops 80000000000 | bytes 16777216 | tf_op jit(solution)/shard_map/weights_reduce/pallas_call | solution.py:638
  535.4 2.1 convert_bitcast_fusion
  537.5 1.5 convert_bitcast_fusion.1
  539.0 0.7 slice_reduce_fusion
  539.7 4.4 copy.103
  544.1 2.5 copy.104
  546.7 0.8 convert_element_type.192
  547.5 0.7 convert_element_type.193
  548.2 0.7 copy.102
  548.9 2.5 fusion.49
  (177 shorter events, 7.6 us)
Async XLA Ops:
  0.6 1.6 copy-start
  0.7 2.3 copy-start.39
  3.3 6.6 %copy-start.10 = (bf16[1,256,1024]{2,1,0:T(8,128)(2,1)S(1)}, bf16[1,256,1024]{2,1,0:T(8,128)(2,1)}, u32[]{:S(2)}) copy-start(bf16[1,256,1024]{2,1,0:T(8,128)(2,1)} %param.11) | copy-start | bytes 1572868
  3.3 11.4 %copy-start.59 = (s32[1,256]{1,0:T(1,128)S(1)}, s32[1,256]{1,0:T(1,128)}, u32[]{:S(2)}) copy-start(s32[1,256]{1,0:T(1,128)} %param.12) | copy-start | bytes 3076
  3.3 12.7 %copy-start.60 = (bf16[64]{0:T(256)(128)(2,1)S(1)}, bf16[64]{0:T(256)(128)(2,1)}, u32[]{:S(2)}) copy-start(bf16[64]{0:T(256)(128)(2,1)} %param.17) | copy-start | bytes 388
  3.3 12.6 %copy-start.61 = (bf16[64]{0:T(256)(128)(2,1)S(1)}, bf16[64]{0:T(256)(128)(2,1)}, u32[]{:S(2)}) copy-start(bf16[64]{0:T(256)(128)(2,1)} %param.14) | copy-start | bytes 388
  3.3 12.8 %copy-start.58 = (bf16[64,16]{0,1:T(8,128)(2,1)S(1)}, bf16[64,16]{0,1:T(8,128)(2,1)}, u32[]{:S(2)}) copy-start(bf16[64,16]{0,1:T(8,128)(2,1)} %param.18) | copy-start | bytes 6148
  4.6 66.1 %all-to-all-start = ((bf16[8,96,1024]{2,1,0:T(8,128)(2,1)}), bf16[8,96,1024]{2,1,0:T(8,128)(2,1)}, u32[]{:S(2)}, u32[]{:S(2)}) async-start(bf16[8,96,1024]{2,1,0:T(8,128)(2,1)} %pad_maximum_fusion.1), calls=%async_computation | async-start | bytes 3145728 | tf_op jit(solution)/shard_map/all_to_all | solution.py:801
  9.9 59.5 %collective-permute-start = (bf16[256,1024]{1,0:T(8,128)(2,1)S(1)}, bf16[256,1024]{1,0:T(8,128)(2,1)}, u32[]{:S(2)}, u32[]{:S(2)}) collective-permute-start(bf16[256,1024]{1,0:T(8,128)(2,1)S(1)} %bitcast.167), channel_id=1, source_target_pairs={{0,16},{1,17},{2,18},{3,19},{4,20},{5,21},{6,22},{7,23},{8,24},{9,... | collective-permute-start | bytes 1572872 | tf_op jit(solution)/shard_map/ppermute | solution.py:826
  14.7 53.3 %collective-permute-start.1 = (s32[1,256]{1,0:T(1,128)S(1)}, s32[1,256]{1,0:T(1,128)S(1)}, u32[]{:S(2)}, u32[]{:S(2)}) collective-permute-start(s32[1,256]{1,0:T(1,128)S(1)} %copy-done.59), channel_id=1, source_target_pairs={{0,16},{1,17},{2,18},{3,19},{4,20},{5,21},{6,22},{7,23},{8,24},{9,... | collective-permute-start | bytes 3080 | tf_op jit(solution)/shard_map/ppermute | solution.py:827
  16.8 50.1 %copy-start.54 = (s32[1,256,8]{1,2,0:T(8,128)S(1)}, s32[1,256,8]{1,2,0:T(8,128)}, u32[]{:S(2)}) copy-start(s32[1,256,8]{1,2,0:T(8,128)} %param.13) | copy-start | bytes 24580
  67.0 32.0 %copy-start.40 = (pred[256,16]{0,1:T(8,128)(4,1)}, pred[256,16]{0,1:T(8,128)(4,1)S(1)}, u32[]{:S(2)}) copy-start(pred[256,16]{0,1:T(8,128)(4,1)S(1)} %fusion.59) | copy-start | bytes 12292
  67.2 3.6 copy-start.20
  68.5 17.5 %copy-start.27 = (f32[256,64]{0,1:T(8,128)}, f32[256,64]{0,1:T(8,128)S(1)}, u32[]{:S(2)}) copy-start(f32[256,64]{0,1:T(8,128)S(1)} %get-tuple-element.140) | copy-start | bytes 196612
  68.5 17.5 %copy-start.31 = (f32[256,64]{0,1:T(8,128)}, f32[256,64]{0,1:T(8,128)S(1)}, u32[]{:S(2)}) copy-start(f32[256,64]{0,1:T(8,128)S(1)} %get-tuple-element.141) | copy-start | bytes 196612
  72.5 3.3 copy-start.44
  72.5 26.0 %copy-start.42 = (f32[1024,1]{0,1:T(1,128)}, f32[1024,1]{0,1:T(1,128)S(1)}, u32[]{:S(2)}) copy-start(f32[1024,1]{0,1:T(1,128)S(1)} %get-tuple-element.120) | copy-start | bytes 12292
  72.6 3.3 copy-start.62
  72.8 4.4 copy-start.29
  83.1 2.9 copy-start.23
  83.1 2.9 copy-start.24
  83.1 71.8 %collective-permute-start.2 = (bf16[8,96,1024]{2,1,0:T(8,128)(2,1)}, bf16[8,96,1024]{2,1,0:T(8,128)(2,1)}, u32[]{:S(2)}, u32[]{:S(2)}) collective-permute-start(bf16[8,96,1024]{2,1,0:T(8,128)(2,1)} %all-to-all-done), channel_id=1, source_target_pairs={{0,8},{1,9},{2,10},{3,11},{4,12},{5,13},{6,14},{7,15},{8,0},{9,1},... | collective-permute-start | bytes 4718600 | tf_op jit(solution)/shard_map/ppermute | solution.py:794
  86.0 6.6 %copy-start.16 = (bf16[512,8,64,1]{0,2,3,1:T(8,128)(2,1)}, bf16[512,8,64,1]{0,2,3,1:T(8,128)(2,1)S(1)}, u32[]{:S(2)}) copy-start(bf16[512,8,64,1]{0,2,3,1:T(8,128)(2,1)S(1)} %fusion.48) | copy-start | bytes 1572868
  86.2 6.4 %copy-start.25 = (bf16[256,8,2,64]{0,3,2,1:T(8,128)(2,1)}, bf16[256,8,2,64]{0,3,2,1:T(8,128)(2,1)S(1)}, u32[]{:S(2)}) copy-start(bf16[256,8,2,64]{0,3,2,1:T(8,128)(2,1)S(1)} %fusion.41) | copy-start | bytes 1572868
  86.2 6.4 %copy-start.37 = (bf16[512,512]{0,1:T(8,128)(2,1)S(1)}, bf16[512,512]{0,1:T(8,128)(2,1)}, u32[]{:S(2)}) copy-start(bf16[512,512]{0,1:T(8,128)(2,1)} %copy.91) | copy-start | bytes 1572868
  92.6 4.4 copy-start.50
  92.6 4.4 copy-start.12
  97.0 2.3 copy-start.18
  97.0 2.0 copy-start.21
  98.5 56.3 %copy-start.52 = (f32[256]{0:T(256)}, f32[256]{0:T(256)S(1)}, u32[]{:S(2)}) copy-start(f32[256]{0:T(256)S(1)} %get-tuple-element.127) | copy-start | bytes 3076
  99.0 60.5 %copy-start.14 = (bf16[256,1024]{1,0:T(8,128)(2,1)}, bf16[256,1024]{1,0:T(8,128)(2,1)S(1)}, u32[]{:S(2)}) copy-start(bf16[256,1024]{1,0:T(8,128)(2,1)S(1)} %multiply_convert_fusion.1.refs_0_) | copy-start | bytes 1572868
  99.3 60.2 %copy-start.34 = (f32[256,16]{0,1:T(8,128)}, f32[256,16]{0,1:T(8,128)S(1)}, u32[]{:S(2)}) copy-start(f32[256,16]{0,1:T(8,128)S(1)} %get-tuple-element.133) | copy-start | bytes 49156
  99.3 60.2 %copy-start.46 = (f32[256]{0:T(256)}, f32[256]{0:T(256)S(1)}, u32[]{:S(2)}) copy-start(f32[256]{0:T(256)S(1)} %get-tuple-element.132) | copy-start | bytes 3076
  99.4 60.2 %copy-start.48 = (f32[256]{0:T(256)}, f32[256]{0:T(256)S(1)}, u32[]{:S(2)}) copy-start(f32[256]{0:T(256)S(1)} %fusion.67) | copy-start | bytes 3076
  285.8 104.3 %copy-start.35 = (f32[256,16]{0,1:T(8,128)S(1)}, f32[256,16]{0,1:T(8,128)}, u32[]{:S(2)}) copy-start(f32[256,16]{0,1:T(8,128)} %copy-done.34) | copy-start | bytes 49156
  285.8 104.3 %copy-start.41 = (pred[256,16]{0,1:T(8,128)(4,1)S(1)}, pred[256,16]{0,1:T(8,128)(4,1)}, u32[]{:S(2)}) copy-start(pred[256,16]{0,1:T(8,128)(4,1)} %copy-done.40) | copy-start | bytes 12292
  285.8 104.3 %copy-start.47 = (f32[256]{0:T(256)S(1)}, f32[256]{0:T(256)}, u32[]{:S(2)}) copy-start(f32[256]{0:T(256)} %copy-done.46) | copy-start | bytes 3076
  285.8 104.4 %copy-start.49 = (f32[256]{0:T(256)S(1)}, f32[256]{0:T(256)}, u32[]{:S(2)}) copy-start(f32[256]{0:T(256)} %copy-done.48) | copy-start | bytes 3076
  285.8 104.4 %copy-start.9 = (f32[256,1024]{1,0:T(8,128)S(1)}, f32[256,1024]{1,0:T(8,128)}, u32[]{:S(2)}) copy-start(f32[256,1024]{1,0:T(8,128)} %copy-done.8) | copy-start | bytes 3145732
  285.8 104.4 %copy-start.22 = (bf16[2,8,64,256]{3,2,1,0:T(8,128)(2,1)S(1)}, bf16[2,8,64,256]{3,2,1,0:T(8,128)(2,1)}, u32[]{:S(2)}) copy-start(bf16[2,8,64,256]{3,2,1,0:T(8,128)(2,1)} %get-tuple-element.37) | copy-start | bytes 1572868
  285.8 104.4 %copy-start.43 = (f32[1024,1]{0,1:T(1,128)S(1)}, f32[1024,1]{0,1:T(1,128)}, u32[]{:S(2)}) copy-start(f32[1024,1]{0,1:T(1,128)} %copy-done.42) | copy-start | bytes 12292
  285.8 104.4 %copy-start.53 = (f32[256]{0:T(256)S(1)}, f32[256]{0:T(256)}, u32[]{:S(2)}) copy-start(f32[256]{0:T(256)} %copy-done.52) | copy-start | bytes 3076
  390.1 3.6 copy-start.2
  390.1 1.7 copy-start.36
  390.1 1.7 copy-start.57
  391.8 1.9 copy-start.13
  393.7 18.2 %copy-start.6 = (f32[256,1024]{1,0:T(8,128)}, f32[256,1024]{1,0:T(8,128)S(1)}, u32[]{:S(2)}) copy-start(f32[256,1024]{1,0:T(8,128)S(1)} %get-tuple-element.109) | copy-start | bytes 3145732
  393.7 1.4 copy-start.38
  404.6 4.5 copy-start.17
  410.2 1.4 copy-start.15
  410.2 1.7 copy-start.19
  411.6 2.6 copy-start.28
  414.0 5.0 collective-permute-start.4
  414.8 2.1 copy-start.3
  414.8 2.4 copy-start.33
  415.1 14.9 %collective-permute-start.3 = (bf16[256,1024]{0,1:T(8,128)(2,1)S(1)}, bf16[256,1024]{0,1:T(8,128)(2,1)S(1)}, u32[]{:S(2)}, u32[]{:S(2)}) collective-permute-start(bf16[256,1024]{0,1:T(8,128)(2,1)S(1)} %fusion.37), channel_id=1, source_target_pairs={{16,0},{17,1},{18,2},{19,3},{20,4},{21,5},{22,6},{23,7},{24,8},{25... | collective-permute-start | bytes 1572872 | tf_op jit(solution)/shard_map/ppermute | solution.py:938
  431.4 3.3 copy-start.11
  431.4 3.3 copy-start.45
  431.4 3.3 copy-start.56
  431.4 3.3 copy-start.63
  439.8 1.4 copy-start.4
  544.1 4.8 copy-start.7
  544.1 4.8 copy-start.55
  544.1 7.2 %copy-start.1 = (bf16[64,16,1024]{2,1,0:T(8,128)(2,1)S(1)}, bf16[64,16,1024]{2,1,0:T(8,128)(2,1)}, u32[]{:S(2)}) copy-start(bf16[64,16,1024]{2,1,0:T(8,128)(2,1)} %param.19) | copy-start | bytes 6291460
  (6 other events, 6.0 us)

commit v5 on v4

--- a/solution.py
+++ b/solution.py
@@ -26,6 +26,8 @@
 MESH = pl.DeviceIdType.MESH
 
 LINKS = ((8, 4, 2), (4, 2, 8), (2, 8, 4))
+TOKEN_LINKS = ((4, 8, 2), (4, 2, 8))
+TOKEN_SUMS = ((8, 2, 4), (2, 8, 4))
 
 
 def flip(value, bit):
@@ -47,9 +49,8 @@
 
 
 def row_parts(rows):
-    first = (rows // 3 + 15) // 16 * 16
-    second = (rows - first) // 2 // 16 * 16
-    return ((0, first), (first, second), (first + second, rows - first - second))
+    first = (rows // 2 + 15) // 16 * 16
+    return ((0, first), (first, rows - first))
 
 
 def my_place():
@@ -101,11 +102,11 @@
     started = []
     live = {}
     for step in range(4):
-        for p in range(3):
+        for p in range(2):
             for a in range(count):
                 if parts[a][p][1] == 0:
                     continue
-                order = LINKS[p]
+                order = TOKEN_LINKS[p]
                 if step > 0:
                     for copy in live.pop((a, p)):
                         copy.wait_recv()
@@ -220,7 +221,7 @@
     def chip_of(mask):
         return flip_mask(rank, mask) // 2
 
-    for p in range(3):
+    for p in range(2):
         for t in range(2):
             rows = pl.ds(*parts[p])
             for c in range(8):
@@ -242,9 +243,9 @@
         copy.wait()
     got = (got1, got2, got3)
     for stage in range(4):
-        for p in range(3):
+        for p in range(2):
             for t in range(2):
-                order = LINKS[p]
+                order = TOKEN_SUMS[p]
                 rows = pl.ds(*parts[p])
                 for copy in live.pop((t, p)):
                     copy.wait_recv()
@@ -470,12 +471,10 @@
 
 def weights_reduce_kernel(count, groups_count, *refs):
     ins = refs[:count]
-    pieces = refs[count]
-    outs = refs[count + 1 : 2 * count + 1]
-    whole = refs[2 * count + 1]
-    rest = refs[2 * count + 2 :]
+    outs = refs[count : 2 * count]
+    rest = refs[2 * count :]
     total, got0, got1, got2, got3, far_got = [rest[i * count : (i + 1) * count] for i in range(6)]
-    sems, far_sems, seq_sems, piece_sems, local, own_sems = rest[6 * count :]
+    sems, far_sems, seq_sems, local = rest[6 * count :]
     rank, peer = my_place()
     chip, core = rank // 2, rank % 2
     home, far = other_groups(groups_count)
@@ -496,15 +495,10 @@
             )
             copy.start()
             loads.append(copy)
-    keep = pltpu.make_async_copy(pieces.at[rank % RANKS], whole.at[rank], own_sems)
-    keep.start()
     barrier = pltpu.get_barrier_semaphore()
-    everyone = [
-        {"seq": 1 - seq if mask & 8 else seq, "dp": flip_mask(dp, mask & 7)} for mask in range(1, 16)
-    ]
-    for there in everyone + far:
+    for there in [peer(bit) for bit in (1, 2, 4, 8)] + far:
         pl.semaphore_signal(barrier, inc=1, device_id=there, device_id_type=MESH)
-    pl.semaphore_wait(barrier, 15 + len(far))
+    pl.semaphore_wait(barrier, 4 + len(far))
 
     started = []
     live = {}
@@ -536,18 +530,6 @@
                         got0[a].at[c, :, :, columns],
                         1,
                     )
-    arrivals = []
-    for mask, there in zip(range(1, 16), everyone):
-        copy = pltpu.make_async_remote_copy(
-            src_ref=pieces.at[flip_mask(rank, mask) % RANKS],
-            dst_ref=whole.at[rank],
-            send_sem=piece_sems.at[0, mask],
-            recv_sem=piece_sems.at[1, mask],
-            device_id=there,
-            device_id_type=MESH,
-        )
-        copy.start()
-        arrivals.append(copy)
     for copy in loads:
         copy.wait()
     got = (got1, got2, got3)
@@ -611,14 +593,13 @@
         )
         copy.start()
         last.append(copy)
-    for copy in last + arrivals:
+    for copy in last:
         copy.wait()
     for copy in started:
         copy.wait_send()
-    keep.wait()
-
-
-def weights_reduce(collective_id, groups_count, arrays, pieces):
+
+
+def weights_reduce(collective_id, groups_count, arrays):
     count = len(arrays)
     views = [a.reshape(groups_count, RANKS, -1, a.shape[1]) for a in arrays]
     rows = views[0].shape[2]
@@ -637,25 +618,22 @@
     any_space = pl.BlockSpec(memory_space=pl.ANY)
     return pl.pallas_call(
         functools.partial(weights_reduce_kernel, count, groups_count),
-        out_shape=[jax.ShapeDtypeStruct((rows, a.shape[1]), a.dtype) for a in arrays]
-        + [jax.ShapeDtypeStruct((EXPERTS,) + pieces.shape[1:], pieces.dtype)],
-        in_specs=[any_space] * count + [vmem],
-        out_specs=[vmem] * count + [any_space],
+        out_shape=[jax.ShapeDtypeStruct((rows, a.shape[1]), a.dtype) for a in arrays],
+        in_specs=[any_space] * count,
+        out_specs=[vmem] * count,
         scratch_shapes=buffers(8) + buffers(8) + buffers(4) + buffers(2) + buffers(1) + far_buffers
         + [
             dma((2, count, 3, 4, 8)),
             dma((2, max(groups_count - 1, 1), count)),
             dma((2, count)),
-            dma((2, 16)),
             dma((count, 8)),
-            dma(()),
         ],
         compiler_params=pltpu.CompilerParams(
             collective_id=collective_id, has_side_effects=True, vmem_limit_bytes=48 * 2**20
         ),
         cost_estimate=pl.CostEstimate(flops=80000000000, bytes_accessed=2**24, transcendentals=0),
         name="weights_reduce",
-    )(*views, pieces)
+    )(*views)
 
 
 def expert_kernel(
@@ -802,14 +780,13 @@
             jnp.concatenate(mine, 1), "dp", split_axis=0, concat_axis=0, tiled=True, axis_index_groups=inside
         )
 
-    def expert_weights(mine, first):
+    def from_groups(mine):
         home = lax.axis_index("dp") // RANKS
         parts = [to_group(mine, k) for k in range(groups_count - 1, 0, -1)] + [mine]
         ring = jnp.stack(parts + parts)
         start = (2 * groups_count - 1 - home) % groups_count
         whole = lax.dynamic_slice_in_dim(ring, start, groups_count, axis=0)
-        width = whole.shape[-1]
-        return whole[:, :, :first].reshape(-1, width), whole[:, :, first:].reshape(-1, width)
+        return whole.reshape(-1, whole.shape[-1])
 
     def body(
         tokens, starts, routes, gain_one, query_key_value_weight, w_out,
@@ -838,7 +815,9 @@
         mine, qkv_weight, out_weight, small = lax.optimization_barrier(
             (expert_pieces(w_gate_up, w_down, seq_rank), qkv_weight, out_weight, small)
         )
-        gate_up_weight, down_weight = expert_weights(mine, w_gate_up.shape[0])
+        first = w_gate_up.shape[0]
+        gate_up_mine = mine[:, :first]
+        down_weight = from_groups(mine[:, first:])
         router_weight = small[:, :EXPERTS]
         gain_a = small[:, 128].astype(f32)
         gain_b = small[:, 129].astype(f32)
@@ -886,9 +865,10 @@
         chosen = jnp.any(routes[0][:, :, None] == expert_ids[None, None, :], axis=1)
         gates = jax.nn.softmax(jnp.where(chosen, logits, -jnp.inf), axis=-1)
 
-        normed_two, gate_up_weight, down_weight = lax.optimization_barrier(
-            (normed_two, gate_up_weight, down_weight)
-        )
+        normed_two, gate_up_mine, down_weight = lax.optimization_barrier(
+            (normed_two, gate_up_mine, down_weight)
+        )
+        gate_up_weight = from_groups(gate_up_mine)
         rows_in, gates_all, grad_all = group_gather(1, normed_two, gates.T, cotangent[0])
         gate = lax.dynamic_slice_in_dim(gates_all, expert, 1, axis=1)
         mixed_part, normed_part, gate_grad_part, expert_wgrads = expert_layer(
@@ -903,7 +883,10 @@
         ).astype(f32)
         for k in range(groups_count - 1):
             expert_grads = expert_grads + expert_far[k].astype(f32)
-        expert_grads = expert_grads.astype(bf16)
+        expert_grads = lax.all_to_all(
+            expert_grads.astype(bf16), "dp", split_axis=0, concat_axis=0, tiled=True,
+            axis_index_groups=inside,
+        )
         gate_grad = gate_grad[:, 0].T
 
         over_rows = (((0,), (0,)), ((), ()))
@@ -953,12 +936,15 @@
         little = jnp.concatenate(
             [spare(router_wgrad), spare(jnp.stack([gain_one_grad, gain_two_grad], 1))], 1
         )
-        qkv_shard, out_shard, little, experts_all = weights_reduce(
+        qkv_shard, out_shard, little = weights_reduce(
             3,
             groups_count,
             (qkv_wgrad.astype(bf16), out_wgrad.astype(bf16), little),
-            expert_grads,
-        )
+        )
+        ours, theirs = expert_grads, lax.ppermute(expert_grads, "seq", [(0, 1), (1, 0)])
+        experts_all = jnp.where(
+            seq_rank == 0, jnp.stack([ours, theirs]), jnp.stack([theirs, ours])
+        ).reshape((EXPERTS,) + ours.shape[1:])
         stat_sums = stat_sums + lax.ppermute(stat_sums, "seq", [(0, 1), (1, 0)])
         first = w_gate_up.shape[0]
         stream_rms = jnp.sqrt(stat_sums / (both * MODEL_WIDTH)).reshape(1, 2)

time: 559 us -> 568 us (1.016)
  waiting for transfers between devices: 63.9 us -> 16.1 us
  Pallas kernels: 370 us -> 413 us
  other arithmetic: 37.7 us -> 45.2 us
    ppermute x1 -> x2, waiting for transfers between devices: 54.8 us -> 4.27 us  [to_group(): return lax.ppermute(value, 'dp', turn)]
    pallas_call x1, Pallas kernels: 71.4 us -> 117 us  [group_gather(): pl.pallas_call(functools.partial(gather_kernel, count), out_shape=[jax.Sh...]
    unnamed x134 -> x136, local copies, waits for them, and re-layouts: 15.4 us -> 8.8 us
    pallas_call x1, Pallas kernels: 94.2 us -> 87.9 us  [weights_reduce(): pl.pallas_call(functools.partial(weights_reduce_kernel, count, groups_cou...]
  transfers between devices with their start and end apart: 6 -> 9, of which waited for: 2 -> 2; matrix products, arithmetic and copies ran while one was open for 4% -> 8% of each run, Pallas kernels for 9% -> 46%
where the time goes in v5:
time: 568 us; the launch traced here: 560 us
  Pallas kernels  413 us (73%)
  other arithmetic  45.2 us (8%)
  matrix products  41.4 us (7%)
  local copies, waits for them, and re-layouts  23.3 us (4%)
  starting transfers between devices  19.3 us (3%)
  waiting for transfers between devices  16.1 us (3%)
    pallas_call x1, Pallas kernels, group_gather(): pl.pallas_call(functools.partial(gather_kernel, count), out_shape=[jax.Sh...  117 us
    pallas_call x1, Pallas kernels, group_reduce(): pl.pallas_call(functools.partial(reduce_kernel, groups_count), out_shape=...  107 us
    pallas_call x1, Pallas kernels, weights_reduce(): pl.pallas_call(functools.partial(weights_reduce_kernel, count, groups_cou...  87.9 us
    pallas_call x1, Pallas kernels, expert_layer(): pl.pallas_call(expert_kernel, grid=(GROUP // shards,), out_shape=[jax.Sha...  50.1 us
    pallas_call x1, Pallas kernels, weights_gather(): pl.pallas_call(functools.partial(weights_gather_kernel, count, groups_cou...  50 us
    ppermute x1, waiting for transfers between devices, body(): kv_back = lax.ppermute(kv_grad[:count].astype(bf16), 'seq', back_pair)  11.9 us
  transfers between devices with their start and end apart: 9, of which 2 were waited for; matrix products, arithmetic and copies ran while one was open for 8% of the time, Pallas kernels for 46%

profile of v5, /device:TPU:0, one launch (start us, length us, event | category | flops | bytes accessed | tf_op | source)
XLA Modules:
  0.0 560.1 jit_solution(1909834700788287372)
XLA Ops:
  0.7 1.6 copy-done
  3.3 1.3 pad_maximum_fusion.1
  4.6 5.3 all-to-all-start
  9.9 4.8 collective-permute-start
  14.6 1.3 collective-permute-start.1
  16.2 0.6 fusion.67.refs_2_
  16.8 50.0 %weights_gather.1 = (bf16[2,8,64,2048]{3,2,1,0:T(8,128)(2,1)}, bf16[2,8,64,1024]{3,2,1,0:T(8,128)(2,1)}, bf16[2,8,64,256]{3,2,1,0:T(8,128)(2,1)}) custom-call(bf16[64,2048]{1,0:T(8,128)(2,1)} %refs_0_.1, bf16[64,1024]{1,0:T(8,128)(2,1)} %refs_1_.1, bf16[64,256]{1,0:T(8,128)(2,1)} %fusion.67.refs_2_), custom_call_target="tpu_custom_call" | custom-call | flops 44999999488 | bytes 16777216 | tf_op jit(solution)/shard_map/weights_gather/pallas_call | solution.py:436
  68.5 0.8 fusion.54
  69.3 1.1 convert_element_type.159
  70.7 1.0 copy.90
  71.7 0.8 slice_convert_fusion.2
  72.8 3.1 fusion.15
  75.9 1.3 fusion.17
  77.2 1.1 slice.137
  78.3 2.2 slice_bitcast_fusion
  80.5 2.3 slice.117
  82.7 1.4 collective-permute-start.2
  84.1 1.1 slice_negate_fusion.1
  85.2 1.6 copy.92
  86.8 1.1 slice_negate_fusion.2
  87.9 1.0 copy.91
  88.9 1.6 fusion.51
  90.8 6.3 %fusion.85 = (f32[8,2,256]{2,1,0:T(2,128)S(1)}, f32[8,2,256,512]{2,3,1,0:T(8,128)}) fusion(pred[256,512]{0,1:T(8,128)(4,1)} %fusion.54, bf16[512,8,64,1]{0,2,3,1:T(8,128)(2,1)S(1)} %fusion.51, bf16[256,8,2,64]{0,3,2,1:T(8,128)(2,1)S(1)} %fusion.44), kind=kOutput, calls=%fused_computation.187 | convolution fusion | flops 276824576 | bytes 9584640 | tf_op jit(solution)/shard_map/sub | solution.py:855
  97.1 4.4 fusion.21
  101.6 0.8 multiply_reduce_fusion.5
  105.3 4.3 collective-permute-done.2
  109.6 2.7 fusion.39
  112.3 117.3 %group_gather.1 = (bf16[16,256,1024]{2,1,0:T(8,128)(2,1)}, f32[16,16,256]{2,1,0:T(8,128)}, bf16[16,256,1024]{2,1,0:T(8,128)(2,1)}) custom-call(bf16[256,1024]{1,0:T(8,128)(2,1)} %copy-done.12, f32[16,256]{1,0:T(8,128)} %fusion.82.refs_1_, bf16[256,1024]{1,0:T(8,128)(2,1)} %bitcast.197), custom_call_target="tpu_custom_call" | custom-call | flops 60000002048 | bytes 16777216 | tf_op jit(solution)/shard_map/group_gather/pallas_call | solution.py:137
  229.6 1.5 constant_dynamic-slice_fusion.gate_ref
  231.1 4.0 fusion.10
  235.1 50.1 %expert_layer.1 = (bf16[16,256,1024]{2,1,0:T(8,128)(2,1)}, bf16[16,256,1024]{2,1,0:T(8,128)(2,1)}, f32[16,8,256]{2,1,0:T(8,128)}, bf16[16,96,1024]{2,1,0:T(8,128)(2,1)}) custom-call(bf16[16,256,1024]{2,1,0:T(8,128)(2,1)} %get-tuple-element.42.rows_ref, bf16[16,256,1024]{2,1,0:T(8,128)(2,1)} %get-tuple-element.43.grad_ref, ...), custom_call_target="tpu_custom_call" | custom-call | flops 44999999488 | bytes 16777216 | tf_op jit(solution)/shard_map/expert_layer/pallas_call | solution.py:700
  285.2 0.9 copy-done.2
  286.2 107.2 %group_reduce.1 = (f32[256,1024]{1,0:T(8,128)S(1)}, f32[256,1024]{1,0:T(8,128)S(1)}, f32[16,8,256]{2,1,0:T(8,128)S(1)}, bf16[1,8,96,1024]{3,2,1,0:T(8,128)(2,1)S(1)}) custom-call(bf16[16,256,1024]{2,1,0:T(8,128)(2,1)} %get-tuple-element.47.mixed_ref, bf16[16,256,1024]{2,1,0:T(8,128)(2,1)} %get-tuple-element.48.normed_ref, f32[16,8,256]{2,1,0:T(8,128)S(1)} %copy-done.2, ...), custom_call_target="tpu_custom_call" | custom-call | flops 70000001024 | bytes 16777216 | tf_op jit(solution)/shard_map/group_reduce/pallas_call | solution.py:286
  393.5 1.5 multiply_reduce_fusion.2
  395.1 1.9 multiply_reduce_fusion.1
  397.0 0.7 convolution_convert_fusion.2
  397.7 1.0 copy.97
  398.8 5.1 fusion.1
  403.9 5.8 %fusion.11 = f32[8,64,512,1]{2,1,3,0:T(8,128)} fusion(bf16[256,8,2,64]{0,3,2,1:T(8,128)(2,1)S(1)} %bitcast.201, f32[8,2,256,512]{2,3,1,0:T(8,128)} %get-tuple-element.129, f32[8,2,256]{2,1,0:T(2,128)S(1)} %copy-done.53), kind=kOutput, calls=%fused_computation.32 | convolution fusion | flops 272629760 | bytes 9977856 | tf_op jit(solution)/shard_map/grqk,qgrd->kgd/dot_general | solution.py:917
  409.6 4.5 fusion.3
  414.2 1.7 fusion.25
  415.9 2.3 fusion.20
  418.6 1.4 pad_maximum_fusion.11
  420.5 1.8 fusion.19
  422.3 4.4 all-to-all-start.1
  428.5 1.6 collective-permute-start.4
  430.2 0.7 convolution_convert_fusion.1
  430.9 1.9 sqrt_bitcast_fusion
  432.8 11.9 %collective-permute-done.4 = bf16[256,1024]{0,1:T(8,128)(2,1)S(1)} collective-permute-done((bf16[256,1024]{0,1:T(8,128)(2,1)S(1)}, bf16[256,1024]{0,1:T(8,128)(2,1)S(1)}, u32[]{:S(2)}, u32[]{:S(2)}) %collective-permute-start.4) | collective-permute-done | bytes 524320 | tf_op jit(solution)/shard_map/ppermute | solution.py:921
  445.2 0.7 copy-done.9
  445.9 1.4 copy-done.65
  447.3 2.4 fusion.33
  449.7 1.1 select_maximum_fusion
  450.8 1.6 copy.101
  452.4 4.6 convolution_convert_fusion
  457.0 87.9 %weights_reduce.1 = (bf16[64,2048]{1,0:T(8,128)(2,1)S(1)}, bf16[64,1024]{1,0:T(8,128)(2,1)S(1)}, f32[64,256]{1,0:T(8,128)S(1)}) custom-call(bf16[2,8,64,2048]{3,2,1,0:T(8,128)(2,1)} %bitcast.218, bf16[2,8,64,1024]{3,2,1,0:T(8,128)(2,1)S(1)} %bitcast.167, f32[2,8,64,256]{3,2,1,0:T(8,128)S(1)} %bitcast.168), custom_call_target="tpu_custom_call" | custom-call | flops 80000000000 | bytes 16777216 | tf_op jit(solution)/shard_map/weights_reduce/pallas_call | solution.py:619
  544.9 0.8 convert_element_type.189
  545.8 0.7 convert_element_type.190
  546.5 0.7 copy.104
  547.2 0.7 slice_reduce_fusion
  547.9 2.8 fusion.52
  550.6 3.4 maximum_select_fusion
  554.4 3.2 convert_bitcast_fusion
  557.7 1.9 convert_bitcast_fusion.1
  (189 shorter events, 9.9 us)
Async XLA Ops:
  0.6 1.6 copy-start
  0.7 2.3 copy-start.41
  3.3 6.6 %copy-start.8 = (bf16[1,256,1024]{2,1,0:T(8,128)(2,1)S(1)}, bf16[1,256,1024]{2,1,0:T(8,128)(2,1)}, u32[]{:S(2)}) copy-start(bf16[1,256,1024]{2,1,0:T(8,128)(2,1)} %param.11) | copy-start | bytes 1572868
  3.3 11.3 %copy-start.61 = (s32[1,256]{1,0:T(1,128)S(1)}, s32[1,256]{1,0:T(1,128)}, u32[]{:S(2)}) copy-start(s32[1,256]{1,0:T(1,128)} %param.12) | copy-start | bytes 3076
  3.3 12.6 %copy-start.62 = (bf16[64]{0:T(256)(128)(2,1)S(1)}, bf16[64]{0:T(256)(128)(2,1)}, u32[]{:S(2)}) copy-start(bf16[64]{0:T(256)(128)(2,1)} %param.17) | copy-start | bytes 388
  3.3 12.6 %copy-start.63 = (bf16[64]{0:T(256)(128)(2,1)S(1)}, bf16[64]{0:T(256)(128)(2,1)}, u32[]{:S(2)}) copy-start(bf16[64]{0:T(256)(128)(2,1)} %param.14) | copy-start | bytes 388
  3.3 12.7 %copy-start.60 = (bf16[64,16]{0,1:T(8,128)(2,1)S(1)}, bf16[64,16]{0,1:T(8,128)(2,1)}, u32[]{:S(2)}) copy-start(bf16[64,16]{0,1:T(8,128)(2,1)} %param.18) | copy-start | bytes 6148
  4.6 66.1 %all-to-all-start = ((bf16[8,96,1024]{2,1,0:T(8,128)(2,1)}), bf16[8,96,1024]{2,1,0:T(8,128)(2,1)}, u32[]{:S(2)}, u32[]{:S(2)}) async-start(bf16[8,96,1024]{2,1,0:T(8,128)(2,1)} %pad_maximum_fusion.1), calls=%async_computation | async-start | bytes 3145728 | tf_op jit(solution)/shard_map/all_to_all | solution.py:779
  9.9 59.4 %collective-permute-start = (bf16[256,1024]{1,0:T(8,128)(2,1)S(1)}, bf16[256,1024]{1,0:T(8,128)(2,1)}, u32[]{:S(2)}, u32[]{:S(2)}) collective-permute-start(bf16[256,1024]{1,0:T(8,128)(2,1)S(1)} %bitcast.175), channel_id=1, source_target_pairs={{0,16},{1,17},{2,18},{3,19},{4,20},{5,21},{6,22},{7,23},{8,24},{9,... | collective-permute-start | bytes 1572872 | tf_op jit(solution)/shard_map/ppermute | solution.py:803
  14.6 53.3 %collective-permute-start.1 = (s32[1,256]{1,0:T(1,128)S(1)}, s32[1,256]{1,0:T(1,128)S(1)}, u32[]{:S(2)}, u32[]{:S(2)}) collective-permute-start(s32[1,256]{1,0:T(1,128)S(1)} %copy-done.61), channel_id=1, source_target_pairs={{0,16},{1,17},{2,18},{3,19},{4,20},{5,21},{6,22},{7,23},{8,24},{9,... | collective-permute-start | bytes 3080 | tf_op jit(solution)/shard_map/ppermute | solution.py:804
  16.8 50.1 %copy-start.56 = (s32[1,256,8]{1,2,0:T(8,128)S(1)}, s32[1,256,8]{1,2,0:T(8,128)}, u32[]{:S(2)}) copy-start(s32[1,256,8]{1,2,0:T(8,128)} %param.13) | copy-start | bytes 24580
  66.9 36.8 %copy-start.42 = (pred[256,16]{0,1:T(8,128)(4,1)}, pred[256,16]{0,1:T(8,128)(4,1)S(1)}, u32[]{:S(2)}) copy-start(pred[256,16]{0,1:T(8,128)(4,1)S(1)} %fusion.62) | copy-start | bytes 12292
  67.1 3.6 copy-start.21
  68.5 22.0 %copy-start.28 = (f32[256,64]{0,1:T(8,128)}, f32[256,64]{0,1:T(8,128)S(1)}, u32[]{:S(2)}) copy-start(f32[256,64]{0,1:T(8,128)S(1)} %get-tuple-element.140) | copy-start | bytes 196612
  68.5 22.0 %copy-start.31 = (f32[256,64]{0,1:T(8,128)}, f32[256,64]{0,1:T(8,128)S(1)}, u32[]{:S(2)}) copy-start(f32[256,64]{0,1:T(8,128)S(1)} %get-tuple-element.141) | copy-start | bytes 196612
  72.5 3.3 copy-start.46
  72.5 30.5 %copy-start.44 = (f32[1024,1]{0,1:T(1,128)}, f32[1024,1]{0,1:T(1,128)S(1)}, u32[]{:S(2)}) copy-start(f32[1024,1]{0,1:T(1,128)S(1)} %get-tuple-element.120) | copy-start | bytes 12292
  72.5 3.3 copy-start.64
  72.8 4.4 copy-start.30
  82.7 26.8 %collective-permute-start.2 = (bf16[8,32,1024]{2,1,0:T(8,128)(2,1)}, bf16[8,32,1024]{2,1,0:T(8,128)(2,1)}, u32[]{:S(2)}, u32[]{:S(2)}) collective-permute-start(bf16[8,32,1024]{2,1,0:T(8,128)(2,1)} %get-tuple-element.106), channel_id=1, source_target_pairs={{0,8},{1,9},{2,10},{3,11},{4,12},{5,13},{6,14},{7,15},{8,0},{9,1},... | collective-permute-start | bytes 1572872 | tf_op jit(solution)/shard_map/ppermute | solution.py:772
  88.9 1.6 copy-start.24
  88.9 1.6 copy-start.25
  90.5 6.6 %copy-start.16 = (bf16[512,8,64,1]{0,2,3,1:T(8,128)(2,1)}, bf16[512,8,64,1]{0,2,3,1:T(8,128)(2,1)S(1)}, u32[]{:S(2)}) copy-start(bf16[512,8,64,1]{0,2,3,1:T(8,128)(2,1)S(1)} %fusion.51) | copy-start | bytes 1572868
  90.7 6.4 %copy-start.26 = (bf16[256,8,2,64]{0,3,2,1:T(8,128)(2,1)}, bf16[256,8,2,64]{0,3,2,1:T(8,128)(2,1)S(1)}, u32[]{:S(2)}) copy-start(bf16[256,8,2,64]{0,3,2,1:T(8,128)(2,1)S(1)} %fusion.44) | copy-start | bytes 1572868
  90.7 6.4 %copy-start.37 = (bf16[512,512]{0,1:T(8,128)(2,1)S(1)}, bf16[512,512]{0,1:T(8,128)(2,1)}, u32[]{:S(2)}) copy-start(bf16[512,512]{0,1:T(8,128)(2,1)} %copy.91) | copy-start | bytes 1572868
  97.1 4.4 copy-start.52
  97.1 4.4 copy-start.10
  101.5 2.2 copy-start.22
  101.6 8.0 %copy-start.20 = (bf16[1,8,32,1024]{3,2,1,0:T(8,128)(2,1)S(1)}, bf16[1,8,32,1024]{3,2,1,0:T(8,128)(2,1)}, u32[]{:S(2)}) copy-start(bf16[1,8,32,1024]{3,2,1,0:T(8,128)(2,1)} %get-tuple-element.105) | copy-start | bytes 1572868
  102.4 127.2 %copy-start.4 = (f32[256,1024]{1,0:T(8,128)}, f32[256,1024]{1,0:T(8,128)S(1)}, u32[]{:S(2)}) copy-start(f32[256,1024]{1,0:T(8,128)S(1)} %get-tuple-element.131) | copy-start | bytes 3145732
  102.4 9.9 %copy-start.14 = (bf16[8,64,1024]{2,1,0:T(8,128)(2,1)S(1)}, bf16[8,64,1024]{2,1,0:T(8,128)(2,1)}, u32[]{:S(2)}) copy-start(bf16[8,64,1024]{2,1,0:T(8,128)(2,1)} %slice.117) | copy-start | bytes 3145732
  103.8 8.5 %copy-start.12 = (bf16[256,1024]{1,0:T(8,128)(2,1)}, bf16[256,1024]{1,0:T(8,128)(2,1)S(1)}, u32[]{:S(2)}) copy-start(bf16[256,1024]{1,0:T(8,128)(2,1)S(1)} %multiply_convert_fusion.1.refs_0_) | copy-start | bytes 1572868
  104.1 125.5 %copy-start.48 = (f32[256]{0:T(256)}, f32[256]{0:T(256)S(1)}, u32[]{:S(2)}) copy-start(f32[256]{0:T(256)S(1)} %get-tuple-element.132) | copy-start | bytes 3076
  112.3 118.8 %collective-permute-start.3 = (bf16[8,64,1024]{2,1,0:T(8,128)(2,1)S(1)}, bf16[8,64,1024]{2,1,0:T(8,128)(2,1)}, u32[]{:S(2)}, u32[]{:S(2)}) collective-permute-start(bf16[8,64,1024]{2,1,0:T(8,128)(2,1)S(1)} %copy-done.14), channel_id=1, source_target_pairs={{0,8},{1,9},{2,10},{3,11},{4,12},{5,13},{6,14},{7,15},{8,0},{9,1},... | collective-permute-start | bytes 3145736 | tf_op jit(solution)/shard_map/ppermute | solution.py:772
  286.1 107.3 %copy-start.35 = (f32[256,16]{0,1:T(8,128)S(1)}, f32[256,16]{0,1:T(8,128)}, u32[]{:S(2)}) copy-start(f32[256,16]{0,1:T(8,128)} %copy-done.34) | copy-start | bytes 49156
  286.1 107.3 %copy-start.43 = (pred[256,16]{0,1:T(8,128)(4,1)S(1)}, pred[256,16]{0,1:T(8,128)(4,1)}, u32[]{:S(2)}) copy-start(pred[256,16]{0,1:T(8,128)(4,1)} %copy-done.42) | copy-start | bytes 12292
  286.1 107.3 %copy-start.49 = (f32[256]{0:T(256)S(1)}, f32[256]{0:T(256)}, u32[]{:S(2)}) copy-start(f32[256]{0:T(256)} %copy-done.48) | copy-start | bytes 3076
  286.1 107.4 %copy-start.51 = (f32[256]{0:T(256)S(1)}, f32[256]{0:T(256)}, u32[]{:S(2)}) copy-start(f32[256]{0:T(256)} %copy-done.50) | copy-start | bytes 3076
  286.1 107.4 %copy-start.5 = (f32[256,1024]{1,0:T(8,128)S(1)}, f32[256,1024]{1,0:T(8,128)}, u32[]{:S(2)}) copy-start(f32[256,1024]{1,0:T(8,128)} %copy-done.4) | copy-start | bytes 3145732
  286.1 107.4 %copy-start.23 = (bf16[2,8,64,256]{3,2,1,0:T(8,128)(2,1)S(1)}, bf16[2,8,64,256]{3,2,1,0:T(8,128)(2,1)}, u32[]{:S(2)}) copy-start(bf16[2,8,64,256]{3,2,1,0:T(8,128)(2,1)} %get-tuple-element.36) | copy-start | bytes 1572868
  286.1 107.4 %copy-start.45 = (f32[1024,1]{0,1:T(1,128)S(1)}, f32[1024,1]{0,1:T(1,128)}, u32[]{:S(2)}) copy-start(f32[1024,1]{0,1:T(1,128)} %copy-done.44) | copy-start | bytes 12292
  286.1 107.4 %copy-start.55 = (f32[256]{0:T(256)S(1)}, f32[256]{0:T(256)}, u32[]{:S(2)}) copy-start(f32[256]{0:T(256)} %copy-done.54) | copy-start | bytes 3076
  393.4 1.7 copy-start.36
  393.4 1.7 copy-start.59
  395.1 1.9 copy-start.11
  397.0 33.1 %copy-start.3 = (f32[256,1024]{1,0:T(8,128)}, f32[256,1024]{1,0:T(8,128)S(1)}, u32[]{:S(2)}) copy-start(f32[256,1024]{1,0:T(8,128)S(1)} %get-tuple-element.109) | copy-start | bytes 3145732
  397.0 1.8 copy-start.53
  398.7 5.1 copy-start.38
  409.6 4.5 copy-start.17
  414.2 1.8 copy-start.27
  415.9 2.3 copy-start.13
  415.9 4.6 copy-start.33
  420.0 10.9 %collective-permute-start.6 = (f32[2]{0:T(128)S(1)}, f32[2]{0:T(128)S(1)}, u32[]{:S(2)}, u32[]{:S(2)}) collective-permute-start(f32[2]{0:T(128)S(1)} %pad_maximum_fusion.11), channel_id=1, source_target_pairs={{0,16},{16,0},{1,17},{17,1},{2,18},{18,2},{3,19},{19,3},{4,20},{20... | collective-permute-start | bytes 32 | tf_op jit(solution)/shard_map/ppermute | solution.py:948
  420.5 6.3 %copy-start.29 = (f32[256,64]{0,1:T(8,128)S(1)}, f32[256,64]{0,1:T(8,128)}, u32[]{:S(2)}) copy-start(f32[256,64]{0,1:T(8,128)} %copy-done.28) | copy-start | bytes 196612
  422.3 4.5 copy-start.6
  422.3 34.6 %all-to-all-start.1 = ((bf16[8,96,1024]{2,1,0:T(8,128)(2,1)}), bf16[8,96,1024]{2,1,0:T(8,128)(2,1)}, u32[]{:S(2)}, u32[]{:S(2)}) async-start(bf16[8,96,1024]{2,1,0:T(8,128)(2,1)} %fusion.19), calls=%async_computation.1 | async-start | bytes 3145728 | tf_op jit(solution)/shard_map/all_to_all | solution.py:886
  427.6 2.5 copy-start.19
  427.8 17.4 %copy-start.39 = (bf16[256,1024]{0,1:T(8,128)(2,1)}, bf16[256,1024]{0,1:T(8,128)(2,1)S(1)}, u32[]{:S(2)}) copy-start(bf16[256,1024]{0,1:T(8,128)(2,1)S(1)} %fusion.46) | copy-start | bytes 1572868
  428.5 16.1 %collective-permute-start.4 = (bf16[256,1024]{0,1:T(8,128)(2,1)S(1)}, bf16[256,1024]{0,1:T(8,128)(2,1)S(1)}, u32[]{:S(2)}, u32[]{:S(2)}) collective-permute-start(bf16[256,1024]{0,1:T(8,128)(2,1)S(1)} %fusion.40), channel_id=1, source_target_pairs={{16,0},{17,1},{18,2},{19,3},{20,4},{21,5},{22,6},{23,7},{24,8},{25... | collective-permute-start | bytes 1572872 | tf_op jit(solution)/shard_map/ppermute | solution.py:921
  444.9 2.4 copy-start.65
  445.1 4.5 copy-start.40
  457.0 93.7 %collective-permute-start.5 = (bf16[8,96,1024]{2,1,0:T(8,128)(2,1)}, bf16[8,96,1024]{2,1,0:T(8,128)(2,1)}, u32[]{:S(2)}, u32[]{:S(2)}) collective-permute-start(bf16[8,96,1024]{2,1,0:T(8,128)(2,1)} %all-to-all-done.1), channel_id=1, source_target_pairs={{0,16},{16,0},{1,17},{17,1},{2,18},{18,2},{3,19},{19,3},{4,20},{20... | collective-permute-start | bytes 4718600 | tf_op jit(solution)/shard_map/ppermute | solution.py:944
  457.0 90.9 %copy-start.57 = (f32[256]{0:T(256)S(1)}, f32[256]{0:T(256)}, u32[]{:S(2)}) copy-start(f32[256]{0:T(256)} %get-tuple-element.124) | copy-start | bytes 3076
  554.4 5.2 copy-start.1
  (11 other events, 10.9 us)

commit v6 on v4

--- a/solution.py
+++ b/solution.py
@@ -161,8 +161,8 @@
 
 
 def reduce_kernel(
-    groups_count, mixed_ref, normed_ref, gate_ref, weights_ref, mixed_out, normed_out, gate_out, far_out,
-    total, got0, got1, got2, got3, sems, gate_sems, local, own_gate, far_sems,
+    mixed_ref, normed_ref, gate_ref, mixed_out, normed_out, gate_out,
+    total, got0, got1, got2, got3, sems, gate_sems, local, own_gate,
 ):
     rank, peer = my_place()
     chip = rank // 2
@@ -182,10 +182,9 @@
     everyone = [
         {"seq": 1 - seq if mask & 8 else seq, "dp": flip_mask(dp, mask & 7)} for mask in range(1, 16)
     ]
-    home, far = other_groups(groups_count)
-    for there in everyone + far:
+    for there in everyone:
         pl.semaphore_signal(barrier, inc=1, device_id=there, device_id_type=MESH)
-    pl.semaphore_wait(barrier, 15 + len(far))
+    pl.semaphore_wait(barrier, 15)
     gates = []
     keep = pltpu.make_async_copy(gate_ref.at[rank], gate_out.at[rank], own_gate)
     keep.start()
@@ -227,17 +226,6 @@
                 send(
                     t, p, 0, c, ins[t].at[2 * c + 1 - core, rows], got0.at[t, c, rows], 1
                 )
-    for k, there in enumerate(far):
-        copy = pltpu.make_async_remote_copy(
-            src_ref=weights_ref.at[there["dp"] // RANKS],
-            dst_ref=far_out.at[k],
-            send_sem=far_sems.at[0, k],
-            recv_sem=far_sems.at[1, k],
-            device_id=there,
-            device_id_type=MESH,
-        )
-        copy.start()
-        gates.append(copy)
     for copy in loads:
         copy.wait()
     got = (got1, got2, got3)
@@ -278,23 +266,19 @@
     keep.wait()
 
 
-def group_reduce(collective_id, mixed, normed, gate_grad, weights):
+def group_reduce(collective_id, mixed, normed, gate_grad):
     rows, width = mixed.shape[1:]
-    groups_count = weights.shape[0]
-    others = max(groups_count - 1, 1)
     return pl.pallas_call(
-        functools.partial(reduce_kernel, groups_count),
+        reduce_kernel,
         out_shape=[
             jax.ShapeDtypeStruct((rows, width), f32),
             jax.ShapeDtypeStruct((rows, width), f32),
             jax.ShapeDtypeStruct(gate_grad.shape, gate_grad.dtype),
-            jax.ShapeDtypeStruct((others,) + weights.shape[1:], weights.dtype),
-        ],
-        in_specs=[pl.BlockSpec(memory_space=pl.ANY)] * 4,
+        ],
+        in_specs=[pl.BlockSpec(memory_space=pl.ANY)] * 3,
         out_specs=[
             pl.BlockSpec(memory_space=pltpu.VMEM),
             pl.BlockSpec(memory_space=pltpu.VMEM),
-            pl.BlockSpec(memory_space=pl.ANY),
             pl.BlockSpec(memory_space=pl.ANY),
         ],
         scratch_shapes=[
@@ -307,14 +291,13 @@
             pltpu.SemaphoreType.DMA((2, 16)),
             pltpu.SemaphoreType.DMA((2, 8)),
             pltpu.SemaphoreType.DMA(()),
-            pltpu.SemaphoreType.DMA((2, others)),
         ],
         compiler_params=pltpu.CompilerParams(
             collective_id=collective_id, has_side_effects=True, vmem_limit_bytes=48 * 2**20
         ),
         cost_estimate=pl.CostEstimate(flops=70000000000, bytes_accessed=2**24, transcendentals=0),
         name="group_reduce",
-    )(mixed, normed, gate_grad, weights)
+    )(mixed, normed, gate_grad)
 
 
 def column_parts(half, which):
@@ -537,17 +520,20 @@
                         1,
                     )
     arrivals = []
-    for mask, there in zip(range(1, 16), everyone):
-        copy = pltpu.make_async_remote_copy(
-            src_ref=pieces.at[flip_mask(rank, mask) % RANKS],
-            dst_ref=whole.at[rank],
-            send_sem=piece_sems.at[0, mask],
-            recv_sem=piece_sems.at[1, mask],
-            device_id=there,
-            device_id_type=MESH,
-        )
-        copy.start()
-        arrivals.append(copy)
+
+    def send_pieces(masks):
+        for mask in masks:
+            copy = pltpu.make_async_remote_copy(
+                src_ref=pieces.at[flip_mask(rank, mask) % RANKS],
+                dst_ref=whole.at[rank],
+                send_sem=piece_sems.at[0, mask],
+                recv_sem=piece_sems.at[1, mask],
+                device_id=everyone[mask - 1],
+                device_id_type=MESH,
+            )
+            copy.start()
+            arrivals.append(copy)
+
     for copy in loads:
         copy.wait()
     got = (got1, got2, got3)
@@ -579,6 +565,7 @@
                             got[stage][a].at[index, :, :, columns],
                             order[stage],
                         )
+        send_pieces(((1, 2, 4, 8), (3, 5, 9, 6), (10, 12, 7), ())[stage])
     waiting = []
     for k, there in enumerate(far):
         for a in range(count):
@@ -592,6 +579,7 @@
             )
             copy.start()
             waiting.append(copy)
+    send_pieces((14, 11, 13, 15))
     for copy in waiting:
         copy.wait()
     last = []
@@ -789,27 +777,19 @@
     inside = [[g * RANKS + j for j in range(RANKS)] for g in range(groups_count)]
     half_experts = EXPERTS // 2
 
-    def to_group(value, k):
-        turn = [(d, (d + k * RANKS) % n_dp) for d in range(n_dp)]
-        return lax.ppermute(value, "dp", turn)
-
-    def expert_pieces(gate_up_shard, down_shard, seq_rank):
-        mine = [
-            jnp.swapaxes(lax.dynamic_slice_in_dim(w, seq_rank * half_experts, half_experts, axis=1), 0, 1)
-            for w in (gate_up_shard, down_shard)
-        ]
-        return lax.all_to_all(
-            jnp.concatenate(mine, 1), "dp", split_axis=0, concat_axis=0, tiled=True, axis_index_groups=inside
-        )
-
-    def expert_weights(mine, first):
-        home = lax.axis_index("dp") // RANKS
-        parts = [to_group(mine, k) for k in range(groups_count - 1, 0, -1)] + [mine]
-        ring = jnp.stack(parts + parts)
-        start = (2 * groups_count - 1 - home) % groups_count
-        whole = lax.dynamic_slice_in_dim(ring, start, groups_count, axis=0)
-        width = whole.shape[-1]
-        return whole[:, :, :first].reshape(-1, width), whole[:, :, first:].reshape(-1, width)
+    between = [[g * RANKS + j for g in range(groups_count)] for j in range(RANKS)]
+
+    def expert_half(w, seq_rank):
+        return lax.dynamic_slice_in_dim(w, seq_rank * half_experts, half_experts, axis=1)
+
+    def expert_weights(halves, first):
+        mine = halves.transpose(2, 0, 1, 3)
+        mine = lax.all_to_all(
+            mine, "dp", split_axis=0, concat_axis=0, tiled=True, axis_index_groups=inside
+        )
+        mine = jnp.swapaxes(mine, 0, 1)
+        width = mine.shape[-1]
+        return mine[:, :, :first].reshape(-1, width), mine[:, :, first:].reshape(-1, width)
 
     def body(
         tokens, starts, routes, gain_one, query_key_value_weight, w_out,
@@ -823,6 +803,10 @@
         group = QUERY_HEADS // KEY_VALUE_HEADS
         forward_pair, back_pair = [(0, 1)], [(1, 0)]
 
+        expert_halves = lax.all_gather(
+            jnp.concatenate([expert_half(w_gate_up, seq_rank), expert_half(w_down, seq_rank)], 0),
+            "dp", axis=0, axis_index_groups=between,
+        )
         tokens_before = lax.ppermute(tokens[0], "seq", forward_pair)
         starts_before = lax.ppermute(starts, "seq", forward_pair)
         spare = lambda value: jnp.pad(value, ((0, 0), (0, 128 - value.shape[1])))
@@ -835,10 +819,6 @@
                 [spare(w_router), spare(jnp.stack([gain_one, gain_two], 1))], 1
             ),
         )
-        mine, qkv_weight, out_weight, small = lax.optimization_barrier(
-            (expert_pieces(w_gate_up, w_down, seq_rank), qkv_weight, out_weight, small)
-        )
-        gate_up_weight, down_weight = expert_weights(mine, w_gate_up.shape[0])
         router_weight = small[:, :EXPERTS]
         gain_a = small[:, 128].astype(f32)
         gain_b = small[:, 129].astype(f32)
@@ -875,7 +855,8 @@
         top = jnp.max(scores, axis=-1, keepdims=True)
         exps = jnp.exp(scores - top)
         probs = exps / jnp.sum(exps, axis=-1, keepdims=True)
-        probs_low = probs.astype(bf16)
+        probs_low, expert_halves = lax.optimization_barrier((probs.astype(bf16), expert_halves))
+        gate_up_weight, down_weight = expert_weights(expert_halves, w_gate_up.shape[0])
         attended = jnp.einsum(
             "grqk,kgd->qgrd", probs_low, values, preferred_element_type=f32
         ).reshape(count, query_columns).astype(bf16)
@@ -894,16 +875,10 @@
         mixed_part, normed_part, gate_grad_part, expert_wgrads = expert_layer(
             n_dp, rows_in, grad_all, gate, gate_up_weight, down_weight
         )
-        expert_wgrads = expert_wgrads.reshape((groups_count, RANKS) + expert_wgrads.shape[1:])
-        mixed, normed_grad, gate_grad, expert_far = group_reduce(
-            2, mixed_part, normed_part, gate_grad_part, expert_wgrads
-        )
-        expert_grads = lax.dynamic_index_in_dim(
-            expert_wgrads, lax.axis_index("dp") // RANKS, 0, keepdims=False
-        ).astype(f32)
-        for k in range(groups_count - 1):
-            expert_grads = expert_grads + expert_far[k].astype(f32)
-        expert_grads = expert_grads.astype(bf16)
+        expert_grads = lax.psum_scatter(
+            expert_wgrads, "dp", scatter_dimension=0, tiled=True, axis_index_groups=between
+        )
+        mixed, normed_grad, gate_grad = group_reduce(2, mixed_part, normed_part, gate_grad_part)
         gate_grad = gate_grad[:, 0].T
 
         over_rows = (((0,), (0,)), ((), ()))
@@ -922,6 +897,7 @@
             branch_low, out_weight, (((1,), (1,)), ((), ())), preferred_element_type=f32
         ).astype(bf16).reshape(count, KEY_VALUE_HEADS, group, HEAD_SIZE)
 
+        attended_grad, expert_grads = lax.optimization_barrier((attended_grad, expert_grads))
         prob_grad = jnp.einsum("qgrd,kgd->grqk", attended_grad, values, preferred_element_type=f32)
         delta = jnp.sum(probs * prob_grad, axis=-1, keepdims=True)
         score_grad = (probs * (prob_grad - delta)).astype(bf16)

time: 559 us -> 589 us (1.054)
  Pallas kernels: 370 us -> 413 us
  waiting for transfers between devices: 63.9 us -> 40 us
  between operations: 2.27 us -> 15.4 us
  local copies, waits for them, and re-layouts: 26.9 us -> 33.5 us
    ppermute x1 -> x0, waiting for transfers between devices: 54.8 us -> none  [to_group(): return lax.ppermute(value, 'dp', turn)]
    pallas_call x1, Pallas kernels: 50 us -> 97.3 us  [weights_gather(): pl.pallas_call(functools.partial(weights_gather_kernel, count, groups_cou...]
    all_to_all x1, waiting for transfers between devices: 0.01 us -> 27.4 us  [expert_weights(): lax.all_to_all(mine, 'dp', split_axis=0, concat_axis=0, tiled=True, axis_...]
    pallas_call x1, Pallas kernels: 94.2 us -> 86.9 us  [weights_reduce(): pl.pallas_call(functools.partial(weights_reduce_kernel, count, groups_cou...]
    unnamed x134 -> x124, local copies, waits for them, and re-layouts: 15.4 us -> 14.3 us
  transfers between devices with their start and end apart: 6 -> 7, of which waited for: 2 -> 2; matrix products, arithmetic and copies ran while one was open for 4% -> 8% of each run, Pallas kernels for 9% -> 35%
where the time goes in v6:
time: 589 us; the launch traced here: 582 us
  Pallas kernels  413 us (70%)
  waiting for transfers between devices  40 us (7%)
  matrix products  34.4 us (6%)
  local copies, waits for them, and re-layouts  33.5 us (6%)
  other arithmetic  32.5 us (6%)
  between operations  15.4 us (3%)
  starting transfers between devices  13.6 us (2%)
    pallas_call x1, Pallas kernels, group_reduce(): pl.pallas_call(reduce_kernel, out_shape=[jax.ShapeDtypeStruct((rows, widt...  108 us
    pallas_call x1, Pallas kernels, weights_gather(): pl.pallas_call(functools.partial(weights_gather_kernel, count, groups_cou...  97.3 us
    pallas_call x1, Pallas kernels, weights_reduce(): pl.pallas_call(functools.partial(weights_reduce_kernel, count, groups_cou...  86.9 us
    pallas_call x1, Pallas kernels, group_gather(): pl.pallas_call(functools.partial(gather_kernel, count), out_shape=[jax.Sh...  71 us
    pallas_call x1, Pallas kernels, expert_layer(): pl.pallas_call(expert_kernel, grid=(GROUP // shards,), out_shape=[jax.Sha...  49.8 us
    all_to_all x1, waiting for transfers between devices, expert_weights(): lax.all_to_all(mine, 'dp', split_axis=0, concat_axis=0, tiled=True, axis_...  27.4 us
    unnamed x124, local copies, waits for them, and re-layouts  14.3 us
    ppermute x1, waiting for transfers between devices, body(): kv_back = lax.ppermute(kv_grad[:count].astype(bf16), 'seq', back_pair)  12.5 us
  transfers between devices with their start and end apart: 7, of which 2 were waited for; matrix products, arithmetic and copies ran while one was open for 8% of the time, Pallas kernels for 35%

profile of v6, /device:TPU:0, one launch (start us, length us, event | category | flops | bytes accessed | tf_op | source)
XLA Modules:
  0.0 582.5 jit_solution(13664908791772759950)
XLA Ops:
  7.2 5.8 %collective-permute-start = (bf16[256,1024]{1,0:T(8,128)(2,1)}, bf16[256,1024]{1,0:T(8,128)(2,1)}, u32[]{:S(2)}, u32[]{:S(2)}) collective-permute-start(bf16[256,1024]{1,0:T(8,128)(2,1)} %bitcast.168), channel_id=1, source_target_pairs={{0,16},{1,17},{2,18},{3,19},{4,20},{5,21},{6,22},{7,23},{8,24},{9,... | collective-permute-start | bytes 1572872 | tf_op jit(solution)/shard_map/ppermute | solution.py:810
  13.1 1.3 collective-permute-start.1
  14.5 1.1 constant_dynamic-slice_fusion.1
  15.6 1.3 pad_maximum_fusion.1
  17.3 0.6 fusion.53.refs_2_
  18.0 97.3 %weights_gather.1 = (bf16[2,8,64,2048]{3,2,1,0:T(8,128)(2,1)}, bf16[2,8,64,1024]{3,2,1,0:T(8,128)(2,1)}, bf16[2,8,64,256]{3,2,1,0:T(8,128)(2,1)}) custom-call(bf16[64,2048]{1,0:T(8,128)(2,1)} %refs_0_.1, bf16[64,1024]{1,0:T(8,128)(2,1)} %refs_1_.1, bf16[64,256]{1,0:T(8,128)(2,1)} %fusion.53.refs_2_), custom_call_target="tpu_custom_call" | custom-call | flops 44999999488 | bytes 16777216 | tf_op jit(solution)/shard_map/weights_gather/pallas_call | solution.py:418
  115.2 1.2 slice_convert_fusion.2
  117.3 0.8 fusion.40
  118.0 1.1 convert_element_type.147
  119.7 1.3 fusion.10
  121.0 1.3 copy-done.23
  122.7 2.7 fusion.8
  125.6 1.0 fusion.30
  127.0 7.4 %fusion.72 = (f32[8,2,256]{2,1,0:T(2,128)S(1)}, f32[8,2,256,512]{2,3,1,0:T(8,128)}) fusion(pred[256,512]{0,1:T(8,128)(4,1)} %fusion.40, bf16[512,8,64,1]{0,2,3,1:T(8,128)(2,1)S(1)} %fusion.37, bf16[256,8,2,64]{0,3,2,1:T(8,128)(2,1)} %fusion.30), kind=kOutput, calls=%fused_computation.165 | convolution fusion | flops 276824576 | bytes 9584640 | tf_op jit(solution)/shard_map/sub | solution.py:856
  134.4 6.3 %fusion.69 = bf16[8,2,256,512]{2,3,1,0:T(8,128)(2,1)} fusion(f32[8,2,256,512]{2,3,1,0:T(8,128)} %get-tuple-element.127, f32[8,2,256]{2,1,0:T(2,128)S(1)} %get-tuple-element.126), kind=kLoop, calls=%fused_computation.162 | loop fusion | flops 4194304 | bytes 12599296 | tf_op jit(solution)/shard_map/convert_element_type | solution.py:858
  140.6 5.6 copy.129
  146.2 4.6 all-to-all-start
  151.9 1.3 slice.212
  153.4 3.2 convolution_convert_fusion.2
  156.6 0.8 multiply_reduce_fusion.5
  157.5 0.6 multiply_multiply_fusion.1
  158.6 0.6 copy-done.30
  159.2 0.6 copy-done.43
  159.8 0.6 fusion.68.refs_1_
  160.4 27.4 %all-to-all-done = bf16[8,2,96,1024]{3,2,1,0:T(8,128)(2,1)} async-done(((bf16[8,2,96,1024]{3,2,1,0:T(8,128)(2,1)}), bf16[8,2,96,1024]{3,2,1,0:T(8,128)(2,1)}, u32[]{:S(2)}, u32[]{:S(2)}) %all-to-all-start) | async-done | bytes 3145760 | tf_op jit(solution)/shard_map/all_to_all | solution.py:787
  187.8 1.8 slice.150
  189.6 1.3 slice.151
  190.9 1.5 copy.95
  192.4 1.0 copy.96
  193.4 71.0 %group_gather.1 = (bf16[16,256,1024]{2,1,0:T(8,128)(2,1)}, f32[16,16,256]{2,1,0:T(8,128)}, bf16[16,256,1024]{2,1,0:T(8,128)(2,1)}) custom-call(bf16[256,1024]{1,0:T(8,128)(2,1)} %copy-done.14, f32[16,256]{1,0:T(8,128)} %fusion.68.refs_1_, bf16[256,1024]{1,0:T(8,128)(2,1)} %bitcast.188), custom_call_target="tpu_custom_call" | custom-call | flops 60000002048 | bytes 16777216 | tf_op jit(solution)/shard_map/group_gather/pallas_call | solution.py:136
  264.5 1.5 constant_dynamic-slice_fusion.gate_ref
  266.0 49.8 %expert_layer.1 = (bf16[16,256,1024]{2,1,0:T(8,128)(2,1)}, bf16[16,256,1024]{2,1,0:T(8,128)(2,1)}, f32[16,8,256]{2,1,0:T(8,128)}, bf16[16,96,1024]{2,1,0:T(8,128)(2,1)}) custom-call(bf16[16,256,1024]{2,1,0:T(8,128)(2,1)} %get-tuple-element.40.rows_ref, bf16[16,256,1024]{2,1,0:T(8,128)(2,1)} %get-tuple-element.41.grad_ref, ...), custom_call_target="tpu_custom_call" | custom-call | flops 44999999488 | bytes 16777216 | tf_op jit(solution)/shard_map/expert_layer/pallas_call | solution.py:710
  315.9 0.9 copy-done.3
  316.8 108.1 %group_reduce.1 = (f32[256,1024]{1,0:T(8,128)S(1)}, f32[256,1024]{1,0:T(8,128)S(1)}, f32[16,8,256]{2,1,0:T(8,128)S(1)}) custom-call(bf16[16,256,1024]{2,1,0:T(8,128)(2,1)} %get-tuple-element.45.mixed_ref, bf16[16,256,1024]{2,1,0:T(8,128)(2,1)} %get-tuple-element.46.normed_ref, f32[16,8,256]{2,1,0:T(8,128)S(1)} %copy-done.3), custom_call_target="tpu_custom_call" | custom-call | flops 70000001024 | bytes 16777216 | tf_op jit(solution)/shard_map/group_reduce/pallas_call | solution.py:271
  425.1 1.5 multiply_reduce_fusion.2
  426.6 1.9 multiply_reduce_fusion.1
  428.5 1.5 pad_maximum_fusion.11
  430.5 0.7 convolution_convert_fusion.3
  431.3 1.0 copy.97
  432.6 1.8 convolution_convert_fusion.1
  434.4 1.9 sqrt_bitcast_fusion
  436.3 5.2 fusion.1
  441.5 1.4 fusion.74
  442.9 1.0 slice-done.1
  443.8 1.5 fusion.3
  445.4 0.8 fusion.14
  446.4 1.4 fusion.12
  447.9 1.3 collective-permute-start.2
  449.7 12.5 %collective-permute-done.2 = bf16[256,1024]{0,1:T(8,128)(2,1)S(1)} collective-permute-done((bf16[256,1024]{0,1:T(8,128)(2,1)S(1)}, bf16[256,1024]{0,1:T(8,128)(2,1)S(1)}, u32[]{:S(2)}, u32[]{:S(2)}) %collective-permute-start.2) | collective-permute-done | bytes 524320 | tf_op jit(solution)/shard_map/ppermute | solution.py:914
  462.8 3.3 convolution_convert_fusion
  466.1 2.4 fusion.22
  468.5 1.1 select_maximum_fusion
  469.6 1.6 copy.101
  471.2 1.4 copy-done.2
  472.6 86.9 %weights_reduce.1 = (bf16[64,2048]{1,0:T(8,128)(2,1)S(1)}, bf16[64,1024]{1,0:T(8,128)(2,1)S(1)}, f32[64,256]{1,0:T(8,128)S(1)}, bf16[16,96,1024]{2,1,0:T(8,128)(2,1)}) custom-call(bf16[2,8,64,2048]{3,2,1,0:T(8,128)(2,1)} %bitcast.205, bf16[2,8,64,1024]{3,2,1,0:T(8,128)(2,1)S(1)} %bitcast.157, f32[2,8,64,256]{3,2,1,0:T(8,128)S(1)} %bitcast.158, ...), custom_call_target="tpu_custom_call" | custom-call | flops 80000000000 | bytes 16777216 | tf_op jit(solution)/shard_map/weights_reduce/pallas_call | solution.py:626
  559.5 2.1 convert_bitcast_fusion
  561.6 1.5 convert_bitcast_fusion.1
  563.0 0.7 slice_reduce_fusion
  563.7 4.4 copy.103
  568.2 2.5 copy.104
  570.7 0.8 convert_element_type.177
  571.6 0.7 convert_element_type.178
  572.3 0.7 copy.102
  573.0 2.5 fusion.38
  (173 shorter events, 6.6 us)
Async XLA Ops:
  7.2 7.2 %copy-start = (bf16[64,16,1024]{2,1,0:T(8,128)(2,1)S(1)}, bf16[64,16,1024]{2,1,0:T(8,128)(2,1)}, u32[]{:S(2)}) copy-start(bf16[64,16,1024]{2,1,0:T(8,128)(2,1)} %param.19) | copy-start | bytes 6291460
  7.2 9.8 %copy-start.9 = (bf16[1,256,1024]{2,1,0:T(8,128)(2,1)S(1)}, bf16[1,256,1024]{2,1,0:T(8,128)(2,1)}, u32[]{:S(2)}) copy-start(bf16[1,256,1024]{2,1,0:T(8,128)(2,1)} %param.11) | copy-start | bytes 1572868
  7.2 133.4 %all-gather.3.cloned.1.call-start = ((), (), s32[]{:S(2)}) async-start(), calls=%async_computation.3 | async-start | bytes 4718592 | tf_op jit(solution)/shard_map/all_gather | solution.py:806
  7.2 110.8 %collective-permute-start = (bf16[256,1024]{1,0:T(8,128)(2,1)}, bf16[256,1024]{1,0:T(8,128)(2,1)}, u32[]{:S(2)}, u32[]{:S(2)}) collective-permute-start(bf16[256,1024]{1,0:T(8,128)(2,1)} %bitcast.168), channel_id=1, source_target_pairs={{0,16},{1,17},{2,18},{3,19},{4,20},{5,21},{6,22},{7,23},{8,24},{9,... | collective-permute-start | bytes 1572872 | tf_op jit(solution)/shard_map/ppermute | solution.py:810
  13.1 103.5 %collective-permute-start.1 = (s32[1,256]{1,0:T(1,128)}, s32[1,256]{1,0:T(1,128)S(1)}, u32[]{:S(2)}, u32[]{:S(2)}) collective-permute-start(s32[1,256]{1,0:T(1,128)} %param.12), channel_id=1, source_target_pairs={{0,16},{1,17},{2,18},{3,19},{4,20},{5,21},{6,22},{7,23},{8,24},{9,... | collective-permute-start | bytes 3080 | tf_op jit(solution)/shard_map/ppermute | solution.py:811
  14.5 2.6 copy-start.53
  14.5 2.6 copy-start.54
  14.5 2.7 copy-start.51
  18.0 98.7 %copy-start.52 = (s32[1,256]{1,0:T(1,128)S(1)}, s32[1,256]{1,0:T(1,128)}, u32[]{:S(2)}) copy-start(s32[1,256]{1,0:T(1,128)} %param.12) | copy-start | bytes 3076
  116.6 4.4 copy-start.39
  116.6 3.1 copy-start.55
  117.2 8.4 %copy-start.24 = (f32[256,64]{0,1:T(8,128)}, f32[256,64]{0,1:T(8,128)S(1)}, u32[]{:S(2)}) copy-start(f32[256,64]{0,1:T(8,128)S(1)} %get-tuple-element.138) | copy-start | bytes 196612
  117.2 8.4 %copy-start.28 = (f32[256,64]{0,1:T(8,128)}, f32[256,64]{0,1:T(8,128)S(1)}, u32[]{:S(2)}) copy-start(f32[256,64]{0,1:T(8,128)S(1)} %get-tuple-element.139) | copy-start | bytes 196612
  119.7 1.3 copy-start.26
  121.0 1.3 copy-start.23
  126.9 7.4 %copy-start.17 = (bf16[512,8,64,1]{0,2,3,1:T(8,128)(2,1)}, bf16[512,8,64,1]{0,2,3,1:T(8,128)(2,1)S(1)}, u32[]{:S(2)}) copy-start(bf16[512,8,64,1]{0,2,3,1:T(8,128)(2,1)S(1)} %fusion.37) | copy-start | bytes 1572868
  134.4 6.3 %copy-start.35 = (f32[8,2,256]{2,1,0:T(2,128)}, f32[8,2,256]{2,1,0:T(2,128)S(1)}, u32[]{:S(2)}) copy-start(f32[8,2,256]{2,1,0:T(2,128)S(1)} %get-tuple-element.126) | copy-start | bytes 49156
  146.2 4.9 copy-start.47
  146.2 41.6 %all-to-all-start = ((bf16[8,2,96,1024]{3,2,1,0:T(8,128)(2,1)}), bf16[8,2,96,1024]{3,2,1,0:T(8,128)(2,1)}, u32[]{:S(2)}, u32[]{:S(2)}) async-start(bf16[8,2,96,1024]{3,2,1,0:T(8,128)(2,1)} %bitcast.161), calls=%async_computation | async-start | bytes 6291456 | tf_op jit(solution)/shard_map/all_to_all | solution.py:787
  150.8 285.4 %reduce-scatter.2.cloned.1.call-start = ((), (), s32[]{:S(2)}) async-start(), calls=%async_computation.2 | async-start | bytes 4718592 | tf_op jit(solution)/shard_map/reduce_scatter | solution.py:878
  151.1 7.0 %copy-start.37 = (f32[1024,1]{0,1:T(1,128)}, f32[1024,1]{0,1:T(1,128)S(1)}, u32[]{:S(2)}) copy-start(f32[1024,1]{0,1:T(1,128)S(1)} %copy.118) | copy-start | bytes 12292
  151.1 7.2 %copy-start.33 = (pred[256,16]{0,1:T(8,128)(4,1)}, pred[256,16]{0,1:T(8,128)(4,1)S(1)}, u32[]{:S(2)}) copy-start(pred[256,16]{0,1:T(8,128)(4,1)S(1)} %fusion.48) | copy-start | bytes 12292
  153.4 3.2 copy-start.16
  153.4 3.3 copy-start.11
  156.6 32.9 %copy-start.13 = (bf16[8,64,2,256]{3,1,2,0:T(8,128)(2,1)}, bf16[8,64,2,256]{3,1,2,0:T(8,128)(2,1)S(1)}, u32[]{:S(2)}) copy-start(bf16[8,64,2,256]{3,1,2,0:T(8,128)(2,1)S(1)} %convolution_convert_fusion.2) | copy-start | bytes 1572868
  156.6 1.7 copy-start.19
  157.5 33.4 %copy-start.7 = (f32[256,1024]{1,0:T(8,128)}, f32[256,1024]{1,0:T(8,128)S(1)}, u32[]{:S(2)}) copy-start(f32[256,1024]{1,0:T(8,128)S(1)} %get-tuple-element.129) | copy-start | bytes 3145732
  158.1 32.7 %copy-start.45 = (f32[256]{0:T(256)}, f32[256]{0:T(256)S(1)}, u32[]{:S(2)}) copy-start(f32[256]{0:T(256)S(1)} %get-tuple-element.125) | copy-start | bytes 3076
  158.3 34.1 %copy-start.14 = (bf16[256,1024]{1,0:T(8,128)(2,1)}, bf16[256,1024]{1,0:T(8,128)(2,1)S(1)}, u32[]{:S(2)}) copy-start(bf16[256,1024]{1,0:T(8,128)(2,1)S(1)} %multiply_convert_fusion.1.refs_0_) | copy-start | bytes 1572868
  158.6 0.6 copy-start.30
  315.8 0.9 copy-start.3
  316.8 108.2 %copy-start.31 = (f32[256,16]{0,1:T(8,128)S(1)}, f32[256,16]{0,1:T(8,128)}, u32[]{:S(2)}) copy-start(f32[256,16]{0,1:T(8,128)} %copy-done.30) | copy-start | bytes 49156
  316.8 108.2 %copy-start.34 = (pred[256,16]{0,1:T(8,128)(4,1)S(1)}, pred[256,16]{0,1:T(8,128)(4,1)}, u32[]{:S(2)}) copy-start(pred[256,16]{0,1:T(8,128)(4,1)} %copy-done.33) | copy-start | bytes 12292
  316.8 108.2 %copy-start.42 = (f32[256]{0:T(256)S(1)}, f32[256]{0:T(256)}, u32[]{:S(2)}) copy-start(f32[256]{0:T(256)} %copy-done.41) | copy-start | bytes 3076
  316.8 108.2 %copy-start.44 = (f32[256]{0:T(256)S(1)}, f32[256]{0:T(256)}, u32[]{:S(2)}) copy-start(f32[256]{0:T(256)} %copy-done.43) | copy-start | bytes 3076
  316.8 108.3 %copy-start.8 = (f32[256,1024]{1,0:T(8,128)S(1)}, f32[256,1024]{1,0:T(8,128)}, u32[]{:S(2)}) copy-start(f32[256,1024]{1,0:T(8,128)} %copy-done.7) | copy-start | bytes 3145732
  316.8 108.3 %copy-start.20 = (bf16[2,8,64,256]{3,2,1,0:T(8,128)(2,1)S(1)}, bf16[2,8,64,256]{3,2,1,0:T(8,128)(2,1)}, u32[]{:S(2)}) copy-start(bf16[2,8,64,256]{3,2,1,0:T(8,128)(2,1)} %get-tuple-element.34) | copy-start | bytes 1572868
  316.8 108.3 %copy-start.38 = (f32[1024,1]{0,1:T(1,128)S(1)}, f32[1024,1]{0,1:T(1,128)}, u32[]{:S(2)}) copy-start(f32[1024,1]{0,1:T(1,128)} %copy-done.37) | copy-start | bytes 12292
  316.8 108.3 %copy-start.46 = (f32[256]{0:T(256)S(1)}, f32[256]{0:T(256)}, u32[]{:S(2)}) copy-start(f32[256]{0:T(256)} %copy-done.45) | copy-start | bytes 3076
  316.8 109.8 %copy-start.32 = (bf16[1,256,1024]{2,1,0:T(8,128)(2,1)S(1)}, bf16[1,256,1024]{2,1,0:T(8,128)(2,1)}, u32[]{:S(2)}) copy-start(bf16[1,256,1024]{2,1,0:T(8,128)(2,1)} %param.21) | copy-start | bytes 1572868
  316.8 109.8 %copy-start.50 = (f32[256]{0:T(256)S(1)}, f32[256]{0:T(256)}, u32[]{:S(2)}) copy-start(f32[256]{0:T(256)} %get-tuple-element.124) | copy-start | bytes 3076
  425.1 5.4 copy-start.12
  428.5 5.8 copy-start.5
  428.5 3.7 copy-start.15
  430.0 4.4 collective-permute-start.3
  430.5 5.8 copy-start.36
  436.3 6.6 %slice-start = ((s8[8388608]{0:T(1024)(128)(4,1)}), s8[4194304]{0:T(1024)(128)(4,1)S(1)}, s32[]{:S(2)}) async-start(s8[8388608]{0:T(1024)(128)(4,1)} %bitcast.159), calls=%async_computation.4 | async-start | bytes 8388608
  436.3 5.2 copy-start.4
  436.3 5.2 copy-start.21
  436.3 7.5 %slice-start.1 = ((s8[8388608]{0:T(1024)(128)(4,1)}), s8[4194304]{0:T(1024)(128)(4,1)S(1)}, s32[]{:S(2)}) async-start(s8[8388608]{0:T(1024)(128)(4,1)} %bitcast.159), calls=%async_computation.5 | async-start | bytes 8388608
  443.8 1.5 copy-start.18
  445.4 1.0 copy-start.22
  446.4 2.8 copy-start.25
  447.8 1.7 copy-start.29
  447.9 14.4 %collective-permute-start.2 = (bf16[256,1024]{0,1:T(8,128)(2,1)S(1)}, bf16[256,1024]{0,1:T(8,128)(2,1)S(1)}, u32[]{:S(2)}, u32[]{:S(2)}) collective-permute-start(bf16[256,1024]{0,1:T(8,128)(2,1)S(1)} %fusion.26), channel_id=1, source_target_pairs={{16,0},{17,1},{18,2},{19,3},{20,4},{21,5},{22,6},{23,7},{24,8},{25... | collective-permute-start | bytes 1572872 | tf_op jit(solution)/shard_map/ppermute | solution.py:914
  449.7 13.1 %copy-start.27 = (bf16[512,1024]{1,0:T(8,128)(2,1)S(1)}, bf16[512,1024]{1,0:T(8,128)(2,1)}, u32[]{:S(2)}) copy-start(bf16[512,1024]{1,0:T(8,128)(2,1)} %copy-done.26) | copy-start | bytes 3145732
  462.6 3.5 copy-start.10
  462.7 3.4 copy-start.40
  462.7 3.4 copy-start.49
  462.7 3.4 copy-start.56
  471.2 1.4 copy-start.2
  563.7 11.7 %copy-start.1 = (bf16[64,16,1024]{2,1,0:T(8,128)(2,1)S(1)}, bf16[64,16,1024]{2,1,0:T(8,128)(2,1)}, u32[]{:S(2)}) copy-start(bf16[64,16,1024]{2,1,0:T(8,128)(2,1)} %param.19) | copy-start | bytes 6291460
  568.2 4.8 copy-start.6
  568.2 4.8 copy-start.48
  (2 other events, 1.2 us)
Sparse Core Ops, SparseCore 0:
  17.1 83.0 all-gather.2
  316.0 77.1 reduce-scatter.1

commit v7 on v6

--- a/solution.py
+++ b/solution.py
@@ -15,7 +15,9 @@
 EXPERTS = 16
 TOPK = 8
 RANKS = 8
-GROUP = 16
+PLACES = 4
+GROUP = 8
+OWN = EXPERTS // GROUP
 
 epsilon = 1e-06
 rope_base = 10000.0
@@ -26,6 +28,7 @@
 MESH = pl.DeviceIdType.MESH
 
 LINKS = ((8, 4, 2), (4, 2, 8), (2, 8, 4))
+TOKEN_LINKS = ((4, 2), (2, 4))
 
 
 def flip(value, bit):
@@ -47,41 +50,41 @@
 
 
 def row_parts(rows):
-    first = (rows // 3 + 15) // 16 * 16
-    second = (rows - first) // 2 // 16 * 16
-    return ((0, first), (first, second), (first + second, rows - first - second))
-
-
-def my_place():
+    first = (rows // 2 + 15) // 16 * 16
+    return ((0, first), (first, rows - first))
+
+
+def my_place(places=RANKS):
     seq = lax.axis_index("seq")
     dp = lax.axis_index("dp")
-    rank = seq * RANKS + dp % RANKS
-
-    def peer(bit):
-        if bit == 8:
-            return {"seq": 1 - seq, "dp": dp}
-        return {"seq": seq, "dp": flip(dp, bit)}
+    rank = seq * places + dp % places
+
+    def peer(mask):
+        return {
+            "seq": 1 - seq if mask & places else seq,
+            "dp": flip_mask(dp, mask & (places - 1)),
+        }
 
     return rank, peer
 
 
-def meet(peer):
+def meet(devices):
     barrier = pltpu.get_barrier_semaphore()
-    for bit in (1, 2, 4, 8):
-        pl.semaphore_signal(barrier, inc=1, device_id=peer(bit), device_id_type=MESH)
-    pl.semaphore_wait(barrier, 4)
+    for there in devices:
+        pl.semaphore_signal(barrier, inc=1, device_id=there, device_id_type=MESH)
+    pl.semaphore_wait(barrier, len(devices))
 
 
 def gather_kernel(count, *refs):
     ins, outs = refs[:count], refs[count : 2 * count]
     send, recv, send_core, recv_core, local = refs[2 * count :]
-    rank, peer = my_place()
+    rank, peer = my_place(PLACES)
     own = [
         pltpu.make_async_copy(ins[a], outs[a].at[rank], local.at[a]) for a in range(count)
     ]
     for copy in own:
         copy.start()
-    meet(peer)
+    meet([peer(bit) for bit in (1, 2, 4)])
     parts = [row_parts(ref.shape[0]) for ref in ins]
 
     def remote(a, p, mask, bit, sems, index):
@@ -100,16 +103,16 @@
 
     started = []
     live = {}
-    for step in range(4):
-        for p in range(3):
+    for step in range(3):
+        for p in range(2):
             for a in range(count):
                 if parts[a][p][1] == 0:
                     continue
-                order = LINKS[p]
+                order = TOKEN_LINKS[p]
                 if step > 0:
                     for copy in live.pop((a, p)):
                         copy.wait_recv()
-                if step < 3:
+                if step < 2:
                     now = []
                     for index, mask in enumerate(subsets(order[:step])):
                         copy = remote(a, p, mask, order[step], (send, recv), 2**step - 1 + index)
@@ -139,10 +142,10 @@
         in_specs=[pl.BlockSpec(memory_space=pltpu.VMEM)] * count,
         out_specs=[pl.BlockSpec(memory_space=pl.ANY)] * count,
         scratch_shapes=[
-            pltpu.SemaphoreType.DMA((count, 3, 7)),
-            pltpu.SemaphoreType.DMA((count, 3, 7)),
-            pltpu.SemaphoreType.DMA((count, 3, 8)),
-            pltpu.SemaphoreType.DMA((count, 3, 8)),
+            pltpu.SemaphoreType.DMA((count, 2, 3)),
+            pltpu.SemaphoreType.DMA((count, 2, 3)),
+            pltpu.SemaphoreType.DMA((count, 2, 4)),
+            pltpu.SemaphoreType.DMA((count, 2, 4)),
             pltpu.SemaphoreType.DMA((count,)),
         ],
         compiler_params=pltpu.CompilerParams(collective_id=collective_id, has_side_effects=True),
@@ -162,9 +165,9 @@
 
 def reduce_kernel(
     mixed_ref, normed_ref, gate_ref, mixed_out, normed_out, gate_out,
-    total, got0, got1, got2, got3, sems, gate_sems, local, own_gate,
+    total, got0, got1, got2, sems, gate_sems, local, own_gate,
 ):
-    rank, peer = my_place()
+    rank, peer = my_place(PLACES)
     chip = rank // 2
     core = rank % 2
     parts = row_parts(mixed_ref.shape[1])
@@ -172,23 +175,16 @@
     outs = (mixed_out, normed_out)
     loads = []
     for t in range(2):
-        for c in range(8):
+        for c in range(4):
             copy = pltpu.make_async_copy(ins[t].at[2 * c + core], total.at[t, c], local.at[t, c])
             copy.start()
             loads.append(copy)
-    barrier = pltpu.get_barrier_semaphore()
-    seq = lax.axis_index("seq")
-    dp = lax.axis_index("dp")
-    everyone = [
-        {"seq": 1 - seq if mask & 8 else seq, "dp": flip_mask(dp, mask & 7)} for mask in range(1, 16)
-    ]
-    for there in everyone:
-        pl.semaphore_signal(barrier, inc=1, device_id=there, device_id_type=MESH)
-    pl.semaphore_wait(barrier, 15)
+    everyone = [peer(mask) for mask in range(1, GROUP)]
+    meet(everyone)
     gates = []
     keep = pltpu.make_async_copy(gate_ref.at[rank], gate_out.at[rank], own_gate)
     keep.start()
-    for mask, there in zip(range(1, 16), everyone):
+    for mask, there in zip(range(1, GROUP), everyone):
         copy = pltpu.make_async_remote_copy(
             src_ref=gate_ref.at[flip_mask(rank, mask)],
             dst_ref=gate_out.at[rank],
@@ -219,20 +215,20 @@
     def chip_of(mask):
         return flip_mask(rank, mask) // 2
 
-    for p in range(3):
+    for p in range(2):
         for t in range(2):
             rows = pl.ds(*parts[p])
-            for c in range(8):
+            for c in range(4):
                 send(
                     t, p, 0, c, ins[t].at[2 * c + 1 - core, rows], got0.at[t, c, rows], 1
                 )
     for copy in loads:
         copy.wait()
-    got = (got1, got2, got3)
-    for stage in range(4):
-        for p in range(3):
+    got = (got1, got2)
+    for stage in range(3):
+        for p in range(2):
             for t in range(2):
-                order = LINKS[p]
+                order = TOKEN_LINKS[p]
                 rows = pl.ds(*parts[p])
                 for copy in live.pop((t, p)):
                     copy.wait_recv()
@@ -242,16 +238,16 @@
                         add_rows(total.at[t, c], got0.at[t, c], *parts[p])
                         return carry
 
-                    lax.fori_loop(0, 8, over_chips, 0)
+                    lax.fori_loop(0, 4, over_chips, 0)
                 else:
                     for index, mask in enumerate(subsets(order[stage:])):
-                        if stage == 3:
-                            outs[t][rows] = total[t, chip, rows].astype(f32) + got3[t, 0, rows].astype(f32)
+                        if stage == 2:
+                            outs[t][rows] = total[t, chip, rows].astype(f32) + got2[t, 0, rows].astype(f32)
                         else:
                             add_rows(
                                 total.at[t, chip_of(mask)], got[stage - 1].at[t, index], *parts[p]
                             )
-                if stage < 3:
+                if stage < 2:
                     for index, mask in enumerate(subsets(order[stage + 1 :])):
                         send(
                             t, p, stage + 1, index,
@@ -282,14 +278,13 @@
             pl.BlockSpec(memory_space=pl.ANY),
         ],
         scratch_shapes=[
-            pltpu.VMEM((2, 8, rows, width), bf16),
-            pltpu.VMEM((2, 8, rows, width), bf16),
+            pltpu.VMEM((2, 4, rows, width), bf16),
             pltpu.VMEM((2, 4, rows, width), bf16),
             pltpu.VMEM((2, 2, rows, width), bf16),
             pltpu.VMEM((2, 1, rows, width), bf16),
-            pltpu.SemaphoreType.DMA((2, 2, 3, 4, 8)),
-            pltpu.SemaphoreType.DMA((2, 16)),
-            pltpu.SemaphoreType.DMA((2, 8)),
+            pltpu.SemaphoreType.DMA((2, 2, 2, 3, 4)),
+            pltpu.SemaphoreType.DMA((2, GROUP)),
+            pltpu.SemaphoreType.DMA((2, 4)),
             pltpu.SemaphoreType.DMA(()),
         ],
         compiler_params=pltpu.CompilerParams(
@@ -350,10 +345,7 @@
     own = [pltpu.make_async_copy(half(ins[a], a), own_slot(a), local.at[a]) for a in range(count)]
     for copy in own:
         copy.start()
-    barrier = pltpu.get_barrier_semaphore()
-    for there in [peer(bit) for bit in (1, 2, 4, 8)] + far:
-        pl.semaphore_signal(barrier, inc=1, device_id=there, device_id_type=MESH)
-    pl.semaphore_wait(barrier, 4 + len(far))
+    meet([peer(bit) for bit in (1, 2, 4, 8)] + far)
     started, waiting = [], []
     for k, there in enumerate(far):
         for a in range(count):
@@ -479,15 +471,12 @@
             )
             copy.start()
             loads.append(copy)
-    keep = pltpu.make_async_copy(pieces.at[rank % RANKS], whole.at[rank], own_sems)
+    place = dp % PLACES
+    slot = seq * PLACES + place
+    keep = pltpu.make_async_copy(pieces.at[place], whole.at[slot], own_sems)
     keep.start()
-    barrier = pltpu.get_barrier_semaphore()
-    everyone = [
-        {"seq": 1 - seq if mask & 8 else seq, "dp": flip_mask(dp, mask & 7)} for mask in range(1, 16)
-    ]
-    for there in everyone + far:
-        pl.semaphore_signal(barrier, inc=1, device_id=there, device_id_type=MESH)
-    pl.semaphore_wait(barrier, 15 + len(far))
+    masks = (1, 2, 4, 8, 3, 9, 10, 11)
+    meet([peer(mask) for mask in masks] + far)
 
     started = []
     live = {}
@@ -524,11 +513,11 @@
     def send_pieces(masks):
         for mask in masks:
             copy = pltpu.make_async_remote_copy(
-                src_ref=pieces.at[flip_mask(rank, mask) % RANKS],
-                dst_ref=whole.at[rank],
+                src_ref=pieces.at[flip_mask(place, mask & 3)],
+                dst_ref=whole.at[slot],
                 send_sem=piece_sems.at[0, mask],
                 recv_sem=piece_sems.at[1, mask],
-                device_id=everyone[mask - 1],
+                device_id=peer(mask),
                 device_id_type=MESH,
             )
             copy.start()
@@ -565,7 +554,7 @@
                             got[stage][a].at[index, :, :, columns],
                             order[stage],
                         )
-        send_pieces(((1, 2, 4, 8), (3, 5, 9, 6), (10, 12, 7), ())[stage])
+        send_pieces(((1, 2, 8), (9, 10), (3,), (11,))[stage])
     waiting = []
     for k, there in enumerate(far):
         for a in range(count):
@@ -579,7 +568,6 @@
             )
             copy.start()
             waiting.append(copy)
-    send_pieces((14, 11, 13, 15))
     for copy in waiting:
         copy.wait()
     last = []
@@ -626,7 +614,7 @@
     return pl.pallas_call(
         functools.partial(weights_reduce_kernel, count, groups_count),
         out_shape=[jax.ShapeDtypeStruct((rows, a.shape[1]), a.dtype) for a in arrays]
-        + [jax.ShapeDtypeStruct((EXPERTS,) + pieces.shape[1:], pieces.dtype)],
+        + [jax.ShapeDtypeStruct((GROUP,) + pieces.shape[1:], pieces.dtype)],
         in_specs=[any_space] * count + [vmem],
         out_specs=[vmem] * count + [any_space],
         scratch_shapes=buffers(8) + buffers(8) + buffers(4) + buffers(2) + buffers(1) + far_buffers
@@ -647,20 +635,25 @@
 
 
 def expert_kernel(
-    rows_ref, grad_ref, gate_ref, gate_up_ref, down_ref,
+    first, rows_ref, grad_ref, gate_ref, weights_ref,
     mixed_ref, normed_ref, gate_grad_ref, weights_out,
-    gate_up_sum, down_sum,
+    gate_up_sum, down_sum, mixed_sum, normed_sum,
 ):
     step = pl.program_id(0)
+    expert = pl.program_id(1)
     shards, each, width = rows_ref.shape
     count = shards * each
     rows = rows_ref[...].reshape(count, width)
     grad = grad_ref[...].reshape(count, width).astype(f32)
     gate = jnp.concatenate(
-        [jnp.broadcast_to(gate_ref[i], (128, each)).T[:, :1] for i in range(shards)], 0
+        [
+            jnp.broadcast_to(gate_ref[i, pl.ds(expert, 1)], (128, each)).T[:, :1]
+            for i in range(shards)
+        ],
+        0,
     )
-    down = down_ref[...]
-    gate_up_weight = gate_up_ref[...]
+    gate_up_weight = weights_ref[:, expert, :first].reshape(-1, width)
+    down = weights_ref[:, expert, first:].reshape(-1, width)
     gate_up = jnp.dot(rows, gate_up_weight, preferred_element_type=f32)
     gate_part, up_part = gate_up[:, :F], gate_up[:, F:]
     sigmoid = 1.0 / (1.0 + jnp.exp(-gate_part))
@@ -670,8 +663,8 @@
     inner = jnp.sum(out * grad, axis=-1, keepdims=True)
     for i in range(shards):
         line = jnp.broadcast_to(inner[i * each : (i + 1) * each], (each, 128)).T
-        gate_grad_ref[i] = line[:8]
-    mixed_ref[...] = (gate * out).astype(bf16).reshape(shards, each, width)
+        gate_grad_ref[i, pl.ds(expert, 1)] = line[:1]
+    mixed = gate * out
     expert_grad = (gate * grad).astype(bf16)
     across = (((1,), (1,)), ((), ()))
     over_rows = (((0,), (0,)), ((), ()))
@@ -679,64 +672,75 @@
     gate_up_grad = jnp.concatenate(
         [act_grad * up_part * (sigmoid * (1.0 + gate_part * (1.0 - sigmoid))), act_grad * silu], -1
     ).astype(bf16)
-    normed_ref[...] = (
-        lax.dot_general(gate_up_grad, gate_up_weight, across, preferred_element_type=f32)
-        .astype(bf16)
-        .reshape(shards, each, width)
-    )
+    normed = lax.dot_general(gate_up_grad, gate_up_weight, across, preferred_element_type=f32)
+
+    @pl.when(expert == 0)
+    def _():
+        mixed_sum[...] = mixed
+        normed_sum[...] = normed
+
+    @pl.when(expert > 0)
+    def _():
+        mixed_sum[...] += mixed
+        normed_sum[...] += normed
+
+    @pl.when(expert == OWN - 1)
+    def _():
+        mixed_ref[...] = mixed_sum[...].astype(bf16).reshape(shards, each, width)
+        normed_ref[...] = normed_sum[...].astype(bf16).reshape(shards, each, width)
 
     @pl.when(step == 0)
     def _():
-        gate_up_sum[...] = jnp.zeros_like(gate_up_sum)
-        down_sum[...] = jnp.zeros_like(down_sum)
-
-    down_sum[...] += lax.dot_general(act, expert_grad, over_rows, preferred_element_type=f32)
-    gate_up_sum[...] += lax.dot_general(rows, gate_up_grad, over_rows, preferred_element_type=f32)
+        gate_up_sum[expert] = jnp.zeros_like(gate_up_sum[0])
+        down_sum[expert] = jnp.zeros_like(down_sum[0])
+
+    down_sum[expert] += lax.dot_general(act, expert_grad, over_rows, preferred_element_type=f32)
+    gate_up_sum[expert] += lax.dot_general(rows, gate_up_grad, over_rows, preferred_element_type=f32)
 
     @pl.when(step == pl.num_programs(0) - 1)
     def _():
-        owners, _, columns = weights_out.shape
-        first = gate_up_sum.shape[0] // owners
-        weights_out[:, :first] = gate_up_sum[...].astype(bf16).reshape(owners, first, columns)
-        weights_out[:, first:] = down_sum[...].astype(bf16).reshape(owners, -1, columns)
-
-
-def expert_layer(n_dp, rows, grad, gate, gate_up_weight, down_weight):
-    packed = (n_dp, (gate_up_weight.shape[0] + down_weight.shape[0]) // n_dp, rows.shape[2])
+        owners = weights_out.shape[0]
+        weights_out[:, expert, :first] = gate_up_sum[expert].astype(bf16).reshape(owners, first, width)
+        weights_out[:, expert, first:] = down_sum[expert].astype(bf16).reshape(owners, -1, width)
+
+
+def expert_layer(first, rows, grad, gate, weights):
     each, width = rows.shape[1:]
     shards = 2
-    tile = pl.BlockSpec((shards, each, width), lambda i: (i, 0, 0))
-    whole = lambda shape: pl.BlockSpec(shape, lambda i: (0, 0))
+    owners = weights.shape[0]
+    tile = pl.BlockSpec((shards, each, width), lambda i, e: (i, 0, 0))
+    whole = pl.BlockSpec(weights.shape, lambda i, e: (0, 0, 0, 0), pipeline_mode=pl.Buffered(1))
     return pl.pallas_call(
-        expert_kernel,
-        grid=(GROUP // shards,),
+        functools.partial(expert_kernel, first),
+        grid=(GROUP // shards, OWN),
         out_shape=[
             jax.ShapeDtypeStruct(rows.shape, bf16),
             jax.ShapeDtypeStruct(rows.shape, bf16),
             jax.ShapeDtypeStruct((GROUP, 8, each), f32),
-            jax.ShapeDtypeStruct(packed, bf16),
+            jax.ShapeDtypeStruct(weights.shape, bf16),
         ],
         in_specs=[
             tile,
             tile,
-            pl.BlockSpec((shards, 1, each), lambda i: (i, 0, 0)),
-            whole(gate_up_weight.shape),
-            whole(down_weight.shape),
+            pl.BlockSpec((shards, OWN, each), lambda i, e: (i, 0, 0)),
+            whole,
         ],
         out_specs=[
             tile,
             tile,
-            pl.BlockSpec((shards, 8, each), lambda i: (i, 0, 0)),
-            pl.BlockSpec(packed, lambda i: (0, 0, 0)),
+            pl.BlockSpec((shards, 8, each), lambda i, e: (i, 0, 0)),
+            whole,
         ],
         scratch_shapes=[
-            pltpu.VMEM(gate_up_weight.shape, f32),
-            pltpu.VMEM(down_weight.shape, f32),
-        ],
-        compiler_params=pltpu.CompilerParams(vmem_limit_bytes=56 * 2**20),
+            pltpu.VMEM((OWN, owners * first, width), f32),
+            pltpu.VMEM((OWN, owners * (weights.shape[2] - first), width), f32),
+            pltpu.VMEM((shards * each, width), f32),
+            pltpu.VMEM((shards * each, width), f32),
+        ],
+        compiler_params=pltpu.CompilerParams(vmem_limit_bytes=62 * 2**20),
         cost_estimate=pl.CostEstimate(flops=45000000000, bytes_accessed=2**24, transcendentals=0),
         name="expert_layer",
-    )(rows, grad, gate, gate_up_weight, down_weight)
+    )(rows, grad, gate, weights)
 
 
 def inverse_rms(rows):
@@ -774,22 +778,21 @@
 
 def make_body(n_dp):
     groups_count = n_dp // RANKS
-    inside = [[g * RANKS + j for j in range(RANKS)] for g in range(groups_count)]
+    expert_groups = n_dp // PLACES
+    inside = [[g * PLACES + j for j in range(PLACES)] for g in range(expert_groups)]
+    between = [[g * PLACES + j for g in range(expert_groups)] for j in range(PLACES)]
     half_experts = EXPERTS // 2
 
-    between = [[g * RANKS + j for g in range(groups_count)] for j in range(RANKS)]
-
-    def expert_half(w, seq_rank):
-        return lax.dynamic_slice_in_dim(w, seq_rank * half_experts, half_experts, axis=1)
-
-    def expert_weights(halves, first):
-        mine = halves.transpose(2, 0, 1, 3)
-        mine = lax.all_to_all(
+    def expert_pieces(gate_up_shard, down_shard, seq_rank):
+        mine = [
+            jnp.swapaxes(lax.dynamic_slice_in_dim(w, seq_rank * half_experts, half_experts, axis=1), 0, 1)
+            for w in (gate_up_shard, down_shard)
+        ]
+        mine = jnp.concatenate(mine, 1)
+        mine = mine.reshape((PLACES, OWN) + mine.shape[1:])
+        return lax.all_to_all(
             mine, "dp", split_axis=0, concat_axis=0, tiled=True, axis_index_groups=inside
         )
-        mine = jnp.swapaxes(mine, 0, 1)
-        width = mine.shape[-1]
-        return mine[:, :, :first].reshape(-1, width), mine[:, :, first:].reshape(-1, width)
 
     def body(
         tokens, starts, routes, gain_one, query_key_value_weight, w_out,
@@ -797,16 +800,13 @@
     ):
         count = tokens.shape[1]
         seq_rank = lax.axis_index("seq")
-        expert = seq_rank * RANKS + lax.axis_index("dp") % RANKS
+        expert = (seq_rank * PLACES + lax.axis_index("dp") % PLACES) * OWN
         query_columns = QUERY_HEADS * HEAD_SIZE
         key_columns = KEY_VALUE_HEADS * HEAD_SIZE
         group = QUERY_HEADS // KEY_VALUE_HEADS
         forward_pair, back_pair = [(0, 1)], [(1, 0)]
 
-        expert_halves = lax.all_gather(
-            jnp.concatenate([expert_half(w_gate_up, seq_rank), expert_half(w_down, seq_rank)], 0),
-            "dp", axis=0, axis_index_groups=between,
-        )
+        mine = expert_pieces(w_gate_up, w_down, seq_rank)
         tokens_before = lax.ppermute(tokens[0], "seq", forward_pair)
         starts_before = lax.ppermute(starts, "seq", forward_pair)
         spare = lambda value: jnp.pad(value, ((0, 0), (0, 128 - value.shape[1])))
@@ -819,6 +819,10 @@
                 [spare(w_router), spare(jnp.stack([gain_one, gain_two], 1))], 1
             ),
         )
+        mine, qkv_weight, out_weight, small = lax.optimization_barrier(
+            (mine, qkv_weight, out_weight, small)
+        )
+        weights = lax.all_gather(mine, "dp", axis=0, tiled=True, axis_index_groups=between)
         router_weight = small[:, :EXPERTS]
         gain_a = small[:, 128].astype(f32)
         gain_b = small[:, 129].astype(f32)
@@ -855,8 +859,7 @@
         top = jnp.max(scores, axis=-1, keepdims=True)
         exps = jnp.exp(scores - top)
         probs = exps / jnp.sum(exps, axis=-1, keepdims=True)
-        probs_low, expert_halves = lax.optimization_barrier((probs.astype(bf16), expert_halves))
-        gate_up_weight, down_weight = expert_weights(expert_halves, w_gate_up.shape[0])
+        probs_low = probs.astype(bf16)
         attended = jnp.einsum(
             "grqk,kgd->qgrd", probs_low, values, preferred_element_type=f32
         ).reshape(count, query_columns).astype(bf16)
@@ -867,19 +870,16 @@
         chosen = jnp.any(routes[0][:, :, None] == expert_ids[None, None, :], axis=1)
         gates = jax.nn.softmax(jnp.where(chosen, logits, -jnp.inf), axis=-1)
 
-        normed_two, gate_up_weight, down_weight = lax.optimization_barrier(
-            (normed_two, gate_up_weight, down_weight)
-        )
         rows_in, gates_all, grad_all = group_gather(1, normed_two, gates.T, cotangent[0])
-        gate = lax.dynamic_slice_in_dim(gates_all, expert, 1, axis=1)
+        gate = lax.dynamic_slice_in_dim(gates_all, expert, OWN, axis=1)
         mixed_part, normed_part, gate_grad_part, expert_wgrads = expert_layer(
-            n_dp, rows_in, grad_all, gate, gate_up_weight, down_weight
+            w_gate_up.shape[0], rows_in, grad_all, gate, weights
         )
         expert_grads = lax.psum_scatter(
             expert_wgrads, "dp", scatter_dimension=0, tiled=True, axis_index_groups=between
         )
         mixed, normed_grad, gate_grad = group_reduce(2, mixed_part, normed_part, gate_grad_part)
-        gate_grad = gate_grad[:, 0].T
+        gate_grad = gate_grad[:, :OWN].reshape(EXPERTS, count).T
 
         over_rows = (((0,), (0,)), ((), ()))
         output = (hidden + mixed).astype(bf16)[None]
@@ -897,7 +897,6 @@
             branch_low, out_weight, (((1,), (1,)), ((), ())), preferred_element_type=f32
         ).astype(bf16).reshape(count, KEY_VALUE_HEADS, group, HEAD_SIZE)
 
-        attended_grad, expert_grads = lax.optimization_barrier((attended_grad, expert_grads))
         prob_grad = jnp.einsum("qgrd,kgd->grqk", attended_grad, values, preferred_element_type=f32)
         delta = jnp.sum(probs * prob_grad, axis=-1, keepdims=True)
         score_grad = (probs * (prob_grad - delta)).astype(bf16)
@@ -935,6 +934,7 @@
             (qkv_wgrad.astype(bf16), out_wgrad.astype(bf16), little),
             expert_grads,
         )
+        experts_all = experts_all.reshape((EXPERTS,) + experts_all.shape[2:])
         stat_sums = stat_sums + lax.ppermute(stat_sums, "seq", [(0, 1), (1, 0)])
         first = w_gate_up.shape[0]
         stream_rms = jnp.sqrt(stat_sums / (both * MODEL_WIDTH)).reshape(1, 2)

time: 589 us -> 478 us (0.81)
  Pallas kernels: 413 us -> 276 us
  waiting for transfers between devices: 40 us -> 77.2 us
  local copies, waits for them, and re-layouts: 33.5 us -> 21.4 us
    pallas_call x1, Pallas kernels: 108 us -> 45.2 us  [group_reduce(): pl.pallas_call(reduce_kernel, out_shape=[jax.ShapeDtypeStruct((rows, widt...]
    all_gather x1, waiting for transfers between devices: 0.01 us -> 53.5 us  [body(): lax.all_gather(mine, 'dp', axis=0, tiled=True, axis_index_groups=between)]
    pallas_call x1, Pallas kernels: 97.3 us -> 45.4 us  [weights_gather(): pl.pallas_call(functools.partial(weights_gather_kernel, count, groups_cou...]
    all_to_all x1, waiting for transfers between devices: 27.4 us -> 0.01 us  [expert_pieces(): lax.all_to_all(mine, 'dp', split_axis=0, concat_axis=0, tiled=True, axis_...]
    pallas_call x1, Pallas kernels: 71 us -> 44.5 us  [group_gather(): pl.pallas_call(functools.partial(gather_kernel, count), out_shape=[jax.Sh...]
    reduce_scatter x1, waiting for transfers between devices: 0.01 us -> 12.9 us  [body(): lax.psum_scatter(expert_wgrads, 'dp', scatter_dimension=0, tiled=True, ax...]
    unnamed x124 -> x118, local copies, waits for them, and re-layouts: 14.3 us -> 6.17 us
    pallas_call x1, Pallas kernels: 49.8 us -> 56.2 us  [expert_layer(): pl.pallas_call(functools.partial(expert_kernel, first), grid=(GROUP // sh...]
  transfers between devices with their start and end apart: 7 -> 7, of which waited for: 2 -> 3; matrix products, arithmetic and copies ran while one was open for 8% -> 12% of each run, Pallas kernels for 35% -> 29%
where the time goes in v7:
time: 478 us; the launch traced here: 471 us
  Pallas kernels  276 us (58%)
  waiting for transfers between devices  77.2 us (16%)
  matrix products  37.1 us (8%)
  other arithmetic  29.4 us (6%)
  local copies, waits for them, and re-layouts  21.4 us (4%)
  between operations  15.6 us (3%)
  starting transfers between devices  13.7 us (3%)
    pallas_call x1, Pallas kernels, weights_reduce(): pl.pallas_call(functools.partial(weights_reduce_kernel, count, groups_cou...  85.2 us
    pallas_call x1, Pallas kernels, expert_layer(): pl.pallas_call(functools.partial(expert_kernel, first), grid=(GROUP // sh...  56.2 us
    all_gather x1, waiting for transfers between devices, body(): lax.all_gather(mine, 'dp', axis=0, tiled=True, axis_index_groups=between)  53.5 us
    pallas_call x1, Pallas kernels, weights_gather(): pl.pallas_call(functools.partial(weights_gather_kernel, count, groups_cou...  45.4 us
    pallas_call x1, Pallas kernels, group_reduce(): pl.pallas_call(reduce_kernel, out_shape=[jax.ShapeDtypeStruct((rows, widt...  45.2 us
    pallas_call x1, Pallas kernels, group_gather(): pl.pallas_call(functools.partial(gather_kernel, count), out_shape=[jax.Sh...  44.5 us
    reduce_scatter x1, waiting for transfers between devices, body(): lax.psum_scatter(expert_wgrads, 'dp', scatter_dimension=0, tiled=True, ax...  12.9 us
    ppermute x1, waiting for transfers between devices, body(): kv_back = lax.ppermute(kv_grad[:count].astype(bf16), 'seq', back_pair)  10.8 us
  transfers between devices with their start and end apart: 7, of which 3 were waited for; matrix products, arithmetic and copies ran while one was open for 12% of the time, Pallas kernels for 29%

profile of v7, /device:TPU:0, one launch (start us, length us, event | category | flops | bytes accessed | tf_op | source)
XLA Modules:
  0.0 470.9 jit_solution(14708052907713439546)
XLA Ops:
  7.2 1.4 dynamic-slice_bitcast_fusion
  9.0 2.0 copy.83
  11.0 4.4 all-to-all-start
  15.4 5.7 %collective-permute-start = (bf16[256,1024]{1,0:T(8,128)(2,1)S(1)}, bf16[256,1024]{1,0:T(8,128)(2,1)}, u32[]{:S(2)}, u32[]{:S(2)}) collective-permute-start(bf16[256,1024]{1,0:T(8,128)(2,1)S(1)} %bitcast.160), channel_id=1, source_target_pairs={{0,16},{1,17},{2,18},{3,19},{4,20},{5,21},{6,22},{7,23},{8,24},{9,... | collective-permute-start | bytes 1572872 | tf_op jit(solution)/shard_map/ppermute | solution.py:810
  21.1 1.3 collective-permute-start.1
  23.0 0.6 multiply_multiply_fusion
  23.6 0.6 fusion.60.refs_2_
  24.2 45.4 %weights_gather.1 = (bf16[2,8,64,2048]{3,2,1,0:T(8,128)(2,1)}, bf16[2,8,64,1024]{3,2,1,0:T(8,128)(2,1)}, bf16[2,8,64,256]{3,2,1,0:T(8,128)(2,1)}) custom-call(bf16[64,2048]{1,0:T(8,128)(2,1)} %refs_0_.1, bf16[64,1024]{1,0:T(8,128)(2,1)} %refs_1_.1, bf16[64,256]{1,0:T(8,128)(2,1)} %fusion.60.refs_2_), custom_call_target="tpu_custom_call" | custom-call | flops 44999999488 | bytes 16777216 | tf_op jit(solution)/shard_map/weights_gather/pallas_call | solution.py:410
  70.3 0.8 fusion.47
  71.0 1.1 convert_element_type.145
  72.4 1.0 copy.86
  73.4 0.9 slice_convert_fusion.2
  74.6 3.1 fusion.12
  77.7 1.3 fusion.14
  79.0 1.1 slice.129
  80.1 1.0 slice_negate_fusion.1
  81.2 1.6 copy.88
  82.7 1.0 copy.87
  84.1 1.4 fusion.37
  85.8 6.2 %fusion.78 = (f32[8,2,256]{2,1,0:T(2,128)S(1)}, f32[8,2,256,512]{2,3,1,0:T(8,128)}) fusion(pred[256,512]{0,1:T(8,128)(4,1)} %fusion.47, bf16[512,8,64,1]{0,2,3,1:T(8,128)(2,1)S(1)} %fusion.44, bf16[256,8,2,64]{0,3,2,1:T(8,128)(2,1)S(1)} %fusion.37), kind=kOutput, calls=%fused_computation.167 | convolution fusion | flops 276824576 | bytes 9584640 | tf_op jit(solution)/shard_map/sub | solution.py:860
  92.1 5.2 %fusion.17 = bf16[8,64,2,256]{3,1,2,0:T(8,128)(2,1)S(1)} fusion(bf16[512,8,64,1]{0,2,3,1:T(8,128)(2,1)S(1)} %bitcast.179, f32[8,2,256,512]{2,3,1,0:T(8,128)} %get-tuple-element.121, f32[8,2,256]{2,1,0:T(2,128)S(1)} %get-tuple-element.120), kind=kOutput, calls=%fused_computation.40 | convolution fusion | flops 272891904 | bytes 9453568 | tf_op jit(solution)/shard_map/grqk,kgd->qgrd/dot_general | solution.py:863
  97.3 0.8 multiply_reduce_fusion.5
  98.2 0.6 multiply_multiply_fusion.1
  98.8 0.6 copy-done.44
  99.9 0.6 copy-done.26
  100.4 0.6 fusion.75.refs_1_
  101.0 44.5 %group_gather.1 = (bf16[8,256,1024]{2,1,0:T(8,128)(2,1)}, f32[8,16,256]{2,1,0:T(8,128)}, bf16[8,256,1024]{2,1,0:T(8,128)(2,1)}) custom-call(bf16[256,1024]{1,0:T(8,128)(2,1)} %copy-done.10, f32[16,256]{1,0:T(8,128)} %fusion.75.refs_1_, bf16[256,1024]{1,0:T(8,128)(2,1)} %bitcast.178), custom_call_target="tpu_custom_call" | custom-call | flops 60000002048 | bytes 16777216 | tf_op jit(solution)/shard_map/group_gather/pallas_call | solution.py:139
  145.6 1.5 constant_dynamic-slice_fusion.gate_ref
  147.0 53.5 %all-gather.2.cloned.1.call-done.weights_ref = bf16[16,2,96,1024]{3,2,1,0:T(8,128)(2,1)} async-done(((bf16[4,2,96,1024]{3,2,1,0:T(8,128)(2,1)}), bf16[16,2,96,1024]{3,2,1,0:T(8,128)(2,1)}) %all-gather.2.cloned.1.call-update) | async-done | bytes 6291472 | tf_op jit(solution)/shard_map/all_gather | solution.py:825
  200.5 56.2 %expert_layer.1 = (bf16[8,256,1024]{2,1,0:T(8,128)(2,1)}, bf16[8,256,1024]{2,1,0:T(8,128)(2,1)}, f32[8,8,256]{2,1,0:T(8,128)}, bf16[16,2,96,1024]{3,2,1,0:T(8,128)(2,1)}) custom-call(bf16[8,256,1024]{2,1,0:T(8,128)(2,1)} %get-tuple-element.37.rows_ref, bf16[8,256,1024]{2,1,0:T(8,128)(2,1)} %get-tuple-element.38.grad_ref, ...), custom_call_target="tpu_custom_call" | custom-call | flops 44999999488 | bytes 16777216 | tf_op jit(solution)/shard_map/expert_layer/pallas_call | solution.py:713
  256.7 0.8 copy-done.3
  257.6 45.2 %group_reduce.1 = (f32[256,1024]{1,0:T(8,128)S(1)}, f32[256,1024]{1,0:T(8,128)S(1)}, f32[8,8,256]{2,1,0:T(8,128)S(1)}) custom-call(bf16[8,256,1024]{2,1,0:T(8,128)(2,1)} %get-tuple-element.41.mixed_ref, bf16[8,256,1024]{2,1,0:T(8,128)(2,1)} %get-tuple-element.42.normed_ref, f32[8,8,256]{2,1,0:T(8,128)S(1)} %copy-done.3), custom_call_target="tpu_custom_call" | custom-call | flops 70000001024 | bytes 16777216 | tf_op jit(solution)/shard_map/group_reduce/pallas_call | solution.py:267
  303.0 3.0 multiply_reduce_fusion.2
  306.0 3.3 multiply_reduce_fusion.1
  309.3 1.4 pad_maximum_fusion.11
  310.7 0.5 collective-permute-start.3
  311.2 0.8 convolution_convert_fusion.2
  312.3 4.9 %fusion.1 = (f32[8,2,256]{2,1,0:T(2,128)S(1)}, f32[8,512,256,2]{2,1,3,0:T(8,128)S(1)}) fusion(f32[8,2,256,512]{2,3,1,0:T(8,128)} %get-tuple-element.121, f32[8,2,256]{2,1,0:T(2,128)S(1)} %copy-done.43, bf16[512,8,64,1]{0,2,3,1:T(8,128)(2,1)S(1)} %bitcast.180, bf16[256,8,2,64]{0,3,2,1:T(8,128)(2,1)S(1)} %bitcast.181), kind=kOutput, calls=%fused_computation.3 | convolution fusion | flops 274722816 | bytes 17858560 | tf_op jit(solution)/shard_map/qgrd,kgd->grqk/dot_general | solution.py:900
  317.2 1.0 slice-done.1
  318.1 1.5 fusion.3
  319.7 0.8 fusion.21
  320.8 0.6 copy-done.25
  321.6 1.4 fusion.16
  323.0 1.4 fusion.8
  324.5 1.5 collective-permute-start.2
  326.4 0.7 convolution_convert_fusion.1
  327.1 1.9 sqrt_bitcast_fusion
  329.0 10.8 %collective-permute-done.2 = bf16[256,1024]{0,1:T(8,128)(2,1)S(1)} collective-permute-done((bf16[256,1024]{0,1:T(8,128)(2,1)S(1)}, bf16[256,1024]{0,1:T(8,128)(2,1)S(1)}, u32[]{:S(2)}, u32[]{:S(2)}) %collective-permute-start.2) | collective-permute-done | bytes 524320 | tf_op jit(solution)/shard_map/ppermute | solution.py:913
  340.4 2.4 fusion.29
  342.8 1.1 select_maximum_fusion
  343.9 1.6 copy.97
  345.5 2.8 fusion.45
  348.3 4.7 convolution_convert_fusion
  353.0 12.9 %reduce-scatter.2.cloned.1.call-done.refs_3_ = bf16[4,2,96,1024]{3,2,1,0:T(8,128)(2,1)} async-done(((bf16[16,2,96,1024]{3,2,1,0:T(8,128)(2,1)}), bf16[4,2,96,1024]{3,2,1,0:T(8,128)(2,1)}) %reduce-scatter.2.cloned.1.call-update) | async-done | bytes 1572880 | tf_op jit(solution)/shard_map/reduce_scatter | solution.py:878
  365.8 1.4 copy-done.2
  367.3 85.2 %weights_reduce.1 = (bf16[64,2048]{1,0:T(8,128)(2,1)S(1)}, bf16[64,1024]{1,0:T(8,128)(2,1)S(1)}, f32[64,256]{1,0:T(8,128)S(1)}, bf16[8,2,96,1024]{3,2,1,0:T(8,128)(2,1)}) custom-call(bf16[2,8,64,2048]{3,2,1,0:T(8,128)(2,1)} %bitcast.199, bf16[2,8,64,1024]{3,2,1,0:T(8,128)(2,1)S(1)} %bitcast.152, f32[2,8,64,256]{3,2,1,0:T(8,128)S(1)} %bitcast.153, ...), custom_call_target="tpu_custom_call" | custom-call | flops 80000000000 | bytes 16777216 | tf_op jit(solution)/shard_map/weights_reduce/pallas_call | solution.py:614
  452.4 1.8 slice.148
  454.2 1.3 slice.149
  455.5 0.7 slice_reduce_fusion
  456.2 3.2 convert_bitcast_fusion
  459.4 1.9 convert_bitcast_fusion.1
  461.4 0.8 convert_element_type.175
  462.2 0.7 convert_element_type.176
  462.9 0.7 copy.100
  (166 shorter events, 5.0 us)
Async XLA Ops:
  7.2 1.5 copy-start
  8.8 6.6 %copy-start.6 = (bf16[1,256,1024]{2,1,0:T(8,128)(2,1)S(1)}, bf16[1,256,1024]{2,1,0:T(8,128)(2,1)}, u32[]{:S(2)}) copy-start(bf16[1,256,1024]{2,1,0:T(8,128)(2,1)} %param.11) | copy-start | bytes 1572868
  8.8 12.3 %copy-start.51 = (s32[1,256]{1,0:T(1,128)S(1)}, s32[1,256]{1,0:T(1,128)}, u32[]{:S(2)}) copy-start(s32[1,256]{1,0:T(1,128)} %param.12) | copy-start | bytes 3076
  8.9 13.8 %copy-start.52 = (bf16[64]{0:T(256)(128)(2,1)S(1)}, bf16[64]{0:T(256)(128)(2,1)}, u32[]{:S(2)}) copy-start(bf16[64]{0:T(256)(128)(2,1)} %param.17) | copy-start | bytes 388
  8.9 13.8 %copy-start.53 = (bf16[64]{0:T(256)(128)(2,1)S(1)}, bf16[64]{0:T(256)(128)(2,1)}, u32[]{:S(2)}) copy-start(bf16[64]{0:T(256)(128)(2,1)} %param.14) | copy-start | bytes 388
  9.0 13.9 %copy-start.50 = (bf16[64,16]{0,1:T(8,128)(2,1)S(1)}, bf16[64,16]{0,1:T(8,128)(2,1)}, u32[]{:S(2)}) copy-start(bf16[64,16]{0,1:T(8,128)(2,1)} %param.18) | copy-start | bytes 6148
  9.0 14.0 %copy-start.46 = (s32[1,256,8]{1,2,0:T(8,128)S(1)}, s32[1,256,8]{1,2,0:T(8,128)}, u32[]{:S(2)}) copy-start(s32[1,256,8]{1,2,0:T(8,128)} %param.13) | copy-start | bytes 24580
  11.0 61.4 %all-to-all-start = ((bf16[4,2,96,1024]{3,2,1,0:T(8,128)(2,1)}), bf16[4,2,96,1024]{3,2,1,0:T(8,128)(2,1)}, u32[]{:S(2)}, u32[]{:S(2)}) async-start(bf16[4,2,96,1024]{3,2,1,0:T(8,128)(2,1)} %bitcast.163), calls=%async_computation | async-start | bytes 3145728 | tf_op jit(solution)/shard_map/all_to_all | solution.py:793
  15.4 185.2 %all-gather.2.cloned.1.call-start = ((), (), s32[]{:S(2)}) async-start(), calls=%async_computation.2 | async-start | bytes 7864320 | tf_op jit(solution)/shard_map/all_gather | solution.py:825
  15.4 55.6 %collective-permute-start = (bf16[256,1024]{1,0:T(8,128)(2,1)S(1)}, bf16[256,1024]{1,0:T(8,128)(2,1)}, u32[]{:S(2)}, u32[]{:S(2)}) collective-permute-start(bf16[256,1024]{1,0:T(8,128)(2,1)S(1)} %bitcast.160), channel_id=1, source_target_pairs={{0,16},{1,17},{2,18},{3,19},{4,20},{5,21},{6,22},{7,23},{8,24},{9,... | collective-permute-start | bytes 1572872 | tf_op jit(solution)/shard_map/ppermute | solution.py:810
  21.1 48.5 %collective-permute-start.1 = (s32[1,256]{1,0:T(1,128)S(1)}, s32[1,256]{1,0:T(1,128)S(1)}, u32[]{:S(2)}, u32[]{:S(2)}) collective-permute-start(s32[1,256]{1,0:T(1,128)S(1)} %copy-done.51), channel_id=1, source_target_pairs={{0,16},{1,17},{2,18},{3,19},{4,20},{5,21},{6,22},{7,23},{8,24},{9,... | collective-permute-start | bytes 3080 | tf_op jit(solution)/shard_map/ppermute | solution.py:811
  23.0 76.5 %copy-start.32 = (pred[256,16]{0,1:T(8,128)(4,1)}, pred[256,16]{0,1:T(8,128)(4,1)S(1)}, u32[]{:S(2)}) copy-start(pred[256,16]{0,1:T(8,128)(4,1)S(1)} %fusion.55) | copy-start | bytes 12292
  69.6 2.8 copy-start.16
  70.2 13.9 %copy-start.21 = (f32[256,64]{0,1:T(8,128)}, f32[256,64]{0,1:T(8,128)S(1)}, u32[]{:S(2)}) copy-start(f32[256,64]{0,1:T(8,128)S(1)} %get-tuple-element.132) | copy-start | bytes 196612
  70.2 13.9 %copy-start.24 = (f32[256,64]{0,1:T(8,128)}, f32[256,64]{0,1:T(8,128)S(1)}, u32[]{:S(2)}) copy-start(f32[256,64]{0,1:T(8,128)S(1)} %get-tuple-element.133) | copy-start | bytes 196612
  73.4 4.2 copy-start.54
  74.3 4.6 copy-start.36
  74.3 24.4 %copy-start.34 = (f32[1024,1]{0,1:T(1,128)}, f32[1024,1]{0,1:T(1,128)S(1)}, u32[]{:S(2)}) copy-start(f32[1024,1]{0,1:T(1,128)S(1)} %get-tuple-element.112) | copy-start | bytes 12292
  74.6 4.4 copy-start.23
  83.7 282.1 %reduce-scatter.2.cloned.1.call-start = ((), (), s32[]{:S(2)}) async-start(), calls=%async_computation.3 | async-start | bytes 7864320 | tf_op jit(solution)/shard_map/reduce_scatter | solution.py:878
  85.5 6.6 %copy-start.19 = (bf16[256,8,2,64]{0,3,2,1:T(8,128)(2,1)}, bf16[256,8,2,64]{0,3,2,1:T(8,128)(2,1)S(1)}, u32[]{:S(2)}) copy-start(bf16[256,8,2,64]{0,3,2,1:T(8,128)(2,1)S(1)} %fusion.37) | copy-start | bytes 1572868
  85.8 6.3 %copy-start.12 = (bf16[512,8,64,1]{0,2,3,1:T(8,128)(2,1)}, bf16[512,8,64,1]{0,2,3,1:T(8,128)(2,1)S(1)}, u32[]{:S(2)}) copy-start(bf16[512,8,64,1]{0,2,3,1:T(8,128)(2,1)S(1)} %fusion.44) | copy-start | bytes 1572868
  85.8 6.3 %copy-start.28 = (bf16[512,512]{0,1:T(8,128)(2,1)S(1)}, bf16[512,512]{0,1:T(8,128)(2,1)}, u32[]{:S(2)}) copy-start(bf16[512,512]{0,1:T(8,128)(2,1)} %copy.87) | copy-start | bytes 1572868
  92.1 5.2 %copy-start.42 = (f32[8,2,256]{2,1,0:T(2,128)}, f32[8,2,256]{2,1,0:T(2,128)S(1)}, u32[]{:S(2)}) copy-start(f32[8,2,256]{2,1,0:T(2,128)S(1)} %get-tuple-element.120) | copy-start | bytes 49156
  92.1 5.2 %copy-start.8 = (bf16[2,8,64,1024]{3,2,1,0:T(8,128)(2,1)S(1)}, bf16[2,8,64,1024]{3,2,1,0:T(8,128)(2,1)}, u32[]{:S(2)}) copy-start(bf16[2,8,64,1024]{3,2,1,0:T(8,128)(2,1)} %get-tuple-element.32) | copy-start | bytes 6291460
  97.3 1.5 copy-start.14
  97.3 2.2 copy-start.17
  98.2 47.4 %copy-start.5 = (f32[256,1024]{1,0:T(8,128)}, f32[256,1024]{1,0:T(8,128)S(1)}, u32[]{:S(2)}) copy-start(f32[256,1024]{1,0:T(8,128)S(1)} %get-tuple-element.123) | copy-start | bytes 3145732
  99.5 1.5 copy-start.10
  99.8 0.6 copy-start.26
  99.8 45.7 %copy-start.38 = (f32[256]{0:T(256)}, f32[256]{0:T(256)S(1)}, u32[]{:S(2)}) copy-start(f32[256]{0:T(256)S(1)} %get-tuple-element.124) | copy-start | bytes 3076
  100.4 45.2 %copy-start.40 = (f32[256]{0:T(256)}, f32[256]{0:T(256)S(1)}, u32[]{:S(2)}) copy-start(f32[256]{0:T(256)S(1)} %fusion.63) | copy-start | bytes 3076
  256.7 0.8 copy-start.3
  257.5 45.3 %copy-start.27 = (f32[256,16]{0,1:T(8,128)S(1)}, f32[256,16]{0,1:T(8,128)}, u32[]{:S(2)}) copy-start(f32[256,16]{0,1:T(8,128)} %copy-done.26) | copy-start | bytes 49156
  257.5 45.3 %copy-start.33 = (pred[256,16]{0,1:T(8,128)(4,1)S(1)}, pred[256,16]{0,1:T(8,128)(4,1)}, u32[]{:S(2)}) copy-start(pred[256,16]{0,1:T(8,128)(4,1)} %copy-done.32) | copy-start | bytes 12292
  257.5 45.3 %copy-start.39 = (f32[256]{0:T(256)S(1)}, f32[256]{0:T(256)}, u32[]{:S(2)}) copy-start(f32[256]{0:T(256)} %copy-done.38) | copy-start | bytes 3076
  257.6 45.4 %copy-start.41 = (f32[256]{0:T(256)S(1)}, f32[256]{0:T(256)}, u32[]{:S(2)}) copy-start(f32[256]{0:T(256)} %copy-done.40) | copy-start | bytes 3076
  257.6 45.4 %copy-start.18 = (bf16[2,8,64,256]{3,2,1,0:T(8,128)(2,1)S(1)}, bf16[2,8,64,256]{3,2,1,0:T(8,128)(2,1)}, u32[]{:S(2)}) copy-start(bf16[2,8,64,256]{3,2,1,0:T(8,128)(2,1)} %get-tuple-element.33) | copy-start | bytes 1572868
  257.6 45.4 %copy-start.35 = (f32[1024,1]{0,1:T(1,128)S(1)}, f32[1024,1]{0,1:T(1,128)}, u32[]{:S(2)}) copy-start(f32[1024,1]{0,1:T(1,128)} %copy-done.34) | copy-start | bytes 12292
  257.6 45.4 %copy-start.45 = (f32[256]{0:T(256)S(1)}, f32[256]{0:T(256)}, u32[]{:S(2)}) copy-start(f32[256]{0:T(256)} %copy-done.44) | copy-start | bytes 3076
  257.6 48.4 %copy-start.49 = (f32[256]{0:T(256)S(1)}, f32[256]{0:T(256)}, u32[]{:S(2)}) copy-start(f32[256]{0:T(256)} %get-tuple-element.118) | copy-start | bytes 3076
  303.0 8.3 %copy-start.9 = (bf16[2,8,64,1024]{3,2,1,0:T(8,128)(2,1)S(1)}, bf16[2,8,64,1024]{3,2,1,0:T(8,128)(2,1)}, u32[]{:S(2)}) copy-start(bf16[2,8,64,1024]{3,2,1,0:T(8,128)(2,1)} %get-tuple-element.32) | copy-start | bytes 6291460
  306.0 6.3 %copy-start.29 = (bf16[512,512]{0,1:T(8,128)(2,1)S(1)}, bf16[512,512]{0,1:T(8,128)(2,1)}, u32[]{:S(2)}) copy-start(bf16[512,512]{0,1:T(8,128)(2,1)} %copy.87) | copy-start | bytes 1572868
  306.0 6.3 %copy-start.43 = (f32[8,2,256]{2,1,0:T(2,128)S(1)}, f32[8,2,256]{2,1,0:T(2,128)}, u32[]{:S(2)}) copy-start(f32[8,2,256]{2,1,0:T(2,128)} %copy-done.42) | copy-start | bytes 49156
  309.3 17.1 %copy-start.4 = (f32[256,1024]{1,0:T(8,128)}, f32[256,1024]{1,0:T(8,128)S(1)}, u32[]{:S(2)}) copy-start(f32[256,1024]{1,0:T(8,128)S(1)} %get-tuple-element.101) | copy-start | bytes 3145732
  310.7 16.4 %collective-permute-start.3 = (f32[2]{0:T(128)S(1)}, f32[2]{0:T(128)S(1)}, u32[]{:S(2)}, u32[]{:S(2)}) collective-permute-start(f32[2]{0:T(128)S(1)} %pad_maximum_fusion.11), channel_id=1, source_target_pairs={{0,16},{16,0},{1,17},{17,1},{2,18},{18,2},{3,19},{19,3},{4,20},{20... | collective-permute-start | bytes 32 | tf_op jit(solution)/shard_map/ppermute | solution.py:938
  312.2 5.0 %slice-start = ((s8[8388608]{0:T(1024)(128)(4,1)}), s8[4194304]{0:T(1024)(128)(4,1)S(1)}, s32[]{:S(2)}) async-start(s8[8388608]{0:T(1024)(128)(4,1)} %bitcast.158), calls=%async_computation.4 | async-start | bytes 8388608
  312.2 5.9 %slice-start.1 = ((s8[8388608]{0:T(1024)(128)(4,1)}), s8[4194304]{0:T(1024)(128)(4,1)S(1)}, s32[]{:S(2)}) async-start(s8[8388608]{0:T(1024)(128)(4,1)} %bitcast.158), calls=%async_computation.5 | async-start | bytes 8388608
  318.1 1.5 copy-start.13
  319.7 0.8 copy-start.22
  320.5 0.8 copy-start.25
  320.5 1.1 copy-start.20
  321.6 18.7 %copy-start.30 = (bf16[256,1024]{0,1:T(8,128)(2,1)}, bf16[256,1024]{0,1:T(8,128)(2,1)S(1)}, u32[]{:S(2)}) copy-start(bf16[256,1024]{0,1:T(8,128)(2,1)S(1)} %fusion.39) | copy-start | bytes 1572868
  323.0 3.1 copy-start.11
  323.0 3.4 copy-start.15
  324.5 15.4 %collective-permute-start.2 = (bf16[256,1024]{0,1:T(8,128)(2,1)S(1)}, bf16[256,1024]{0,1:T(8,128)(2,1)S(1)}, u32[]{:S(2)}, u32[]{:S(2)}) collective-permute-start(bf16[256,1024]{0,1:T(8,128)(2,1)S(1)} %fusion.33), channel_id=1, source_target_pairs={{16,0},{17,1},{18,2},{19,3},{20,4},{21,5},{22,6},{23,7},{24,8},{25... | collective-permute-start | bytes 1572872 | tf_op jit(solution)/shard_map/ppermute | solution.py:913
  329.0 11.4 %copy-start.7 = (bf16[1,256,1024]{2,1,0:T(8,128)(2,1)S(1)}, bf16[1,256,1024]{2,1,0:T(8,128)(2,1)}, u32[]{:S(2)}) copy-start(bf16[1,256,1024]{2,1,0:T(8,128)(2,1)} %param.11) | copy-start | bytes 1572868
  329.0 11.4 %copy-start.37 = (f32[1024,1]{0,1:T(1,128)S(1)}, f32[1024,1]{0,1:T(1,128)}, u32[]{:S(2)}) copy-start(f32[1024,1]{0,1:T(1,128)} %copy-done.36) | copy-start | bytes 12292
  329.0 11.4 %copy-start.48 = (f32[256]{0:T(256)S(1)}, f32[256]{0:T(256)}, u32[]{:S(2)}) copy-start(f32[256]{0:T(256)} %get-tuple-element.117) | copy-start | bytes 3076
  329.0 11.4 %copy-start.55 = (bf16[2,8,64,2048]{3,2,1,0:T(8,128)(2,1)S(1)}, bf16[2,8,64,2048]{3,2,1,0:T(8,128)(2,1)}, u32[]{:S(2)}) copy-start(bf16[2,8,64,2048]{3,2,1,0:T(8,128)(2,1)} %get-tuple-element.31) | copy-start | bytes 12582916
  340.3 2.4 copy-start.31
  342.8 2.7 copy-start.47
  365.8 1.4 copy-start.2
  455.5 8.1 %copy-start.1 = (bf16[32,16,1024]{2,1,0:T(8,128)(2,1)S(1)}, bf16[32,16,1024]{2,1,0:T(8,128)(2,1)}, u32[]{:S(2)}) copy-start(bf16[32,16,1024]{2,1,0:T(8,128)(2,1)} %param.20) | copy-start | bytes 3145732
  (1 other events, 0.6 us)
Sparse Core Ops, SparseCore 0:
  83.9 116.5 all-gather.1
  256.9 108.9 reduce-scatter.1

commit v8 on v7

--- a/solution.py
+++ b/solution.py
@@ -27,7 +27,8 @@
 bf16 = jnp.bfloat16
 MESH = pl.DeviceIdType.MESH
 
-LINKS = ((8, 4, 2), (4, 2, 8), (2, 8, 4))
+GATHER_LINKS = ((4, 8, 2), (4, 2, 8))
+SUM_LINKS = ((8, 2, 4), (2, 8, 4))
 TOKEN_LINKS = ((4, 2), (2, 4))
 
 
@@ -149,7 +150,7 @@
             pltpu.SemaphoreType.DMA((count,)),
         ],
         compiler_params=pltpu.CompilerParams(collective_id=collective_id, has_side_effects=True),
-        cost_estimate=pl.CostEstimate(flops=60000000000, bytes_accessed=2**24, transcendentals=0),
+        cost_estimate=pl.CostEstimate(flops=1000000000, bytes_accessed=2**24, transcendentals=0),
         name="group_gather",
     )(*arrays)
 
@@ -290,30 +291,18 @@
         compiler_params=pltpu.CompilerParams(
             collective_id=collective_id, has_side_effects=True, vmem_limit_bytes=48 * 2**20
         ),
-        cost_estimate=pl.CostEstimate(flops=70000000000, bytes_accessed=2**24, transcendentals=0),
+        cost_estimate=pl.CostEstimate(flops=1000000, bytes_accessed=2**24, transcendentals=0),
         name="group_reduce",
     )(mixed, normed, gate_grad)
 
 
-def column_parts(half, which):
-    tiles = half // 128
-    if tiles == 1:
-        sizes = (1, 0, 0)
-    elif which % 2 == 0:
-        big = -(-tiles // 3)
-        sizes = (big, big, tiles - 2 * big)
-    else:
-        small = tiles // 3
-        sizes = (small, small, tiles - 2 * small)
-    out, start = [], 0
-    for size in sizes:
-        out.append((start * 128, size * 128))
-        start += size
-    return out
+def column_parts(half):
+    first = -(-(half // 128) // 2) * 128
+    return ((0, first), (first, half - first))
 
 
 def shard_view(ref, halves, a, p, rank_value):
-    start, size = column_parts(halves[a], a)[p]
+    start, size = column_parts(halves[a])[p]
     offset = pl.multiple_of((rank_value // RANKS) * halves[a] + start, 128)
     return ref.at[:, rank_value % RANKS, :, pl.ds(offset, size)]
 
@@ -382,11 +371,11 @@
     live = {}
     last = []
     for step in range(4):
-        for p in range(3):
+        for p in range(2):
             for a in range(count):
-                if column_parts(halves[a], a)[p][1] == 0:
+                if column_parts(halves[a])[p][1] == 0:
                     continue
-                order = LINKS[p]
+                order = GATHER_LINKS[p]
                 if step > 0:
                     for copy in live.pop((a, p)):
                         copy.wait_recv()
@@ -415,8 +404,8 @@
         in_specs=[pl.BlockSpec(memory_space=pltpu.VMEM)] * count,
         out_specs=[pl.BlockSpec(memory_space=pl.ANY)] * count,
         scratch_shapes=[
-            pltpu.SemaphoreType.DMA((count, 3, 15)),
-            pltpu.SemaphoreType.DMA((count, 3, 15)),
+            pltpu.SemaphoreType.DMA((count, 2, 15)),
+            pltpu.SemaphoreType.DMA((count, 2, 15)),
             pltpu.SemaphoreType.DMA((max(groups_count - 1, 1), count)),
             pltpu.SemaphoreType.DMA((max(groups_count - 1, 1), count)),
             pltpu.SemaphoreType.DMA((count,)),
@@ -445,19 +434,17 @@
 
 def weights_reduce_kernel(count, groups_count, *refs):
     ins = refs[:count]
-    pieces = refs[count]
-    outs = refs[count + 1 : 2 * count + 1]
-    whole = refs[2 * count + 1]
-    rest = refs[2 * count + 2 :]
+    outs = refs[count : 2 * count]
+    rest = refs[2 * count :]
     total, got0, got1, got2, got3, far_got = [rest[i * count : (i + 1) * count] for i in range(6)]
-    sems, far_sems, seq_sems, piece_sems, local, own_sems = rest[6 * count :]
+    sems, far_sems, seq_sems, local = rest[6 * count :]
     rank, peer = my_place()
     chip, core = rank // 2, rank % 2
     home, far = other_groups(groups_count)
     seq = lax.axis_index("seq")
     dp = lax.axis_index("dp")
     halves = [ref.shape[3] // 2 for ref in ins]
-    parts = [column_parts(halves[a], a) for a in range(count)]
+    parts = [column_parts(halves[a]) for a in range(count)]
 
     def half_view(ref, a, rank_value):
         offset = pl.multiple_of((rank_value // RANKS) * halves[a], 128)
@@ -471,12 +458,7 @@
             )
             copy.start()
             loads.append(copy)
-    place = dp % PLACES
-    slot = seq * PLACES + place
-    keep = pltpu.make_async_copy(pieces.at[place], whole.at[slot], own_sems)
-    keep.start()
-    masks = (1, 2, 4, 8, 3, 9, 10, 11)
-    meet([peer(mask) for mask in masks] + far)
+    meet([peer(bit) for bit in (1, 2, 4, 8)] + far)
 
     started = []
     live = {}
@@ -497,7 +479,7 @@
     def chip_of(mask):
         return flip_mask(rank, mask) // 2
 
-    for p in range(3):
+    for p in range(2):
         for a in range(count):
             columns = pl.ds(*parts[a][p])
             if parts[a][p][1]:
@@ -508,31 +490,16 @@
                         got0[a].at[c, :, :, columns],
                         1,
                     )
-    arrivals = []
-
-    def send_pieces(masks):
-        for mask in masks:
-            copy = pltpu.make_async_remote_copy(
-                src_ref=pieces.at[flip_mask(place, mask & 3)],
-                dst_ref=whole.at[slot],
-                send_sem=piece_sems.at[0, mask],
-                recv_sem=piece_sems.at[1, mask],
-                device_id=peer(mask),
-                device_id_type=MESH,
-            )
-            copy.start()
-            arrivals.append(copy)
-
     for copy in loads:
         copy.wait()
     got = (got1, got2, got3)
     for stage in range(4):
-        for p in range(3):
+        for p in range(2):
             for a in range(count):
                 start, size = parts[a][p]
                 if size == 0:
                     continue
-                order = LINKS[p]
+                order = SUM_LINKS[p]
                 columns = pl.ds(start, size)
                 for copy in live.pop((a, p)):
                     copy.wait_recv()
@@ -554,7 +521,6 @@
                             got[stage][a].at[index, :, :, columns],
                             order[stage],
                         )
-        send_pieces(((1, 2, 8), (9, 10), (3,), (11,))[stage])
     waiting = []
     for k, there in enumerate(far):
         for a in range(count):
@@ -587,14 +553,53 @@
         )
         copy.start()
         last.append(copy)
-    for copy in last + arrivals:
+    for copy in last:
         copy.wait()
     for copy in started:
         copy.wait_send()
+
+
+def pieces_kernel(pieces, whole, send, recv, local):
+    rank, peer = my_place(PLACES)
+    place = rank % PLACES
+    keep = pltpu.make_async_copy(pieces.at[place], whole.at[rank], local)
+    keep.start()
+    masks = (6, 7, 2, 4, 3, 5, 1)
+    meet([peer(mask) for mask in masks])
+    copies = []
+    for mask in masks:
+        copy = pltpu.make_async_remote_copy(
+            src_ref=pieces.at[flip_mask(place, mask & (PLACES - 1))],
+            dst_ref=whole.at[rank],
+            send_sem=send.at[mask],
+            recv_sem=recv.at[mask],
+            device_id=peer(mask),
+            device_id_type=MESH,
+        )
+        copy.start()
+        copies.append(copy)
+    for copy in copies:
+        copy.wait()
     keep.wait()
 
 
-def weights_reduce(collective_id, groups_count, arrays, pieces):
+def send_pieces(collective_id, pieces):
+    return pl.pallas_call(
+        pieces_kernel,
+        out_shape=jax.ShapeDtypeStruct((GROUP,) + pieces.shape[1:], pieces.dtype),
+        in_specs=[pl.BlockSpec(memory_space=pltpu.VMEM)],
+        out_specs=pl.BlockSpec(memory_space=pl.ANY),
+        scratch_shapes=[
+            pltpu.SemaphoreType.DMA((GROUP,)),
+            pltpu.SemaphoreType.DMA((GROUP,)),
+            pltpu.SemaphoreType.DMA(()),
+        ],
+        compiler_params=pltpu.CompilerParams(collective_id=collective_id, has_side_effects=True),
+        name="send_pieces",
+    )(pieces)
+
+
+def weights_reduce(collective_id, groups_count, arrays):
     count = len(arrays)
     views = [a.reshape(groups_count, RANKS, -1, a.shape[1]) for a in arrays]
     rows = views[0].shape[2]
@@ -613,25 +618,22 @@
     any_space = pl.BlockSpec(memory_space=pl.ANY)
     return pl.pallas_call(
         functools.partial(weights_reduce_kernel, count, groups_count),
-        out_shape=[jax.ShapeDtypeStruct((rows, a.shape[1]), a.dtype) for a in arrays]
-        + [jax.ShapeDtypeStruct((GROUP,) + pieces.shape[1:], pieces.dtype)],
-        in_specs=[any_space] * count + [vmem],
-        out_specs=[vmem] * count + [any_space],
+        out_shape=[jax.ShapeDtypeStruct((rows, a.shape[1]), a.dtype) for a in arrays],
+        in_specs=[any_space] * count,
+        out_specs=[vmem] * count,
         scratch_shapes=buffers(8) + buffers(8) + buffers(4) + buffers(2) + buffers(1) + far_buffers
         + [
-            dma((2, count, 3, 4, 8)),
+            dma((2, count, 2, 4, 8)),
             dma((2, max(groups_count - 1, 1), count)),
             dma((2, count)),
-            dma((2, 16)),
             dma((count, 8)),
-            dma(()),
         ],
         compiler_params=pltpu.CompilerParams(
             collective_id=collective_id, has_side_effects=True, vmem_limit_bytes=48 * 2**20
         ),
-        cost_estimate=pl.CostEstimate(flops=80000000000, bytes_accessed=2**24, transcendentals=0),
+        cost_estimate=pl.CostEstimate(flops=1000000, bytes_accessed=2**24, transcendentals=0),
         name="weights_reduce",
-    )(*views, pieces)
+    )(*views)
 
 
 def expert_kernel(
@@ -809,6 +811,8 @@
         mine = expert_pieces(w_gate_up, w_down, seq_rank)
         tokens_before = lax.ppermute(tokens[0], "seq", forward_pair)
         starts_before = lax.ppermute(starts, "seq", forward_pair)
+        mine, query_key_value_weight = lax.optimization_barrier((mine, query_key_value_weight))
+        weights = lax.all_gather(mine, "dp", axis=0, tiled=True, axis_index_groups=between)
         spare = lambda value: jnp.pad(value, ((0, 0), (0, 128 - value.shape[1])))
         qkv_weight, out_weight, small = weights_gather(
             0,
@@ -819,10 +823,6 @@
                 [spare(w_router), spare(jnp.stack([gain_one, gain_two], 1))], 1
             ),
         )
-        mine, qkv_weight, out_weight, small = lax.optimization_barrier(
-            (mine, qkv_weight, out_weight, small)
-        )
-        weights = lax.all_gather(mine, "dp", axis=0, tiled=True, axis_index_groups=between)
         router_weight = small[:, :EXPERTS]
         gain_a = small[:, 128].astype(f32)
         gain_b = small[:, 129].astype(f32)
@@ -928,12 +928,12 @@
         little = jnp.concatenate(
             [spare(router_wgrad), spare(jnp.stack([gain_one_grad, gain_two_grad], 1))], 1
         )
-        qkv_shard, out_shard, little, experts_all = weights_reduce(
+        qkv_shard, out_shard, little = weights_reduce(
             3,
             groups_count,
             (qkv_wgrad.astype(bf16), out_wgrad.astype(bf16), little),
-            expert_grads,
-        )
+        )
+        experts_all = send_pieces(4, expert_grads)
         experts_all = experts_all.reshape((EXPERTS,) + experts_all.shape[2:])
         stat_sums = stat_sums + lax.ppermute(stat_sums, "seq", [(0, 1), (1, 0)])
         first = w_gate_up.shape[0]

time: 478 us -> 474 us (level)
  Pallas kernels: 276 us -> 337 us
  waiting for transfers between devices: 77.2 us -> 22 us
  local copies, waits for them, and re-layouts: 21.4 us -> 16.4 us
    all_gather x1, waiting for transfers between devices: 53.5 us -> 0.01 us  [body(): lax.all_gather(mine, 'dp', axis=0, tiled=True, axis_index_groups=between)]
    pallas_call x1, Pallas kernels: 45.4 us -> 88 us  [weights_gather(): pl.pallas_call(functools.partial(weights_gather_kernel, count, groups_cou...]
    pallas_call x0 -> x1, Pallas kernels: none -> 39.3 us  [send_pieces(): pl.pallas_call(pieces_kernel, out_shape=jax.ShapeDtypeStruct((GROUP,) + p...]
    pallas_call x1, Pallas kernels: 85.2 us -> 65.5 us  [weights_reduce(): pl.pallas_call(functools.partial(weights_reduce_kernel, count, groups_cou...]
    reduce_scatter x1, waiting for transfers between devices: 12.9 us -> 0.01 us  [body(): lax.psum_scatter(expert_wgrads, 'dp', scatter_dimension=0, tiled=True, ax...]
    ppermute x1, waiting for transfers between devices: 0.01 us -> 9.37 us  [body(): starts_before = lax.ppermute(starts, 'seq', forward_pair)]
  transfers between devices with their start and end apart: 7 -> 7, of which waited for: 3 -> 3; matrix products, arithmetic and copies ran while one was open for 12% -> 14% of each run, Pallas kernels for 29% -> 52%
where the time goes in v8:
time: 474 us; the launch traced here: 467 us
  Pallas kernels  337 us (71%)
  matrix products  36.6 us (8%)
  other arithmetic  26 us (5%)
  waiting for transfers between devices  22 us (5%)
  local copies, waits for them, and re-layouts  16.4 us (3%)
  between operations  15.3 us (3%)
  starting transfers between devices  13.1 us (3%)
    pallas_call x1, Pallas kernels, weights_gather(): pl.pallas_call(functools.partial(weights_gather_kernel, count, groups_cou...  88 us
    pallas_call x1, Pallas kernels, weights_reduce(): pl.pallas_call(functools.partial(weights_reduce_kernel, count, groups_cou...  65.5 us
    pallas_call x1, Pallas kernels, expert_layer(): pl.pallas_call(functools.partial(expert_kernel, first), grid=(GROUP // sh...  56.2 us
    pallas_call x1, Pallas kernels, group_reduce(): pl.pallas_call(reduce_kernel, out_shape=[jax.ShapeDtypeStruct((rows, widt...  44.8 us
    pallas_call x1, Pallas kernels, group_gather(): pl.pallas_call(functools.partial(gather_kernel, count), out_shape=[jax.Sh...  43.4 us
    pallas_call x1, Pallas kernels, send_pieces(): pl.pallas_call(pieces_kernel, out_shape=jax.ShapeDtypeStruct((GROUP,) + p...  39.3 us
    ppermute x1, waiting for transfers between devices, body(): kv_back = lax.ppermute(kv_grad[:count].astype(bf16), 'seq', back_pair)  10.9 us
  transfers between devices with their start and end apart: 7, of which 3 were waited for; matrix products, arithmetic and copies ran while one was open for 14% of the time, Pallas kernels for 52%

profile of v8, /device:TPU:0, one launch (start us, length us, event | category | flops | bytes accessed | tf_op | source)
XLA Modules:
  0.0 466.6 jit_solution(8368275556002489938)
XLA Ops:
  7.2 1.4 dynamic-slice_bitcast_fusion
  9.0 2.0 copy.83
  11.0 4.4 all-to-all-start
  15.4 4.9 %collective-permute-start = (bf16[256,1024]{1,0:T(8,128)(2,1)S(1)}, bf16[256,1024]{1,0:T(8,128)(2,1)S(1)}, u32[]{:S(2)}, u32[]{:S(2)}) collective-permute-start(bf16[256,1024]{1,0:T(8,128)(2,1)S(1)} %bitcast.162), channel_id=1, source_target_pairs={{0,16},{1,17},{2,18},{3,19},{4,20},{5,21},{6,22},{7,23},{8,24},{9,... | collective-permute-start | bytes 1572872 | tf_op jit(solution)/shard_map/ppermute | solution.py:812
  20.4 1.3 collective-permute-start.1
  22.1 0.6 fusion.60.refs_2_
  22.7 9.4 %collective-permute-done.1 = s32[1,256]{1,0:T(1,128)S(1)} collective-permute-done((s32[1,256]{1,0:T(1,128)S(1)}, s32[1,256]{1,0:T(1,128)S(1)}, u32[]{:S(2)}, u32[]{:S(2)}) %collective-permute-start.1) | collective-permute-done | bytes 1056 | tf_op jit(solution)/shard_map/ppermute | solution.py:813
  32.3 0.3 multiply_cosine_fusion
  32.6 0.7 pad_maximum_fusion.8
  33.3 0.8 fusion.47
  34.2 0.2 multiply_reduce_fusion
  34.4 1.7 all-to-all-done
  36.2 88.0 %weights_gather.1 = (bf16[2,8,64,2048]{3,2,1,0:T(8,128)(2,1)}, bf16[2,8,64,1024]{3,2,1,0:T(8,128)(2,1)}, bf16[2,8,64,256]{3,2,1,0:T(8,128)(2,1)}) custom-call(bf16[64,2048]{1,0:T(8,128)(2,1)} %refs_0_, bf16[64,1024]{1,0:T(8,128)(2,1)} %refs_1_.1, bf16[64,256]{1,0:T(8,128)(2,1)} %fusion.60.refs_2_), custom_call_target="tpu_custom_call" | custom-call | flops 44999999488 | bytes 16777216 | tf_op jit(solution)/shard_map/weights_gather/pallas_call | solution.py:399
  124.2 1.2 slice_convert_fusion.2
  125.6 0.3 multiply_convert_fusion
  125.8 3.2 fusion.10
  129.3 0.3 copy.88
  129.6 1.0 copy.87
  130.8 2.7 fusion.8
  133.7 0.2 fusion.37
  134.0 0.5 copy-done.20
  134.4 0.3 fusion.44
  134.7 5.2 %fusion.78 = (f32[8,2,256]{2,1,0:T(2,128)S(1)}, f32[8,2,256,512]{2,3,1,0:T(8,128)}) fusion(pred[256,512]{0,1:T(8,128)(4,1)S(1)} %copy-done.27, bf16[512,8,64,1]{0,2,3,1:T(8,128)(2,1)S(1)} %fusion.44, bf16[256,8,2,64]{0,3,2,1:T(8,128)(2,1)S(1)} %fusion.37), kind=kOutput, calls=%fused_computation.167 | convolution fusion | flops 276824576 | bytes 9584640 | tf_op jit(solution)/shard_map/sub | solution.py:860
  140.0 4.4 fusion.17
  144.5 0.8 multiply_reduce_fusion.5
  145.7 0.3 fusion.79
  146.0 0.6 fusion.75.refs_1_
  146.6 43.4 %group_gather.1 = (bf16[8,256,1024]{2,1,0:T(8,128)(2,1)}, f32[8,16,256]{2,1,0:T(8,128)}, bf16[8,256,1024]{2,1,0:T(8,128)(2,1)}) custom-call(bf16[256,1024]{1,0:T(8,128)(2,1)} %copy-done.10, f32[16,256]{1,0:T(8,128)} %fusion.75.refs_1_, bf16[256,1024]{1,0:T(8,128)(2,1)} %bitcast.178), custom_call_target="tpu_custom_call" | custom-call | flops 1000000000 | bytes 16777216 | tf_op jit(solution)/shard_map/group_gather/pallas_call | solution.py:140
  190.0 1.5 constant_dynamic-slice_fusion.gate_ref
  191.5 56.2 %expert_layer.1 = (bf16[8,256,1024]{2,1,0:T(8,128)(2,1)}, bf16[8,256,1024]{2,1,0:T(8,128)(2,1)}, f32[8,8,256]{2,1,0:T(8,128)}, bf16[16,2,96,1024]{3,2,1,0:T(8,128)(2,1)}) custom-call(bf16[8,256,1024]{2,1,0:T(8,128)(2,1)} %get-tuple-element.32.rows_ref, bf16[8,256,1024]{2,1,0:T(8,128)(2,1)} %get-tuple-element.33.grad_ref, ...), custom_call_target="tpu_custom_call" | custom-call | flops 44999999488 | bytes 16777216 | tf_op jit(solution)/shard_map/expert_layer/pallas_call | solution.py:715
  247.9 0.6 copy-done.2
  248.5 44.8 %group_reduce.1 = (f32[256,1024]{1,0:T(8,128)S(1)}, f32[256,1024]{1,0:T(8,128)S(1)}, f32[8,8,256]{2,1,0:T(8,128)S(1)}) custom-call(bf16[8,256,1024]{2,1,0:T(8,128)(2,1)} %get-tuple-element.36.mixed_ref, bf16[8,256,1024]{2,1,0:T(8,128)(2,1)} %get-tuple-element.37.normed_ref, f32[8,8,256]{2,1,0:T(8,128)S(1)} %copy-done.2), custom_call_target="tpu_custom_call" | custom-call | flops 1000000 | bytes 16777216 | tf_op jit(solution)/shard_map/group_reduce/pallas_call | solution.py:268
  293.4 2.7 multiply_reduce_fusion.2
  296.1 3.3 multiply_reduce_fusion.1
  299.4 1.4 pad_maximum_fusion.11
  300.8 0.9 collective-permute-start.3
  301.7 0.8 convolution_convert_fusion.2
  302.7 4.9 %fusion.1 = (f32[8,2,256]{2,1,0:T(2,128)S(1)}, f32[8,512,256,2]{2,1,3,0:T(8,128)S(1)}) fusion(f32[8,2,256,512]{2,3,1,0:T(8,128)} %get-tuple-element.115, f32[8,2,256]{2,1,0:T(2,128)S(1)} %get-tuple-element.114, bf16[512,8,64,1]{0,2,3,1:T(8,128)(2,1)S(1)} %bitcast.180, bf16[256,8,2,64]{0,3,2,1:T(8,128)(2,1)S(1)} %bitcast.181), kind=kOutput, calls=%fused_computation.3 | convolution fusion | flops 274722816 | bytes 17858560 | tf_op jit(solution)/shard_map/qgrd,kgd->grqk/dot_general | solution.py:900
  307.6 1.0 slice-done.1
  308.6 1.5 fusion.3
  310.1 0.8 fusion.21
  311.4 0.6 copy-done.18
  312.0 1.4 fusion.16
  313.4 1.4 fusion.12
  314.8 1.5 collective-permute-start.2
  316.4 0.3 fusion.66
  316.7 0.7 convolution_convert_fusion.1
  317.5 1.9 sqrt_bitcast_fusion
  319.4 10.9 %collective-permute-done.2 = bf16[256,1024]{0,1:T(8,128)(2,1)S(1)} collective-permute-done((bf16[256,1024]{0,1:T(8,128)(2,1)S(1)}, bf16[256,1024]{0,1:T(8,128)(2,1)S(1)}, u32[]{:S(2)}, u32[]{:S(2)}) %collective-permute-start.2) | collective-permute-done | bytes 524320 | tf_op jit(solution)/shard_map/ppermute | solution.py:913
  330.8 2.4 fusion.29
  333.2 1.1 select_maximum_fusion
  334.3 1.6 copy.97
  335.9 4.6 convolution_convert_fusion
  340.5 65.5 %weights_reduce.1 = (bf16[64,2048]{1,0:T(8,128)(2,1)S(1)}, bf16[64,1024]{1,0:T(8,128)(2,1)S(1)}, f32[64,256]{1,0:T(8,128)S(1)}) custom-call(bf16[2,8,64,2048]{3,2,1,0:T(8,128)(2,1)} %bitcast.165, bf16[2,8,64,1024]{3,2,1,0:T(8,128)(2,1)S(1)} %bitcast.152, f32[2,8,64,256]{3,2,1,0:T(8,128)S(1)} %bitcast.153), custom_call_target="tpu_custom_call" | custom-call | flops 1000000 | bytes 16777216 | tf_op jit(solution)/shard_map/weights_reduce/pallas_call | solution.py:619
  406.0 0.8 convert_element_type.177
  406.8 0.7 convert_element_type.178
  407.6 0.7 copy.100
  408.2 0.7 slice_reduce_fusion
  408.9 2.8 fusion.45
  411.7 39.3 %send_pieces.1 = bf16[8,2,96,1024]{3,2,1,0:T(8,128)(2,1)} custom-call(bf16[4,2,96,1024]{3,2,1,0:T(8,128)(2,1)} %reduce-scatter.2.cloned.1.call-done.pieces), custom_call_target="tpu_custom_call" | custom-call | tf_op jit(solution)/shard_map/send_pieces/pallas_call | solution.py:587
  451.0 1.8 slice.151
  452.8 1.4 slice.152
  454.2 3.2 convert_bitcast_fusion
  457.4 1.9 convert_bitcast_fusion.1
  (124 shorter events, 3.8 us)
Async XLA Ops:
  7.2 1.5 copy-start
  8.8 6.6 %copy-start.5 = (bf16[1,256,1024]{2,1,0:T(8,128)(2,1)S(1)}, bf16[1,256,1024]{2,1,0:T(8,128)(2,1)}, u32[]{:S(2)}) copy-start(bf16[1,256,1024]{2,1,0:T(8,128)(2,1)} %param.11) | copy-start | bytes 1572868
  8.8 11.6 %copy-start.30 = (s32[1,256]{1,0:T(1,128)S(1)}, s32[1,256]{1,0:T(1,128)}, u32[]{:S(2)}) copy-start(s32[1,256]{1,0:T(1,128)} %param.12) | copy-start | bytes 3076
  8.9 12.9 %copy-start.31 = (bf16[64]{0:T(256)(128)(2,1)S(1)}, bf16[64]{0:T(256)(128)(2,1)}, u32[]{:S(2)}) copy-start(bf16[64]{0:T(256)(128)(2,1)} %param.17) | copy-start | bytes 388
  8.9 12.9 %copy-start.32 = (bf16[64]{0:T(256)(128)(2,1)S(1)}, bf16[64]{0:T(256)(128)(2,1)}, u32[]{:S(2)}) copy-start(bf16[64]{0:T(256)(128)(2,1)} %param.14) | copy-start | bytes 388
  9.0 13.0 %copy-start.29 = (bf16[64,16]{0,1:T(8,128)(2,1)S(1)}, bf16[64,16]{0,1:T(8,128)(2,1)}, u32[]{:S(2)}) copy-start(bf16[64,16]{0,1:T(8,128)(2,1)} %param.18) | copy-start | bytes 6148
  9.0 13.1 %copy-start.28 = (s32[1,256,8]{1,2,0:T(8,128)S(1)}, s32[1,256,8]{1,2,0:T(8,128)}, u32[]{:S(2)}) copy-start(s32[1,256,8]{1,2,0:T(8,128)} %param.13) | copy-start | bytes 24580
  11.0 25.1 %all-to-all-start = ((bf16[4,2,96,1024]{3,2,1,0:T(8,128)(2,1)}), bf16[4,2,96,1024]{3,2,1,0:T(8,128)(2,1)}, u32[]{:S(2)}, u32[]{:S(2)}) async-start(bf16[4,2,96,1024]{3,2,1,0:T(8,128)(2,1)} %bitcast.3), calls=%async_computation | async-start | bytes 3145728 | tf_op jit(solution)/shard_map/all_to_all | solution.py:795
  15.4 176.1 %all-gather.2.cloned.1.call-start = ((), (), s32[]{:S(2)}) async-start(), calls=%async_computation.2 | async-start | bytes 7864320 | tf_op jit(solution)/shard_map/all_gather | solution.py:815
  15.4 18.7 %collective-permute-start = (bf16[256,1024]{1,0:T(8,128)(2,1)S(1)}, bf16[256,1024]{1,0:T(8,128)(2,1)S(1)}, u32[]{:S(2)}, u32[]{:S(2)}) collective-permute-start(bf16[256,1024]{1,0:T(8,128)(2,1)S(1)} %bitcast.162), channel_id=1, source_target_pairs={{0,16},{1,17},{2,18},{3,19},{4,20},{5,21},{6,22},{7,23},{8,24},{9,... | collective-permute-start | bytes 1572872 | tf_op jit(solution)/shard_map/ppermute | solution.py:812
  20.4 11.7 %collective-permute-start.1 = (s32[1,256]{1,0:T(1,128)S(1)}, s32[1,256]{1,0:T(1,128)S(1)}, u32[]{:S(2)}, u32[]{:S(2)}) collective-permute-start(s32[1,256]{1,0:T(1,128)S(1)} %copy-done.30), channel_id=1, source_target_pairs={{0,16},{1,17},{2,18},{3,19},{4,20},{5,21},{6,22},{7,23},{8,24},{9,... | collective-permute-start | bytes 3080 | tf_op jit(solution)/shard_map/ppermute | solution.py:813
  36.1 375.6 %reduce-scatter.2.cloned.1.call-start = ((), (), s32[]{:S(2)}) async-start(), calls=%async_computation.3 | async-start | bytes 7864320 | tf_op jit(solution)/shard_map/reduce_scatter | solution.py:878
  125.8 3.3 copy-start.19
  133.5 0.9 copy-start.20
  133.6 1.1 copy-start.27
  133.9 6.0 %copy-start.17 = (bf16[256,8,2,64]{0,3,2,1:T(8,128)(2,1)}, bf16[256,8,2,64]{0,3,2,1:T(8,128)(2,1)S(1)}, u32[]{:S(2)}) copy-start(bf16[256,8,2,64]{0,3,2,1:T(8,128)(2,1)S(1)} %fusion.37) | copy-start | bytes 1572868
  134.7 5.3 %copy-start.12 = (bf16[512,8,64,1]{0,2,3,1:T(8,128)(2,1)}, bf16[512,8,64,1]{0,2,3,1:T(8,128)(2,1)S(1)}, u32[]{:S(2)}) copy-start(bf16[512,8,64,1]{0,2,3,1:T(8,128)(2,1)S(1)} %fusion.44) | copy-start | bytes 1572868
  134.7 5.3 %copy-start.21 = (bf16[512,512]{0,1:T(8,128)(2,1)S(1)}, bf16[512,512]{0,1:T(8,128)(2,1)}, u32[]{:S(2)}) copy-start(bf16[512,512]{0,1:T(8,128)(2,1)} %copy.87) | copy-start | bytes 1572868
  140.0 4.4 copy-start.6
  140.0 4.4 copy-start.8
  144.4 0.9 copy-start.14
  144.4 1.2 copy-start.16
  145.3 148.1 %copy-start.4 = (f32[256,1024]{1,0:T(8,128)}, f32[256,1024]{1,0:T(8,128)S(1)}, u32[]{:S(2)}) copy-start(f32[256,1024]{1,0:T(8,128)S(1)} %get-tuple-element.117) | copy-start | bytes 3145732
  145.7 0.9 copy-start.10
  247.7 0.8 copy-start.2
  293.4 8.3 %copy-start.9 = (bf16[2,8,64,1024]{3,2,1,0:T(8,128)(2,1)S(1)}, bf16[2,8,64,1024]{3,2,1,0:T(8,128)(2,1)}, u32[]{:S(2)}) copy-start(bf16[2,8,64,1024]{3,2,1,0:T(8,128)(2,1)} %get-tuple-element.31) | copy-start | bytes 6291460
  296.1 6.6 %copy-start.22 = (bf16[512,512]{0,1:T(8,128)(2,1)S(1)}, bf16[512,512]{0,1:T(8,128)(2,1)}, u32[]{:S(2)}) copy-start(bf16[512,512]{0,1:T(8,128)(2,1)} %copy.87) | copy-start | bytes 1572868
  299.4 17.3 %copy-start.3 = (f32[256,1024]{1,0:T(8,128)}, f32[256,1024]{1,0:T(8,128)S(1)}, u32[]{:S(2)}) copy-start(f32[256,1024]{1,0:T(8,128)S(1)} %get-tuple-element.95) | copy-start | bytes 3145732
  300.8 16.7 %collective-permute-start.3 = (f32[2]{0:T(128)S(1)}, f32[2]{0:T(128)S(1)}, u32[]{:S(2)}, u32[]{:S(2)}) collective-permute-start(f32[2]{0:T(128)S(1)} %pad_maximum_fusion.11), channel_id=1, source_target_pairs={{0,16},{16,0},{1,17},{17,1},{2,18},{18,2},{3,19},{19,3},{4,20},{20... | collective-permute-start | bytes 32 | tf_op jit(solution)/shard_map/ppermute | solution.py:938
  302.7 4.9 %slice-start = ((s8[8388608]{0:T(1024)(128)(4,1)}), s8[4194304]{0:T(1024)(128)(4,1)S(1)}, s32[]{:S(2)}) async-start(s8[8388608]{0:T(1024)(128)(4,1)} %bitcast.160), calls=%async_computation.4 | async-start | bytes 8388608
  302.7 5.9 %slice-start.1 = ((s8[8388608]{0:T(1024)(128)(4,1)}), s8[4194304]{0:T(1024)(128)(4,1)S(1)}, s32[]{:S(2)}) async-start(s8[8388608]{0:T(1024)(128)(4,1)} %bitcast.160), calls=%async_computation.5 | async-start | bytes 8388608
  308.6 1.5 copy-start.13
  310.9 1.1 copy-start.18
  312.0 18.8 %copy-start.23 = (bf16[256,1024]{0,1:T(8,128)(2,1)}, bf16[256,1024]{0,1:T(8,128)(2,1)S(1)}, u32[]{:S(2)}) copy-start(bf16[256,1024]{0,1:T(8,128)(2,1)S(1)} %fusion.39) | copy-start | bytes 1572868
  313.3 3.1 copy-start.11
  313.4 3.4 copy-start.15
  314.8 15.4 %collective-permute-start.2 = (bf16[256,1024]{0,1:T(8,128)(2,1)S(1)}, bf16[256,1024]{0,1:T(8,128)(2,1)S(1)}, u32[]{:S(2)}, u32[]{:S(2)}) collective-permute-start(bf16[256,1024]{0,1:T(8,128)(2,1)S(1)} %fusion.33), channel_id=1, source_target_pairs={{16,0},{17,1},{18,2},{19,3},{20,4},{21,5},{22,6},{23,7},{24,8},{25... | collective-permute-start | bytes 1572872 | tf_op jit(solution)/shard_map/ppermute | solution.py:913
  319.4 11.4 %copy-start.7 = (bf16[1,256,1024]{2,1,0:T(8,128)(2,1)S(1)}, bf16[1,256,1024]{2,1,0:T(8,128)(2,1)}, u32[]{:S(2)}) copy-start(bf16[1,256,1024]{2,1,0:T(8,128)(2,1)} %param.11) | copy-start | bytes 1572868
  319.4 11.4 %copy-start.33 = (bf16[2,8,64,2048]{3,2,1,0:T(8,128)(2,1)S(1)}, bf16[2,8,64,2048]{3,2,1,0:T(8,128)(2,1)}, u32[]{:S(2)}) copy-start(bf16[2,8,64,2048]{3,2,1,0:T(8,128)(2,1)} %get-tuple-element.30) | copy-start | bytes 12582916
  330.5 2.7 copy-start.24
  330.7 2.4 copy-start.26
  333.1 2.7 copy-start.25
  452.8 6.6 %copy-start.1 = (bf16[32,16,1024]{2,1,0:T(8,128)(2,1)S(1)}, bf16[32,16,1024]{2,1,0:T(8,128)(2,1)}, u32[]{:S(2)}) copy-start(bf16[32,16,1024]{2,1,0:T(8,128)(2,1)} %param.20) | copy-start | bytes 3145732
Sparse Core Ops, SparseCore 0:
  36.3 125.7 all-gather.1
  247.8 108.0 reduce-scatter.1
